TPU v7x, 32 devices: a whole 2x2x4 slice. The times are simulated.
32 devices in a mesh: lb: 8 (over y, x, core), rb: 4 (over z).
Axes of the slice: x: 2, y: 2, z: 4, core: 2. Of those that a mesh axis runs over, the one named last changes fastest.
Arguments:
- wavefunction: bfloat16 [3072, 4, 3072], P('lb', None, 'rb'), may hold values from -6 to 6
- left_environment: bfloat16 [8, 1024, 3072], P(None, 'lb'), may hold values from -0.109375 to 0.109375
- operator_left: float32 [8, 8, 2, 2], replicated, may hold values from -1.5 to 1.5
- operator_right: float32 [8, 8, 2, 2], replicated, may hold values from -1.5 to 1.5
- right_environment: bfloat16 [8, 3072, 3072], P(None, 'rb', 'lb'), may hold values from -0.0546875 to 0.0546875
- row_sector: int32 [8], replicated, may hold values from 0 to 3, never falling along the last dimension, each value on 1 to 4 neighbouring positions
Outputs:
- applied_state: bfloat16 [1024, 4, 3072], P('lb', None, 'rb')
- density: float32 [1024, 1024], P('lb', 'rb')
Inputs may be any that keep to these rules, and one draw needn't show every extreme that they name: `row_sector`: entry t is the sector of output rows t * 128 to (t + 1) * 128 - 1. Entries never fall along t; each sector holds 1 to 4 tiles, and one holds exactly 4.
All inputs are finite; a program needn't handle non-finite values.
Results may differ from a plain program's by a relative error of at most 0.013.
Values may be sent and summed in bfloat16 or wider, within the bound.
No kernel may reach another device: no remote copies, remote signals or barrier semaphores. Data moves between devices by JAX's collectives and lax.ppermute only.
A program may use at most 128 MiB of HBM per device.

v0:
```python
import functools
import math

import jax
import jax.numpy as jnp
from jax import lax
from jax.experimental import pallas as pl
from jax.experimental.pallas import tpu as pltpu
from jax.sharding import PartitionSpec as P


BOND_WIDTH = 3072
ROW_BLOCKS = 4


def hop(value, mask):
    devices = lax.axis_size("lb")
    return lax.ppermute(value, "lb", [(i, i ^ mask) for i in range(devices)])


def rb_hop(value, mask):
    devices = lax.axis_size("rb")
    return lax.ppermute(value, "rb", [(i, i ^ mask) for i in range(devices)])


def spread(piece, bits):
    held = {0: piece}
    for bit in bits:
        for q in list(held):
            held[q | bit] = hop(held[q], 2 * bit)
    return held


def combine_operators(operator_left, operator_right):
    channels = operator_left.shape[0]
    joined = jnp.einsum(
        "aups,uvqt->avpqst", operator_left, operator_right, precision=lax.Precision.HIGHEST
    )
    return joined.reshape(channels, channels, 4, 4)


def right_kernel(chips, blocks, steps, *refs):
    lhs, refs = refs[: 2 * blocks], refs[2 * blocks :]
    first, second = refs[:chips], refs[chips : 2 * chips]
    out_ref, rhs, total = refs[2 * chips :]
    step = pl.program_id(0)
    width = first[0].shape[1]

    @pl.when(step == 0)
    def _():
        total[...] = jnp.zeros_like(total)

    def load(pieces):
        for q in range(chips):
            rhs[:, q * width : (q + 1) * width] = pieces[q][...]

    @pl.when(step < steps // 2)
    def _():
        load(first)

    @pl.when(step >= steps // 2)
    def _():
        load(second)

    rows = blocks * lhs[0].shape[0]
    for e in range(2):
        left = jnp.concatenate([r[...] for r in lhs[e * blocks : (e + 1) * blocks]], axis=0)
        total[e * rows : (e + 1) * rows, :] += jnp.dot(
            left, rhs[...], preferred_element_type=jnp.float32
        )

    @pl.when(step == steps - 1)
    def _():
        for q in range(chips):
            out_ref[q] = total[:, q * width : (q + 1) * width].astype(out_ref.dtype)


def right_product(own, sib, first, second, steps):
    chips, blocks = len(first), len(own)
    block_rows, depth = own[0].shape
    rows = 2 * blocks * block_rows
    width = first[0].shape[1]
    block = depth // steps
    half = steps // 2
    lhs_spec = pl.BlockSpec((block_rows, block), lambda k: (0, k))
    first_spec = pl.BlockSpec((block, width), lambda k: (jnp.minimum(k, half - 1), 0))
    second_spec = pl.BlockSpec((block, width), lambda k: (jnp.maximum(k - half, 0), 0))
    shape = (chips, rows, width)
    return pl.pallas_call(
        functools.partial(right_kernel, chips, blocks, steps),
        out_shape=jax.ShapeDtypeStruct(shape, jnp.bfloat16),
        grid=(steps,),
        in_specs=[lhs_spec] * (2 * blocks) + [first_spec] * chips + [second_spec] * chips,
        out_specs=pl.BlockSpec(shape, lambda k: (0, 0, 0)),
        scratch_shapes=[
            pltpu.VMEM((block, chips * width), jnp.bfloat16),
            pltpu.VMEM((rows, chips * width), jnp.float32),
        ],
        cost_estimate=pl.CostEstimate(
            flops=2 * rows * depth * chips * width,
            bytes_accessed=2 * depth * (rows + chips * width),
            transcendentals=0,
        ),
        name="right_product",
    )(*own, *sib, *first, *second)


def exchange(parts, own_slot):
    devices = lax.axis_size("rb")
    z = lax.axis_index("rb")

    def slot(target):
        return lax.dynamic_index_in_dim(parts, target ^ own_slot, 0, keepdims=False)

    total = slot(z).astype(jnp.float32)
    for mask in range(1, devices):
        total = total + rb_hop(slot(z ^ mask), mask).astype(jnp.float32)
    return total


def shards(
    wavefunction, left_environment, operator_left, operator_right, right_environment, row_sector
):
    channels, row_count, full_bond = left_environment.shape
    piece_rows, states, local_right = wavefunction.shape
    tile_width = right_environment.shape[2]
    tiles = lax.axis_size("lb")
    chips = tiles // 2
    me = lax.axis_index("lb")
    z = lax.axis_index("rb")
    chip, core = me // 2, me % 2
    first_core = core == 0
    bits = [1 << i for i in range(chips.bit_length() - 1)]
    orders = (bits[::-1], bits)

    flat = wavefunction.reshape(piece_rows, states * local_right)
    half_rows = piece_rows // 2
    state = jnp.zeros((full_bond, states * local_right), wavefunction.dtype)
    for half in range(2):
        held = spread(flat[half * half_rows : (half + 1) * half_rows], orders[half])
        for q, piece in held.items():
            for e in range(2):
                value = piece if e == 0 else hop(piece, 1)
                start = (me ^ (2 * q + e)) * piece_rows + half * half_rows
                state = lax.dynamic_update_slice(state, value, (start, jnp.int32(0)))

    combined = combine_operators(operator_left, operator_right)
    block_rows = row_count // ROW_BLOCKS
    mixed, mixed_sibling = [], []
    for s in range(ROW_BLOCKS):
        rows = left_environment[:, s * block_rows : (s + 1) * block_rows]
        left_part = jnp.dot(
            rows.reshape(channels * block_rows, full_bond),
            state,
            preferred_element_type=jnp.float32,
        )
        left_part = left_part.reshape(channels, block_rows, states, local_right)
        part = jnp.einsum(
            "avyx,alxr->lyvr", combined, left_part, precision=lax.Precision.HIGHEST
        ).astype(jnp.bfloat16)
        part = part.reshape(block_rows * states, channels * local_right)
        mixed.append(part)
        mixed_sibling.append(hop(part, 1))

    chunks = max(1, tile_width // 128)
    width = tile_width // chunks
    half = channels // 2
    mine, theirs = [], []
    gram = [0.0] * chips
    for j in range(chunks):
        columns = right_environment[:, :, j * width : (j + 1) * width]
        pieces = []
        for h in range(2):
            part = columns[h * half : (h + 1) * half].reshape(half * local_right, width)
            held = spread(part, orders[h])
            pieces.append([held[q] for q in range(chips)])
        parts = right_product(mixed, mixed_sibling, pieces[0], pieces[1], channels)
        applied = exchange(parts, chip).astype(jnp.bfloat16)
        own_rows = row_count * states
        mine.append(applied[:own_rows])
        theirs.append(hop(applied[own_rows:], 1))
        flat_tiles = applied.reshape(2 * row_count, states * width)
        others = spread(flat_tiles, orders[j % 2])
        for q in range(chips):
            gram[q] = gram[q] + lax.dot_general(
                flat_tiles,
                others[q],
                (((1,), (1,)), ((), ())),
                preferred_element_type=jnp.float32,
            )

    def ordered(value, other):
        return (jnp.where(first_core, value, other), jnp.where(first_core, other, value))

    columns = [ordered(a, b) for a, b in zip(mine, theirs)]
    applied = jnp.concatenate([c[0] for c in columns] + [c[1] for c in columns], axis=1)
    applied = applied.reshape(row_count, states, 2 * tile_width)

    gram = jnp.stack(gram)
    received = hop(gram[:, row_count:].astype(jnp.bfloat16), 1).astype(jnp.float32)
    kept = gram[:, :row_count]
    own_first = kept[:, :, :row_count] + received[:, :, row_count:]
    own_second = kept[:, :, row_count:] + received[:, :, :row_count]
    gram = jnp.concatenate(ordered(own_first, own_second), axis=2).astype(jnp.bfloat16)
    block = exchange(gram, chip)
    own_label = lax.dynamic_index_in_dim(row_sector, me, keepdims=False)
    labels = lax.dynamic_slice_in_dim(row_sector, 2 * z, 2)
    keep = jnp.repeat(labels == own_label, row_count)[None, :]
    density = jnp.where(keep, block, jnp.float32(0.0)) * (1.0 / math.sqrt(4.0 * BOND_WIDTH))
    return (applied, density)


def solution(mesh):
    placed = (P("lb", None, "rb"), P(None, "lb", None), P(), P(), P(None, "rb", "lb"), P())
    return jax.shard_map(
        shards,
        mesh=mesh,
        in_specs=placed,
        out_specs=(P("lb", None, "rb"), P("lb", "rb")),
        check_vma=False,
    )
```

profile of v0, /device:TPU:0, one launch (start us, length us, event | category | flops | bytes accessed | tf_op | source)
XLA Modules:
  0.0 433.0 jit_solution(13557014878736257767)
XLA Ops:
  0.7 2.6 fusion.52
  4.0 2.6 collective-permute-start.1
  8.3 3.3 fusion.50
  12.8 2.7 fusion.51
  15.5 17.7 %collective-permute-done.1 = bf16[192,3072]{1,0:T(8,128)(2,1)} collective-permute-done((bf16[192,3072]{1,0:T(8,128)(2,1)S(1)}, bf16[192,3072]{1,0:T(8,128)(2,1)}, u32[]{:S(2)}, u32[]{:S(2)}) %collective-permute-start.1) | collective-permute-done | bytes 1179680 | tf_op jit(solution)/shard_map/ppermute | solution.py:18
  35.6 2.6 broadcast_in_dim.20
  41.5 1.8 collective-permute-start.10
  43.3 19.1 %collective-permute-done.5 = bf16[192,3072]{1,0:T(8,128)(2,1)} collective-permute-done((bf16[192,3072]{1,0:T(8,128)(2,1)}, bf16[192,3072]{1,0:T(8,128)(2,1)}, u32[]{:S(2)}, u32[]{:S(2)}) %collective-permute-start.5) | collective-permute-done | bytes 1179680 | tf_op jit(solution)/shard_map/ppermute | solution.py:18
  65.2 21.9 %collective-permute-done.8 = bf16[192,3072]{1,0:T(8,128)(2,1)S(1)} collective-permute-done((bf16[192,3072]{1,0:T(8,128)(2,1)S(1)}, bf16[192,3072]{1,0:T(8,128)(2,1)S(1)}, u32[]{:S(2)}, u32[]{:S(2)}) %collective-permute-start.8) | collective-permute-done | bytes 1179680 | tf_op jit(solution)/shard_map/ppermute | solution.py:18
  94.8 36.9 %collective-permute-done.12 = bf16[192,3072]{1,0:T(8,128)(2,1)S(1)} collective-permute-done((bf16[192,3072]{1,0:T(8,128)(2,1)S(1)}, bf16[192,3072]{1,0:T(8,128)(2,1)S(1)}, u32[]{:S(2)}, u32[]{:S(2)}) %collective-permute-start.12) | collective-permute-done | bytes 1179680 | tf_op jit(solution)/shard_map/ppermute | solution.py:18
  132.0 1.8 collective-permute-start.32
  136.4 7.3 %convolution_bitcast_fusion.2 = f32[256,3072]{0,1:T(8,128)} fusion(bf16[3072,3072]{1,0:T(8,128)(2,1)S(1)} %constant_dynamic-update-slice_fusion, bf16[256,3072]{1,0:T(8,128)(2,1)S(1)} %bitcast.181), kind=kOutput, calls=%fused_computation.2 | convolution fusion | flops 4831838208 | bytes 23592960 | tf_op jit(solution)/shard_map/dot_general | solution.py:152
  143.7 7.7 %convolution_bitcast_fusion.1 = f32[256,3072]{0,1:T(8,128)} fusion(bf16[3072,3072]{1,0:T(8,128)(2,1)S(1)} %constant_dynamic-update-slice_fusion, bf16[256,3072]{1,0:T(8,128)(2,1)S(1)} %bitcast.180), kind=kOutput, calls=%fused_computation.1 | convolution fusion | flops 4831838208 | bytes 23592960 | tf_op jit(solution)/shard_map/dot_general | solution.py:152
  151.4 7.2 %convolution_bitcast_fusion = f32[256,3072]{0,1:T(8,128)} fusion(bf16[3072,3072]{1,0:T(8,128)(2,1)S(1)} %constant_dynamic-update-slice_fusion, bf16[256,3072]{1,0:T(8,128)(2,1)S(1)} %bitcast.179), kind=kOutput, calls=%fused_computation | convolution fusion | flops 4831838208 | bytes 23592960 | tf_op jit(solution)/shard_map/dot_general | solution.py:152
  158.7 7.4 %convolution_bitcast_fusion.3 = f32[256,3072]{0,1:T(8,128)} fusion(bf16[3072,3072]{1,0:T(8,128)(2,1)S(1)} %constant_dynamic-update-slice_fusion, bf16[256,3072]{1,0:T(8,128)(2,1)S(1)} %bitcast.178), kind=kOutput, calls=%fused_computation.3 | convolution fusion | flops 4831838208 | bytes 23592960 | tf_op jit(solution)/shard_map/dot_general | solution.py:152
  166.1 2.4 copy.21
  168.5 2.8 reshape.90
  171.2 3.6 copy.24
  174.9 3.5 reshape.93
  178.3 5.7 %bitcast_convert_fusion.2 = bf16[32,768,8,4]{1,2,3,0:T(8,128)(2,1)S(1)} fusion(f32[8,8,4,4,1]{1,0,3,2,4:T(8,128)S(1)} %bitcast.174, f32[8,32,4,768]{3,2,1,0:T(4,128)} %reshape.90), kind=kOutput, calls=%fused_computation.10 | convolution fusion | flops 302776320 | bytes 4722688 | tf_op jit(solution)/shard_map/avyx,alxr->lyvr/dot_general | solution.py:158
  186.1 3.7 bitcast_convert_fusion.1
  192.9 2.4 copy.27
  195.3 2.9 reshape.96
  198.2 5.8 %bitcast_convert_fusion = bf16[32,768,8,4]{1,2,3,0:T(8,128)(2,1)S(1)} fusion(f32[8,8,4,4,1]{1,0,3,2,4:T(8,128)S(1)} %bitcast.176, f32[8,32,4,768]{3,2,1,0:T(4,128)} %reshape.96), kind=kOutput, calls=%fused_computation.4 | convolution fusion | flops 302776320 | bytes 4722688 | tf_op jit(solution)/shard_map/avyx,alxr->lyvr/dot_general | solution.py:158
  205.6 2.3 copy.15
  208.0 3.5 reshape.86
  211.5 3.7 bitcast_convert_fusion.3
  217.0 17.6 %collective-permute-done.30.refs_11_ = bf16[3072,128]{1,0:T(8,128)(2,1)S(1)} collective-permute-done((bf16[3072,128]{1,0:T(8,128)(2,1)}, bf16[3072,128]{1,0:T(8,128)(2,1)S(1)}, u32[]{:S(2)}, u32[]{:S(2)}) %collective-permute-start.30) | collective-permute-done | bytes 786464 | tf_op jit(solution)/shard_map/ppermute | solution.py:18
  237.4 15.4 %collective-permute-done.33.refs_15_ = bf16[3072,128]{1,0:T(8,128)(2,1)} collective-permute-done((bf16[3072,128]{1,0:T(8,128)(2,1)}, bf16[3072,128]{1,0:T(8,128)(2,1)}, u32[]{:S(2)}, u32[]{:S(2)}) %collective-permute-start.33) | collective-permute-done | bytes 786464 | tf_op jit(solution)/shard_map/ppermute | solution.py:18
  258.0 14.3 %right_product.4 = bf16[4,1024,128]{2,1,0:T(8,128)(2,1)} custom-call(bf16[128,6144]{1,0:T(8,128)(2,1)} %bitcast.183, bf16[128,6144]{1,0:T(8,128)(2,1)} %bitcast.74.refs_1_, bf16[128,6144]{1,0:T(8,128)(2,1)} %bitcast.77.refs_2_, bf16[128,6144]{1,0:T(8,128)(2,1)} %bitcast.80.refs_3_, bf16[128,6144]{1,0:T(8,128)(2,1)} %collective-permute-done.14.refs_4_, ...), custom_call_target="tpu_custom_call" | custom-call | flops 6442450944 | bytes 18874368 | tf_op jit(solution)/shard_map/right_product/pallas_call | solution.py:89
  272.2 18.2 %collective-permute-done.21.refs_13_ = bf16[3072,128]{1,0:T(8,128)(2,1)} collective-permute-done((bf16[3072,128]{1,0:T(8,128)(2,1)S(1)}, bf16[3072,128]{1,0:T(8,128)(2,1)}, u32[]{:S(2)}, u32[]{:S(2)}) %collective-permute-start.21) | collective-permute-done | bytes 786464 | tf_op jit(solution)/shard_map/ppermute | solution.py:18
  293.9 13.3 %collective-permute-done.40.refs_11_ = bf16[3072,128]{1,0:T(8,128)(2,1)} collective-permute-done((bf16[3072,128]{1,0:T(8,128)(2,1)}, bf16[3072,128]{1,0:T(8,128)(2,1)}, u32[]{:S(2)}, u32[]{:S(2)}) %collective-permute-start.40) | collective-permute-done | bytes 786464 | tf_op jit(solution)/shard_map/ppermute | solution.py:18
  311.6 14.1 %right_product.5 = bf16[4,1024,128]{2,1,0:T(8,128)(2,1)} custom-call(bf16[128,6144]{1,0:T(8,128)(2,1)} %bitcast.184, bf16[128,6144]{1,0:T(8,128)(2,1)} %bitcast.74.refs_1_, bf16[128,6144]{1,0:T(8,128)(2,1)} %bitcast.77.refs_2_, bf16[128,6144]{1,0:T(8,128)(2,1)} %bitcast.80.refs_3_, bf16[128,6144]{1,0:T(8,128)(2,1)} %collective-permute-done.14.refs_4_, ...), custom_call_target="tpu_custom_call" | custom-call | flops 6442450944 | bytes 18874368 | tf_op jit(solution)/shard_map/right_product/pallas_call | solution.py:89
  326.8 2.6 collective-permute-start.35
  329.7 7.9 %collective-permute-done.20.refs_11_ = bf16[3072,128]{1,0:T(8,128)(2,1)} collective-permute-done((bf16[3072,128]{1,0:T(8,128)(2,1)}, bf16[3072,128]{1,0:T(8,128)(2,1)}, u32[]{:S(2)}, u32[]{:S(2)}) %collective-permute-start.20) | collective-permute-done | bytes 786464 | tf_op jit(solution)/shard_map/ppermute | solution.py:18
  339.2 2.5 collective-permute-start.45
  341.8 14.1 %right_product.3 = bf16[4,1024,128]{2,1,0:T(8,128)(2,1)} custom-call(bf16[128,6144]{1,0:T(8,128)(2,1)} %bitcast.185, bf16[128,6144]{1,0:T(8,128)(2,1)} %bitcast.74.refs_1_, bf16[128,6144]{1,0:T(8,128)(2,1)} %bitcast.77.refs_2_, bf16[128,6144]{1,0:T(8,128)(2,1)} %bitcast.80.refs_3_, bf16[128,6144]{1,0:T(8,128)(2,1)} %collective-permute-done.14.refs_4_, ...), custom_call_target="tpu_custom_call" | custom-call | flops 6442450944 | bytes 18874368 | tf_op jit(solution)/shard_map/right_product/pallas_call | solution.py:89
  356.1 1.9 dynamic-slice_bitcast_fusion.8
  358.8 3.4 collective-permute-start.25
  364.4 2.7 collective-permute-done.46
  370.9 16.2 %collective-permute-done.25 = bf16[1024,128]{1,0:T(8,128)(2,1)S(1)} collective-permute-done((bf16[1024,128]{1,0:T(8,128)(2,1)}, bf16[1024,128]{1,0:T(8,128)(2,1)S(1)}, u32[]{:S(2)}, u32[]{:S(2)}) %collective-permute-start.25) | collective-permute-done | bytes 262176 | tf_op jit(solution)/shard_map/ppermute | solution.py:23
  395.2 2.1 collective-permute-start.51
  397.5 6.8 %collective-permute-done.53 = bf16[256,512]{1,0:T(8,128)(2,1)S(1)} collective-permute-done((bf16[256,512]{1,0:T(8,128)(2,1)S(1)}, bf16[256,512]{1,0:T(8,128)(2,1)S(1)}, u32[]{:S(2)}, u32[]{:S(2)}) %collective-permute-start.53) | collective-permute-done | bytes 262176 | tf_op jit(solution)/shard_map/ppermute | solution.py:18
  405.9 4.0 collective-permute-done.51
  411.2 3.5 collective-permute-done.55
  415.3 2.0 collective-permute-done.54
  419.4 4.0 collective-permute-start.58
  427.1 4.6 %collective-permute-done.59 = bf16[128,256]{0,1:T(8,128)(2,1)S(1)} collective-permute-done((bf16[128,256]{0,1:T(8,128)(2,1)S(1)}, bf16[128,256]{0,1:T(8,128)(2,1)S(1)}, u32[]{:S(2)}, u32[]{:S(2)}) %collective-permute-start.59) | collective-permute-done | bytes 65568 | tf_op jit(solution)/shard_map/ppermute | solution.py:23
  (196 shorter events, 74.8 us)
Async XLA Ops:
  3.4 34.9 %collective-permute-start = (bf16[192,3072]{1,0:T(8,128)(2,1)S(1)}, bf16[192,3072]{1,0:T(8,128)(2,1)}, u32[]{:S(2)}, u32[]{:S(2)}) collective-permute-start(bf16[192,3072]{1,0:T(8,128)(2,1)S(1)} %bitcast.166), channel_id=1, source_target_pairs={{0,4},{4,0},{8,12},{12,8},{16,20},{20,16},{24,28},{28,24},{1,5},{5... | collective-permute-start | bytes 3538952 | tf_op jit(solution)/shard_map/ppermute | solution.py:18
  4.0 29.2 %collective-permute-start.1 = (bf16[192,3072]{1,0:T(8,128)(2,1)S(1)}, bf16[192,3072]{1,0:T(8,128)(2,1)}, u32[]{:S(2)}, u32[]{:S(2)}) collective-permute-start(bf16[192,3072]{1,0:T(8,128)(2,1)S(1)} %bitcast.167), channel_id=1, source_target_pairs={{0,16},{4,20},{8,24},{12,28},{16,0},{20,4},{24,8},{28,12},{1,17},{... | collective-permute-start | bytes 3538952 | tf_op jit(solution)/shard_map/ppermute | solution.py:18
  6.6 32.1 %collective-permute-start.3 = (bf16[192,3072]{1,0:T(8,128)(2,1)S(1)}, bf16[192,3072]{1,0:T(8,128)(2,1)}, u32[]{:S(2)}, u32[]{:S(2)}) collective-permute-start(bf16[192,3072]{1,0:T(8,128)(2,1)S(1)} %bitcast.168), channel_id=1, source_target_pairs={{0,8},{4,12},{8,0},{12,4},{16,24},{20,28},{24,16},{28,20},{1,9},{5... | collective-permute-start | bytes 3538952 | tf_op jit(solution)/shard_map/ppermute | solution.py:18
  8.3 82.8 %collective-permute-start.7 = (bf16[192,3072]{1,0:T(8,128)(2,1)S(1)}, bf16[192,3072]{1,0:T(8,128)(2,1)}, u32[]{:S(2)}, u32[]{:S(2)}) collective-permute-start(bf16[192,3072]{1,0:T(8,128)(2,1)S(1)} %bitcast.162), channel_id=1, source_target_pairs={{0,4},{4,0},{8,12},{12,8},{16,20},{20,16},{24,28},{28,24},{1,5},{5... | collective-permute-start | bytes 3538952 | tf_op jit(solution)/shard_map/ppermute | solution.py:18
  33.2 29.2 %collective-permute-start.5 = (bf16[192,3072]{1,0:T(8,128)(2,1)}, bf16[192,3072]{1,0:T(8,128)(2,1)}, u32[]{:S(2)}, u32[]{:S(2)}) collective-permute-start(bf16[192,3072]{1,0:T(8,128)(2,1)} %collective-permute-done.1), channel_id=1, source_target_pairs={{0,8},{4,12},{8,0},{12,4},{16,24},{20,28},{24,16},{28,20},{1,9},{5... | collective-permute-start | bytes 3538952 | tf_op jit(solution)/shard_map/ppermute | solution.py:18
  38.3 48.8 %collective-permute-start.8 = (bf16[192,3072]{1,0:T(8,128)(2,1)S(1)}, bf16[192,3072]{1,0:T(8,128)(2,1)S(1)}, u32[]{:S(2)}, u32[]{:S(2)}) collective-permute-start(bf16[192,3072]{1,0:T(8,128)(2,1)S(1)} %bitcast.163), channel_id=1, source_target_pairs={{0,8},{4,12},{8,0},{12,4},{16,24},{20,28},{24,16},{28,20},{1,9},{5... | collective-permute-start | bytes 3538952 | tf_op jit(solution)/shard_map/ppermute | solution.py:18
  38.7 50.2 %collective-permute-start.4 = (bf16[192,3072]{1,0:T(8,128)(2,1)}, bf16[192,3072]{1,0:T(8,128)(2,1)S(1)}, u32[]{:S(2)}, u32[]{:S(2)}) collective-permute-start(bf16[192,3072]{1,0:T(8,128)(2,1)} %collective-permute-done.3), channel_id=1, source_target_pairs={{0,4},{4,0},{8,12},{12,8},{16,20},{20,16},{24,28},{28,24},{1,5},{5... | collective-permute-start | bytes 3538952 | tf_op jit(solution)/shard_map/ppermute | solution.py:18
  41.5 51.3 %collective-permute-start.10 = (bf16[192,3072]{1,0:T(8,128)(2,1)S(1)}, bf16[192,3072]{1,0:T(8,128)(2,1)S(1)}, u32[]{:S(2)}, u32[]{:S(2)}) collective-permute-start(bf16[192,3072]{1,0:T(8,128)(2,1)S(1)} %bitcast.164), channel_id=1, source_target_pairs={{0,16},{4,20},{8,24},{12,28},{16,0},{20,4},{24,8},{28,12},{1,17},{... | collective-permute-start | bytes 3538952 | tf_op jit(solution)/shard_map/ppermute | solution.py:18
  62.4 28.0 %collective-permute-start.6 = (bf16[192,3072]{1,0:T(8,128)(2,1)}, bf16[192,3072]{1,0:T(8,128)(2,1)S(1)}, u32[]{:S(2)}, u32[]{:S(2)}) collective-permute-start(bf16[192,3072]{1,0:T(8,128)(2,1)} %collective-permute-done.5), channel_id=1, source_target_pairs={{0,4},{4,0},{8,12},{12,8},{16,20},{20,16},{24,28},{28,24},{1,5},{5... | collective-permute-start | bytes 3538952 | tf_op jit(solution)/shard_map/ppermute | solution.py:18
  87.1 96.9 %collective-permute-start.29 = (bf16[3072,128]{1,0:T(8,128)(2,1)}, bf16[3072,128]{1,0:T(8,128)(2,1)}, u32[]{:S(2)}, u32[]{:S(2)}) collective-permute-start(bf16[3072,128]{1,0:T(8,128)(2,1)} %bitcast.38.refs_8_), channel_id=1, source_target_pairs={{0,16},{4,20},{8,24},{12,28},{16,0},{20,4},{24,8},{28,12},{1,17},{... | collective-permute-start | bytes 2359304 | tf_op jit(solution)/shard_map/ppermute | solution.py:18
  90.4 41.3 %collective-permute-start.12 = (bf16[192,3072]{1,0:T(8,128)(2,1)S(1)}, bf16[192,3072]{1,0:T(8,128)(2,1)S(1)}, u32[]{:S(2)}, u32[]{:S(2)}) collective-permute-start(bf16[192,3072]{1,0:T(8,128)(2,1)S(1)} %collective-permute-done.8), channel_id=1, source_target_pairs={{0,16},{4,20},{8,24},{12,28},{16,0},{20,4},{24,8},{28,12},{1,17},{... | collective-permute-start | bytes 3538952 | tf_op jit(solution)/shard_map/ppermute | solution.py:18
  91.0 124.5 %collective-permute-start.28 = (bf16[3072,128]{1,0:T(8,128)(2,1)}, bf16[3072,128]{1,0:T(8,128)(2,1)}, u32[]{:S(2)}, u32[]{:S(2)}) collective-permute-start(bf16[3072,128]{1,0:T(8,128)(2,1)} %bitcast.38.refs_8_), channel_id=1, source_target_pairs={{0,8},{4,12},{8,0},{12,4},{16,24},{20,28},{24,16},{28,20},{1,9},{5... | collective-permute-start | bytes 2359304 | tf_op jit(solution)/shard_map/ppermute | solution.py:18
  92.8 39.2 %collective-permute-start.11 = (bf16[192,3072]{1,0:T(8,128)(2,1)S(1)}, bf16[192,3072]{1,0:T(8,128)(2,1)S(1)}, u32[]{:S(2)}, u32[]{:S(2)}) collective-permute-start(bf16[192,3072]{1,0:T(8,128)(2,1)S(1)} %collective-permute-done.10), channel_id=1, source_target_pairs={{0,4},{4,0},{8,12},{12,8},{16,20},{20,16},{24,28},{28,24},{1,5},{5... | collective-permute-start | bytes 3538952 | tf_op jit(solution)/shard_map/ppermute | solution.py:18
  94.4 90.0 %collective-permute-start.31 = (bf16[3072,128]{1,0:T(8,128)(2,1)}, bf16[3072,128]{1,0:T(8,128)(2,1)}, u32[]{:S(2)}, u32[]{:S(2)}) collective-permute-start(bf16[3072,128]{1,0:T(8,128)(2,1)} %bitcast.39.refs_12_), channel_id=1, source_target_pairs={{0,8},{4,12},{8,0},{12,4},{16,24},{20,28},{24,16},{28,20},{1,9},{5... | collective-permute-start | bytes 2359304 | tf_op jit(solution)/shard_map/ppermute | solution.py:18
  132.0 84.0 %collective-permute-start.32 = (bf16[3072,128]{1,0:T(8,128)(2,1)}, bf16[3072,128]{1,0:T(8,128)(2,1)}, u32[]{:S(2)}, u32[]{:S(2)}) collective-permute-start(bf16[3072,128]{1,0:T(8,128)(2,1)} %bitcast.39.refs_12_), channel_id=1, source_target_pairs={{0,16},{4,20},{8,24},{12,28},{16,0},{20,4},{24,8},{28,12},{1,17},{... | collective-permute-start | bytes 2359304 | tf_op jit(solution)/shard_map/ppermute | solution.py:18
  134.5 81.4 %collective-permute-start.19 = (bf16[3072,128]{1,0:T(8,128)(2,1)}, bf16[3072,128]{1,0:T(8,128)(2,1)}, u32[]{:S(2)}, u32[]{:S(2)}) collective-permute-start(bf16[3072,128]{1,0:T(8,128)(2,1)} %bitcast.32.refs_8_), channel_id=1, source_target_pairs={{0,16},{4,20},{8,24},{12,28},{16,0},{20,4},{24,8},{28,12},{1,17},{... | collective-permute-start | bytes 2359304 | tf_op jit(solution)/shard_map/ppermute | solution.py:18
  184.0 32.5 %collective-permute-start.39 = (bf16[3072,128]{1,0:T(8,128)(2,1)}, bf16[3072,128]{1,0:T(8,128)(2,1)}, u32[]{:S(2)}, u32[]{:S(2)}) collective-permute-start(bf16[3072,128]{1,0:T(8,128)(2,1)} %bitcast.44.refs_8_), channel_id=1, source_target_pairs={{0,16},{4,20},{8,24},{12,28},{16,0},{20,4},{24,8},{28,12},{1,17},{... | collective-permute-start | bytes 2359304 | tf_op jit(solution)/shard_map/ppermute | solution.py:18
  184.4 32.2 %collective-permute-start.41 = (bf16[3072,128]{1,0:T(8,128)(2,1)}, bf16[3072,128]{1,0:T(8,128)(2,1)}, u32[]{:S(2)}, u32[]{:S(2)}) collective-permute-start(bf16[3072,128]{1,0:T(8,128)(2,1)} %bitcast.45.refs_12_), channel_id=1, source_target_pairs={{0,8},{4,12},{8,0},{12,4},{16,24},{20,28},{24,16},{28,20},{1,9},{5... | collective-permute-start | bytes 2359304 | tf_op jit(solution)/shard_map/ppermute | solution.py:18
  215.6 19.0 %collective-permute-start.30 = (bf16[3072,128]{1,0:T(8,128)(2,1)}, bf16[3072,128]{1,0:T(8,128)(2,1)S(1)}, u32[]{:S(2)}, u32[]{:S(2)}) collective-permute-start(bf16[3072,128]{1,0:T(8,128)(2,1)} %collective-permute-done.29.refs_10_), channel_id=1, source_target_pairs={{0,8},{4,12},{8,0},{12,4},{16,24},{20,28},{24,16},{28,20},{1,9},{5... | collective-permute-start | bytes 2359304 | tf_op jit(solution)/shard_map/ppermute | solution.py:18
  216.0 37.3 %collective-permute-start.15 = (bf16[128,6144]{1,0:T(8,128)(2,1)}, bf16[128,6144]{1,0:T(8,128)(2,1)}, u32[]{:S(2)}, u32[]{:S(2)}) collective-permute-start(bf16[128,6144]{1,0:T(8,128)(2,1)} %bitcast.74.refs_1_), channel_id=1, source_target_pairs={{0,4},{4,0},{8,12},{12,8},{16,20},{20,16},{24,28},{28,24},{1,5},{5... | collective-permute-start | bytes 4718600 | tf_op jit(solution)/shard_map/ppermute | solution.py:18
  216.0 38.9 %collective-permute-start.16 = (bf16[128,6144]{1,0:T(8,128)(2,1)}, bf16[128,6144]{1,0:T(8,128)(2,1)}, u32[]{:S(2)}, u32[]{:S(2)}) collective-permute-start(bf16[128,6144]{1,0:T(8,128)(2,1)} %bitcast.77.refs_2_), channel_id=1, source_target_pairs={{0,4},{4,0},{8,12},{12,8},{16,20},{20,16},{24,28},{28,24},{1,5},{5... | collective-permute-start | bytes 4718600 | tf_op jit(solution)/shard_map/ppermute | solution.py:18
  216.5 39.9 %collective-permute-start.17 = (bf16[128,6144]{1,0:T(8,128)(2,1)}, bf16[128,6144]{1,0:T(8,128)(2,1)}, u32[]{:S(2)}, u32[]{:S(2)}) collective-permute-start(bf16[128,6144]{1,0:T(8,128)(2,1)} %bitcast.80.refs_3_), channel_id=1, source_target_pairs={{0,4},{4,0},{8,12},{12,8},{16,20},{20,16},{24,28},{28,24},{1,5},{5... | collective-permute-start | bytes 4718600 | tf_op jit(solution)/shard_map/ppermute | solution.py:18
  216.6 40.4 %collective-permute-start.14 = (bf16[128,6144]{1,0:T(8,128)(2,1)S(1)}, bf16[128,6144]{1,0:T(8,128)(2,1)}, u32[]{:S(2)}, u32[]{:S(2)}) collective-permute-start(bf16[128,6144]{1,0:T(8,128)(2,1)S(1)} %bitcast.182), channel_id=1, source_target_pairs={{0,4},{4,0},{8,12},{12,8},{16,20},{20,16},{24,28},{28,24},{1,5},{5... | collective-permute-start | bytes 4718600 | tf_op jit(solution)/shard_map/ppermute | solution.py:18
  234.6 18.2 %collective-permute-start.33 = (bf16[3072,128]{1,0:T(8,128)(2,1)}, bf16[3072,128]{1,0:T(8,128)(2,1)}, u32[]{:S(2)}, u32[]{:S(2)}) collective-permute-start(bf16[3072,128]{1,0:T(8,128)(2,1)} %collective-permute-done.31.refs_13_), channel_id=1, source_target_pairs={{0,16},{4,20},{8,24},{12,28},{16,0},{20,4},{24,8},{28,12},{1,17},{... | collective-permute-start | bytes 2359304 | tf_op jit(solution)/shard_map/ppermute | solution.py:18
  252.8 38.1 %collective-permute-start.38 = (bf16[3072,128]{1,0:T(8,128)(2,1)}, bf16[3072,128]{1,0:T(8,128)(2,1)}, u32[]{:S(2)}, u32[]{:S(2)}) collective-permute-start(bf16[3072,128]{1,0:T(8,128)(2,1)} %bitcast.44.refs_8_), channel_id=1, source_target_pairs={{0,8},{4,12},{8,0},{12,4},{16,24},{20,28},{24,16},{28,20},{1,9},{5... | collective-permute-start | bytes 2359304 | tf_op jit(solution)/shard_map/ppermute | solution.py:18
  253.3 39.2 %collective-permute-start.42 = (bf16[3072,128]{1,0:T(8,128)(2,1)}, bf16[3072,128]{1,0:T(8,128)(2,1)}, u32[]{:S(2)}, u32[]{:S(2)}) collective-permute-start(bf16[3072,128]{1,0:T(8,128)(2,1)} %bitcast.45.refs_12_), channel_id=1, source_target_pairs={{0,16},{4,20},{8,24},{12,28},{16,0},{20,4},{24,8},{28,12},{1,17},{... | collective-permute-start | bytes 2359304 | tf_op jit(solution)/shard_map/ppermute | solution.py:18
  254.9 35.5 %collective-permute-start.21 = (bf16[3072,128]{1,0:T(8,128)(2,1)S(1)}, bf16[3072,128]{1,0:T(8,128)(2,1)}, u32[]{:S(2)}, u32[]{:S(2)}) collective-permute-start(bf16[3072,128]{1,0:T(8,128)(2,1)S(1)} %bitcast.187), channel_id=1, source_target_pairs={{0,8},{4,12},{8,0},{12,4},{16,24},{20,28},{24,16},{28,20},{1,9},{5... | collective-permute-start | bytes 2359304 | tf_op jit(solution)/shard_map/ppermute | solution.py:18
  256.4 50.9 %collective-permute-start.40 = (bf16[3072,128]{1,0:T(8,128)(2,1)}, bf16[3072,128]{1,0:T(8,128)(2,1)}, u32[]{:S(2)}, u32[]{:S(2)}) collective-permute-start(bf16[3072,128]{1,0:T(8,128)(2,1)} %collective-permute-done.39.refs_10_), channel_id=1, source_target_pairs={{0,8},{4,12},{8,0},{12,4},{16,24},{20,28},{24,16},{28,20},{1,9},{5... | collective-permute-start | bytes 2359304 | tf_op jit(solution)/shard_map/ppermute | solution.py:18
  256.9 53.0 %collective-permute-start.43 = (bf16[3072,128]{1,0:T(8,128)(2,1)}, bf16[3072,128]{1,0:T(8,128)(2,1)}, u32[]{:S(2)}, u32[]{:S(2)}) collective-permute-start(bf16[3072,128]{1,0:T(8,128)(2,1)} %collective-permute-done.41.refs_13_), channel_id=1, source_target_pairs={{0,16},{4,20},{8,24},{12,28},{16,0},{20,4},{24,8},{28,12},{1,17},{... | collective-permute-start | bytes 2359304 | tf_op jit(solution)/shard_map/ppermute | solution.py:18
  290.4 36.4 %collective-permute-start.18 = (bf16[3072,128]{1,0:T(8,128)(2,1)}, bf16[3072,128]{1,0:T(8,128)(2,1)}, u32[]{:S(2)}, u32[]{:S(2)}) collective-permute-start(bf16[3072,128]{1,0:T(8,128)(2,1)} %bitcast.32.refs_8_), channel_id=1, source_target_pairs={{0,8},{4,12},{8,0},{12,4},{16,24},{20,28},{24,16},{28,20},{1,9},{5... | collective-permute-start | bytes 2359304 | tf_op jit(solution)/shard_map/ppermute | solution.py:18
  290.9 38.6 %collective-permute-start.22 = (bf16[3072,128]{1,0:T(8,128)(2,1)S(1)}, bf16[3072,128]{1,0:T(8,128)(2,1)}, u32[]{:S(2)}, u32[]{:S(2)}) collective-permute-start(bf16[3072,128]{1,0:T(8,128)(2,1)S(1)} %bitcast.188), channel_id=1, source_target_pairs={{0,16},{4,20},{8,24},{12,28},{16,0},{20,4},{24,8},{28,12},{1,17},{... | collective-permute-start | bytes 2359304 | tf_op jit(solution)/shard_map/ppermute | solution.py:18
  292.5 45.1 %collective-permute-start.20 = (bf16[3072,128]{1,0:T(8,128)(2,1)}, bf16[3072,128]{1,0:T(8,128)(2,1)}, u32[]{:S(2)}, u32[]{:S(2)}) collective-permute-start(bf16[3072,128]{1,0:T(8,128)(2,1)} %collective-permute-done.19.refs_10_), channel_id=1, source_target_pairs={{0,8},{4,12},{8,0},{12,4},{16,24},{20,28},{24,16},{28,20},{1,9},{5... | collective-permute-start | bytes 2359304 | tf_op jit(solution)/shard_map/ppermute | solution.py:18
  307.3 31.9 %collective-permute-start.23 = (bf16[3072,128]{1,0:T(8,128)(2,1)}, bf16[3072,128]{1,0:T(8,128)(2,1)}, u32[]{:S(2)}, u32[]{:S(2)}) collective-permute-start(bf16[3072,128]{1,0:T(8,128)(2,1)} %collective-permute-done.21.refs_13_), channel_id=1, source_target_pairs={{0,16},{4,20},{8,24},{12,28},{16,0},{20,4},{24,8},{28,12},{1,17},{... | collective-permute-start | bytes 2359304 | tf_op jit(solution)/shard_map/ppermute | solution.py:18
  309.9 45.9 %collective-permute-start.34 = (bf16[1024,128]{1,0:T(8,128)(2,1)S(1)}, bf16[1024,128]{1,0:T(8,128)(2,1)S(1)}, u32[]{:S(2)}, u32[]{:S(2)}) collective-permute-start(bf16[1024,128]{1,0:T(8,128)(2,1)S(1)} %get-tuple-element.23), channel_id=1, source_target_pairs={{0,1},{1,0},{2,3},{3,2},{4,5},{5,4},{6,7},{7,6},{8,9},{9,8},{10,11... | collective-permute-start | bytes 786440 | tf_op jit(solution)/shard_map/ppermute | solution.py:23
  326.8 31.2 %collective-permute-start.35 = (bf16[1024,128]{1,0:T(8,128)(2,1)S(1)}, bf16[1024,128]{1,0:T(8,128)(2,1)S(1)}, u32[]{:S(2)}, u32[]{:S(2)}) collective-permute-start(bf16[1024,128]{1,0:T(8,128)(2,1)S(1)} %get-tuple-element.25), channel_id=1, source_target_pairs={{0,2},{1,3},{2,0},{3,1},{4,6},{5,7},{6,4},{7,5},{8,10},{9,11},{10,... | collective-permute-start | bytes 786440 | tf_op jit(solution)/shard_map/ppermute | solution.py:23
  329.5 29.3 %collective-permute-start.36 = (bf16[1024,128]{1,0:T(8,128)(2,1)S(1)}, bf16[1024,128]{1,0:T(8,128)(2,1)S(1)}, u32[]{:S(2)}, u32[]{:S(2)}) collective-permute-start(bf16[1024,128]{1,0:T(8,128)(2,1)S(1)} %get-tuple-element.24), channel_id=1, source_target_pairs={{0,3},{1,2},{2,1},{3,0},{4,7},{5,6},{6,5},{7,4},{8,11},{9,10},{10,... | collective-permute-start | bytes 786440 | tf_op jit(solution)/shard_map/ppermute | solution.py:23
  337.6 25.9 %collective-permute-start.44 = (bf16[1024,128]{1,0:T(8,128)(2,1)S(1)}, bf16[1024,128]{1,0:T(8,128)(2,1)S(1)}, u32[]{:S(2)}, u32[]{:S(2)}) collective-permute-start(bf16[1024,128]{1,0:T(8,128)(2,1)S(1)} %get-tuple-element.20), channel_id=1, source_target_pairs={{0,1},{1,0},{2,3},{3,2},{4,5},{5,4},{6,7},{7,6},{8,9},{9,8},{10,11... | collective-permute-start | bytes 786440 | tf_op jit(solution)/shard_map/ppermute | solution.py:23
  339.2 24.6 %collective-permute-start.45 = (bf16[1024,128]{1,0:T(8,128)(2,1)S(1)}, bf16[1024,128]{1,0:T(8,128)(2,1)S(1)}, u32[]{:S(2)}, u32[]{:S(2)}) collective-permute-start(bf16[1024,128]{1,0:T(8,128)(2,1)S(1)} %get-tuple-element.22), channel_id=1, source_target_pairs={{0,2},{1,3},{2,0},{3,1},{4,6},{5,7},{6,4},{7,5},{8,10},{9,11},{10,... | collective-permute-start | bytes 786440 | tf_op jit(solution)/shard_map/ppermute | solution.py:23
  355.8 11.2 %collective-permute-start.46 = (bf16[1024,128]{1,0:T(8,128)(2,1)S(1)}, bf16[1024,128]{1,0:T(8,128)(2,1)}, u32[]{:S(2)}, u32[]{:S(2)}) collective-permute-start(bf16[1024,128]{1,0:T(8,128)(2,1)S(1)} %get-tuple-element.21), channel_id=1, source_target_pairs={{0,3},{1,2},{2,1},{3,0},{4,7},{5,6},{6,5},{7,4},{8,11},{9,10},{10,... | collective-permute-start | bytes 786440 | tf_op jit(solution)/shard_map/ppermute | solution.py:23
  358.1 12.8 %collective-permute-start.24 = (bf16[1024,128]{1,0:T(8,128)(2,1)}, bf16[1024,128]{1,0:T(8,128)(2,1)S(1)}, u32[]{:S(2)}, u32[]{:S(2)}) collective-permute-start(bf16[1024,128]{1,0:T(8,128)(2,1)} %get-tuple-element.26), channel_id=1, source_target_pairs={{0,1},{1,0},{2,3},{3,2},{4,5},{5,4},{6,7},{7,6},{8,9},{9,8},{10,11... | collective-permute-start | bytes 786440 | tf_op jit(solution)/shard_map/ppermute | solution.py:23
  358.8 28.4 %collective-permute-start.25 = (bf16[1024,128]{1,0:T(8,128)(2,1)}, bf16[1024,128]{1,0:T(8,128)(2,1)S(1)}, u32[]{:S(2)}, u32[]{:S(2)}) collective-permute-start(bf16[1024,128]{1,0:T(8,128)(2,1)} %get-tuple-element.28), channel_id=1, source_target_pairs={{0,2},{1,3},{2,0},{3,1},{4,6},{5,7},{6,4},{7,5},{8,10},{9,11},{10,... | collective-permute-start | bytes 786440 | tf_op jit(solution)/shard_map/ppermute | solution.py:23
  363.5 23.7 %collective-permute-start.26 = (bf16[1024,128]{1,0:T(8,128)(2,1)S(1)}, bf16[1024,128]{1,0:T(8,128)(2,1)S(1)}, u32[]{:S(2)}, u32[]{:S(2)}) collective-permute-start(bf16[1024,128]{1,0:T(8,128)(2,1)S(1)} %get-tuple-element.27), channel_id=1, source_target_pairs={{0,3},{1,2},{2,1},{3,0},{4,7},{5,6},{6,5},{7,4},{8,11},{9,10},{10,... | collective-permute-start | bytes 786440 | tf_op jit(solution)/shard_map/ppermute | solution.py:23
  363.8 31.4 %collective-permute-start.49 = (bf16[256,512]{1,0:T(8,128)(2,1)S(1)}, bf16[256,512]{1,0:T(8,128)(2,1)S(1)}, u32[]{:S(2)}, u32[]{:S(2)}) collective-permute-start(bf16[256,512]{1,0:T(8,128)(2,1)S(1)} %reshape.106), channel_id=1, source_target_pairs={{0,8},{4,12},{8,0},{12,4},{16,24},{20,28},{24,16},{28,20},{1,9},{5... | collective-permute-start | bytes 786440 | tf_op jit(solution)/shard_map/ppermute | solution.py:18
  367.1 38.5 %collective-permute-start.52 = (bf16[256,512]{1,0:T(8,128)(2,1)S(1)}, bf16[256,512]{1,0:T(8,128)(2,1)S(1)}, u32[]{:S(2)}, u32[]{:S(2)}) collective-permute-start(bf16[256,512]{1,0:T(8,128)(2,1)S(1)} %reshape.106), channel_id=1, source_target_pairs={{0,16},{4,20},{8,24},{12,28},{16,0},{20,4},{24,8},{28,12},{1,17},{... | collective-permute-start | bytes 786440 | tf_op jit(solution)/shard_map/ppermute | solution.py:18
  388.4 22.4 %collective-permute-start.48 = (bf16[256,512]{1,0:T(8,128)(2,1)S(1)}, bf16[256,512]{1,0:T(8,128)(2,1)S(1)}, u32[]{:S(2)}, u32[]{:S(2)}) collective-permute-start(bf16[256,512]{1,0:T(8,128)(2,1)S(1)} %reshape.105), channel_id=1, source_target_pairs={{0,8},{4,12},{8,0},{12,4},{16,24},{20,28},{24,16},{28,20},{1,9},{5... | collective-permute-start | bytes 786440 | tf_op jit(solution)/shard_map/ppermute | solution.py:18
  389.5 15.1 %collective-permute-start.50 = (bf16[256,512]{1,0:T(8,128)(2,1)S(1)}, bf16[256,512]{1,0:T(8,128)(2,1)S(1)}, u32[]{:S(2)}, u32[]{:S(2)}) collective-permute-start(bf16[256,512]{1,0:T(8,128)(2,1)S(1)} %reshape.107), channel_id=1, source_target_pairs={{0,8},{4,12},{8,0},{12,4},{16,24},{20,28},{24,16},{28,20},{1,9},{5... | collective-permute-start | bytes 786440 | tf_op jit(solution)/shard_map/ppermute | solution.py:18
  395.2 14.7 %collective-permute-start.51 = (bf16[256,512]{1,0:T(8,128)(2,1)S(1)}, bf16[256,512]{1,0:T(8,128)(2,1)S(1)}, u32[]{:S(2)}, u32[]{:S(2)}) collective-permute-start(bf16[256,512]{1,0:T(8,128)(2,1)S(1)} %reshape.105), channel_id=1, source_target_pairs={{0,16},{4,20},{8,24},{12,28},{16,0},{20,4},{24,8},{28,12},{1,17},{... | collective-permute-start | bytes 786440 | tf_op jit(solution)/shard_map/ppermute | solution.py:18
  404.3 10.4 %collective-permute-start.55 = (bf16[256,512]{1,0:T(8,128)(2,1)S(1)}, bf16[256,512]{1,0:T(8,128)(2,1)S(1)}, u32[]{:S(2)}, u32[]{:S(2)}) collective-permute-start(bf16[256,512]{1,0:T(8,128)(2,1)S(1)} %collective-permute-done.49), channel_id=1, source_target_pairs={{0,16},{4,20},{8,24},{12,28},{16,0},{20,4},{24,8},{28,12},{1,17},{... | collective-permute-start | bytes 786440 | tf_op jit(solution)/shard_map/ppermute | solution.py:18
  (29 other events, 336.8 us)
where the time goes:
time: 437 us; the launch traced here: 433 us
  waiting for transfers between devices  213 us (49%)
  local copies, waits for them, and re-layouts  59.3 us (14%)
  starting transfers between devices  59 us (14%)
  matrix products  52.1 us (12%)
  Pallas kernels  42.4 us (10%)
  other arithmetic  4.8 us (1%)
    ppermute x49, waiting for transfers between devices, hop(): return lax.ppermute(value, 'lb', [(i, i ^ mask) for i in range(devices)])  190 us
    pallas_call x3, Pallas kernels, right_product(): pl.pallas_call(functools.partial(right_kernel, chips, blocks, steps), out...  42.4 us
    ppermute x49, starting transfers between devices, hop(): return lax.ppermute(value, 'lb', [(i, i ^ mask) for i in range(devices)])  39.1 us
    dot_general x4, matrix products, shards(): jnp.dot(rows.reshape(channels * block_rows, full_bond), state, preferred_...  29.6 us
    ppermute x12, waiting for transfers between devices, rb_hop(): return lax.ppermute(value, 'rb', [(i, i ^ mask) for i in range(devices)])  23.5 us
    ppermute x12, starting transfers between devices, rb_hop(): return lax.ppermute(value, 'rb', [(i, i ^ mask) for i in range(devices)])  20 us
    dot_general x4, matrix products, shards(): jnp.einsum('avyx,alxr->lyvr', combined, left_part, precision=lax.Precisio...  19 us
    reshape x4, local copies, waits for them, and re-layouts, shards(): left_part = left_part.reshape(channels, block_rows, states, local_right)  12.7 us
  transfers between devices with their start and end apart: 61, of which 21 were waited for; matrix products, arithmetic and copies ran while one was open for 26% of the time, Pallas kernels for 10%

commit v1 on v0

--- a/solution.py
+++ b/solution.py
@@ -10,7 +10,7 @@
 
 
 BOND_WIDTH = 3072
-ROW_BLOCKS = 4
+ROW_BLOCKS = 2
 
 
 def hop(value, mask):
@@ -144,7 +144,7 @@
                 start = (me ^ (2 * q + e)) * piece_rows + half * half_rows
                 state = lax.dynamic_update_slice(state, value, (start, jnp.int32(0)))
 
-    combined = combine_operators(operator_left, operator_right)
+    combined = combine_operators(operator_left, operator_right).astype(jnp.bfloat16)
     block_rows = row_count // ROW_BLOCKS
     mixed, mixed_sibling = [], []
     for s in range(ROW_BLOCKS):
@@ -153,10 +153,10 @@
             rows.reshape(channels * block_rows, full_bond),
             state,
             preferred_element_type=jnp.float32,
-        )
+        ).astype(jnp.bfloat16)
         left_part = left_part.reshape(channels, block_rows, states, local_right)
         part = jnp.einsum(
-            "avyx,alxr->lyvr", combined, left_part, precision=lax.Precision.HIGHEST
+            "avyx,alxr->lyvr", combined, left_part, preferred_element_type=jnp.float32
         ).astype(jnp.bfloat16)
         part = part.reshape(block_rows * states, channels * local_right)
         mixed.append(part)
@@ -180,7 +180,10 @@
         mine.append(applied[:own_rows])
         theirs.append(hop(applied[own_rows:], 1))
         flat_tiles = applied.reshape(2 * row_count, states * width)
-        others = spread(flat_tiles, orders[j % 2])
+        if j < chunks - 1:
+            others = spread(flat_tiles, orders[j % 2])
+        else:
+            others = {q: hop(flat_tiles, 2 * q) if q else flat_tiles for q in range(chips)}
         for q in range(chips):
             gram[q] = gram[q] + lax.dot_general(
                 flat_tiles,
@@ -197,12 +200,22 @@
     applied = applied.reshape(row_count, states, 2 * tile_width)
 
     gram = jnp.stack(gram)
-    received = hop(gram[:, row_count:].astype(jnp.bfloat16), 1).astype(jnp.float32)
-    kept = gram[:, :row_count]
-    own_first = kept[:, :, :row_count] + received[:, :, row_count:]
-    own_second = kept[:, :, row_count:] + received[:, :, :row_count]
-    gram = jnp.concatenate(ordered(own_first, own_second), axis=2).astype(jnp.bfloat16)
-    block = exchange(gram, chip)
+    gram = jnp.concatenate(ordered(gram[:, :, :row_count], gram[:, :, row_count:]), axis=2)
+    gram = gram.astype(jnp.bfloat16)
+    rb_size = lax.axis_size("rb")
+    block = 0.0
+    for e in range(2):
+        for mask in range(rb_size):
+            part = lax.dynamic_index_in_dim(gram, (z ^ mask) ^ chip, 0, keepdims=False)
+            part = part[e * row_count : (e + 1) * row_count]
+            if e or mask:
+                pairs = [
+                    (b * rb_size + i, (b ^ e) * rb_size + (i ^ mask))
+                    for b in range(tiles)
+                    for i in range(rb_size)
+                ]
+                part = lax.ppermute(part, ("lb", "rb"), pairs)
+            block = block + part.astype(jnp.float32)
     own_label = lax.dynamic_index_in_dim(row_sector, me, keepdims=False)
     labels = lax.dynamic_slice_in_dim(row_sector, 2 * z, 2)
     keep = jnp.repeat(labels == own_label, row_count)[None, :]

time: 437 us -> 445 us (1.018)
  local copies, waits for them, and re-layouts: 59.3 us -> 82.4 us
  matrix products: 52.1 us -> 35.7 us
  starting transfers between devices: 59 us -> 65.1 us
    reshape x4, local copies, waits for them, and re-layouts: 12.7 us -> 33.1 us  [shards(): left_part = left_part.reshape(channels, block_rows, states, local_right)]
    dot_general x4 -> x2, matrix products: 19 us -> 3.28 us  [shards(): jnp.einsum('avyx,alxr->lyvr', combined, left_part, preferred_element_type...]
    dot_general x4 -> x0, local copies, waits for them, and re-layouts: 10.7 us -> none  [shards(): jnp.dot(rows.reshape(channels * block_rows, full_bond), state, preferred_...]
    ppermute x12 -> x9, waiting for transfers between devices: 23.5 us -> 13.3 us  [rb_hop(): return lax.ppermute(value, 'rb', [(i, i ^ mask) for i in range(devices)])]
    ppermute x0 -> x7, starting transfers between devices: none -> 9.9 us  [shards(): part = lax.ppermute(part, ('lb', 'rb'), pairs)]
    unnamed x39 -> x43, local copies, waits for them, and re-layouts: 7.25 us -> 15.8 us
    ppermute x12 -> x9, starting transfers between devices: 20 us -> 13.4 us  [rb_hop(): return lax.ppermute(value, 'rb', [(i, i ^ mask) for i in range(devices)])]
    ppermute x49 -> x46, waiting for transfers between devices: 190 us -> 193 us  [hop(): return lax.ppermute(value, 'lb', [(i, i ^ mask) for i in range(devices)])]
  transfers between devices with their start and end apart: 61 -> 62, of which waited for: 21 -> 28; matrix products, arithmetic and copies ran while one was open for 26% -> 16% of each run, Pallas kernels for 10% -> 9%
where the time goes in v1:
time: 445 us; the launch traced here: 442 us
  waiting for transfers between devices  210 us (47%)
  local copies, waits for them, and re-layouts  82.4 us (19%)
  starting transfers between devices  65.1 us (15%)
  Pallas kernels  41.8 us (9%)
  matrix products  35.7 us (8%)
  other arithmetic  4.68 us (1%)
    ppermute x46, waiting for transfers between devices, hop(): return lax.ppermute(value, 'lb', [(i, i ^ mask) for i in range(devices)])  193 us
    ppermute x46, starting transfers between devices, hop(): return lax.ppermute(value, 'lb', [(i, i ^ mask) for i in range(devices)])  41.9 us
    pallas_call x3, Pallas kernels, right_product(): pl.pallas_call(functools.partial(right_kernel, chips, blocks, steps), out...  41.8 us
    reshape x4, local copies, waits for them, and re-layouts, shards(): left_part = left_part.reshape(channels, block_rows, states, local_right)  33.1 us
    dot_general x2, matrix products, shards(): jnp.dot(rows.reshape(channels * block_rows, full_bond), state, preferred_...  28.9 us
    unnamed x43, local copies, waits for them, and re-layouts  15.8 us
    ppermute x9, starting transfers between devices, rb_hop(): return lax.ppermute(value, 'rb', [(i, i ^ mask) for i in range(devices)])  13.4 us
    ppermute x9, waiting for transfers between devices, rb_hop(): return lax.ppermute(value, 'rb', [(i, i ^ mask) for i in range(devices)])  13.3 us
  transfers between devices with their start and end apart: 62, of which 28 were waited for; matrix products, arithmetic and copies ran while one was open for 16% of the time, Pallas kernels for 9%

profile of v1, /device:TPU:0, one launch (start us, length us, event | category | flops | bytes accessed | tf_op | source)
XLA Modules:
  0.0 441.6 jit_solution(5121235629975740538)
XLA Ops:
  0.7 2.6 fusion.37
  4.5 3.0 collective-permute-start.1
  10.7 3.3 fusion.35
  14.0 19.7 %collective-permute-done.1 = bf16[192,3072]{1,0:T(8,128)(2,1)} collective-permute-done((bf16[192,3072]{1,0:T(8,128)(2,1)}, bf16[192,3072]{1,0:T(8,128)(2,1)}, u32[]{:S(2)}, u32[]{:S(2)}) %collective-permute-start.1) | collective-permute-done | bytes 1179680 | tf_op jit(solution)/shard_map/ppermute | solution.py:18
  33.7 1.7 collective-permute-start.5
  36.1 2.7 broadcast_in_dim.20
  41.8 20.1 %collective-permute-done.8 = bf16[192,3072]{1,0:T(8,128)(2,1)} collective-permute-done((bf16[192,3072]{1,0:T(8,128)(2,1)}, bf16[192,3072]{1,0:T(8,128)(2,1)}, u32[]{:S(2)}, u32[]{:S(2)}) %collective-permute-start.8) | collective-permute-done | bytes 1179680 | tf_op jit(solution)/shard_map/ppermute | solution.py:18
  64.8 21.9 %collective-permute-done.5 = bf16[192,3072]{1,0:T(8,128)(2,1)} collective-permute-done((bf16[192,3072]{1,0:T(8,128)(2,1)}, bf16[192,3072]{1,0:T(8,128)(2,1)}, u32[]{:S(2)}, u32[]{:S(2)}) %collective-permute-start.5) | collective-permute-done | bytes 1179680 | tf_op jit(solution)/shard_map/ppermute | solution.py:18
  90.2 3.7 collective-permute-done.12
  99.3 6.4 %copy-done.2 = bf16[3072,3072]{1,0:T(8,128)(2,1)} copy-done((bf16[3072,3072]{1,0:T(8,128)(2,1)}, bf16[3072,3072]{1,0:T(8,128)(2,1)S(1)}, u32[]{:S(2)}) %copy-start.2) | copy-done | bytes 18874392
  105.7 14.9 %fusion = bf16[512,3072]{0,1:T(8,128)(2,1)} fusion(bf16[3072,3072]{1,0:T(8,128)(2,1)S(1)} %constant_dynamic-update-slice_fusion, bf16[512,3072]{1,0:T(8,128)(2,1)} %bitcast.143), kind=kOutput, calls=%fused_computation.4 | convolution fusion | flops 9665249280 | bytes 25165824 | tf_op jit(solution)/shard_map/dot_general | solution.py:152
  120.6 8.9 %reshape.103 = bf16[8,64,4,768]{1,0,3,2:T(8,128)(2,1)} reshape(bf16[512,3072]{0,1:T(8,128)(2,1)} %fusion) | data formatting | bytes 6291456 | tf_op jit(solution)/shard_map/reshape | solution.py:157
  129.5 9.5 %copy.25 = bf16[8,64,4,768,1]{3,2,0,4,1:T(4,128)(2,1)S(1)} copy(bf16[8,64,4,768,1]{1,0,3,2,4:T(8,128)(2,1)} %bitcast.132) | data formatting | bytes 6291456 | tf_op jit(solution)/shard_map/reshape | solution.py:157
  140.6 2.6 copy.49
  143.7 14.0 %fusion.1 = bf16[512,3072]{0,1:T(8,128)(2,1)S(1)} fusion(bf16[3072,3072]{1,0:T(8,128)(2,1)} %copy-done.2, bf16[512,3072]{1,0:T(8,128)(2,1)S(1)} %bitcast.142), kind=kOutput, calls=%fused_computation.5 | convolution fusion | flops 9665249280 | bytes 25165824 | tf_op jit(solution)/shard_map/dot_general | solution.py:152
  157.7 5.6 %reshape.104 = bf16[8,64,4,768]{1,0,3,2:T(8,128)(2,1)} reshape(bf16[512,3072]{0,1:T(8,128)(2,1)S(1)} %fusion.1) | data formatting | bytes 6291456 | tf_op jit(solution)/shard_map/reshape | solution.py:157
  163.3 9.1 %copy.28 = bf16[8,64,4,768,1]{3,2,0,4,1:T(4,128)(2,1)S(1)} copy(bf16[8,64,4,768,1]{1,0,3,2,4:T(8,128)(2,1)} %bitcast.133) | data formatting | bytes 6291456 | tf_op jit(solution)/shard_map/reshape | solution.py:157
  172.4 1.6 bitcast_convert_fusion
  175.1 4.9 %fusion.36 = (bf16[4,768,128]{2,1,0:T(8,128)(2,1)}, bf16[4,768,128]{2,1,0:T(8,128)(2,1)S(1)}, bf16[4,768,128]{2,1,0:T(8,128)(2,1)S(1)}, bf16[4,768,128]{2,1,0:T(...) fusion(bf16[8,768,384]{2,1,0:T(8,128)(2,1)} %param.10), kind=kLoop, calls=%fused_computation.102 | loop fusion | bytes 9437184 | tf_op jit(solution)/shard_map/slice | solution.py:174
  183.6 16.0 %collective-permute-done.27.refs_6_ = bf16[3072,128]{1,0:T(8,128)(2,1)} collective-permute-done((bf16[3072,128]{1,0:T(8,128)(2,1)S(1)}, bf16[3072,128]{1,0:T(8,128)(2,1)}, u32[]{:S(2)}, u32[]{:S(2)}) %collective-permute-start.27) | collective-permute-done | bytes 786464 | tf_op jit(solution)/shard_map/ppermute | solution.py:18
  202.6 14.9 %collective-permute-done.26.refs_5_ = bf16[3072,128]{1,0:T(8,128)(2,1)S(1)} collective-permute-done((bf16[3072,128]{1,0:T(8,128)(2,1)S(1)}, bf16[3072,128]{1,0:T(8,128)(2,1)S(1)}, u32[]{:S(2)}, u32[]{:S(2)}) %collective-permute-start.26) | collective-permute-done | bytes 786464 | tf_op jit(solution)/shard_map/ppermute | solution.py:18
  220.3 16.6 %collective-permute-done.17.refs_6_ = bf16[3072,128]{1,0:T(8,128)(2,1)} collective-permute-done((bf16[3072,128]{1,0:T(8,128)(2,1)S(1)}, bf16[3072,128]{1,0:T(8,128)(2,1)}, u32[]{:S(2)}, u32[]{:S(2)}) %collective-permute-start.17) | collective-permute-done | bytes 786464 | tf_op jit(solution)/shard_map/ppermute | solution.py:18
  237.3 14.6 %collective-permute-done.37.refs_6_ = bf16[3072,128]{1,0:T(8,128)(2,1)S(1)} collective-permute-done((bf16[3072,128]{1,0:T(8,128)(2,1)S(1)}, bf16[3072,128]{1,0:T(8,128)(2,1)S(1)}, u32[]{:S(2)}, u32[]{:S(2)}) %collective-permute-start.37) | collective-permute-done | bytes 786464 | tf_op jit(solution)/shard_map/ppermute | solution.py:18
  256.4 17.0 %collective-permute-done.31.refs_11_ = bf16[3072,128]{1,0:T(8,128)(2,1)} collective-permute-done((bf16[3072,128]{1,0:T(8,128)(2,1)}, bf16[3072,128]{1,0:T(8,128)(2,1)}, u32[]{:S(2)}, u32[]{:S(2)}) %collective-permute-start.31) | collective-permute-done | bytes 786464 | tf_op jit(solution)/shard_map/ppermute | solution.py:18
  273.8 1.7 collective-permute-start.38
  277.7 13.9 %right_product.4 = bf16[4,1024,128]{2,1,0:T(8,128)(2,1)} custom-call(bf16[256,6144]{1,0:T(8,128)(2,1)} %bitcast.62.refs_0_, bf16[256,6144]{1,0:T(8,128)(2,1)} %bitcast.139, bf16[256,6144]{1,0:T(8,128)(2,1)} %collective-permute-done.14.refs_2_, bf16[256,6144]{1,0:T(8,128)(2,1)} %collective-permute-done.15.refs_3_, bf16[3072,128]{1,0:T(8,128)(2,1)} %bitcast.158, ...), custom_call_target="tpu_custom_call" | custom-call | flops 6442450944 | bytes 18874368 | tf_op jit(solution)/shard_map/right_product/pallas_call | solution.py:89
  291.6 2.6 collective-permute-done.19.refs_9_
  294.5 1.7 collective-permute-start.20
  297.8 13.3 %collective-permute-done.38.refs_7_ = bf16[3072,128]{1,0:T(8,128)(2,1)} collective-permute-done((bf16[3072,128]{1,0:T(8,128)(2,1)}, bf16[3072,128]{1,0:T(8,128)(2,1)}, u32[]{:S(2)}, u32[]{:S(2)}) %collective-permute-start.38) | collective-permute-done | bytes 786464 | tf_op jit(solution)/shard_map/ppermute | solution.py:18
  316.2 13.8 %right_product.5 = bf16[4,1024,128]{2,1,0:T(8,128)(2,1)} custom-call(bf16[256,6144]{1,0:T(8,128)(2,1)} %bitcast.62.refs_0_, bf16[256,6144]{1,0:T(8,128)(2,1)} %bitcast.140, bf16[256,6144]{1,0:T(8,128)(2,1)} %collective-permute-done.14.refs_2_, bf16[256,6144]{1,0:T(8,128)(2,1)} %collective-permute-done.15.refs_3_, bf16[3072,128]{1,0:T(8,128)(2,1)} %bitcast.152, ...), custom_call_target="tpu_custom_call" | custom-call | flops 6442450944 | bytes 18874368 | tf_op jit(solution)/shard_map/right_product/pallas_call | solution.py:89
  331.2 2.7 collective-permute-start.33
  334.1 6.7 %collective-permute-done.18.refs_7_ = bf16[3072,128]{1,0:T(8,128)(2,1)} collective-permute-done((bf16[3072,128]{1,0:T(8,128)(2,1)}, bf16[3072,128]{1,0:T(8,128)(2,1)}, u32[]{:S(2)}, u32[]{:S(2)}) %collective-permute-start.18) | collective-permute-done | bytes 786464 | tf_op jit(solution)/shard_map/ppermute | solution.py:18
  342.4 2.6 collective-permute-start.43
  345.0 14.0 %right_product.3 = bf16[4,1024,128]{2,1,0:T(8,128)(2,1)} custom-call(bf16[256,6144]{1,0:T(8,128)(2,1)} %bitcast.62.refs_0_, bf16[256,6144]{1,0:T(8,128)(2,1)} %bitcast.141, bf16[256,6144]{1,0:T(8,128)(2,1)} %collective-permute-done.14.refs_2_, bf16[256,6144]{1,0:T(8,128)(2,1)} %collective-permute-done.15.refs_3_, bf16[3072,128]{1,0:T(8,128)(2,1)} %bitcast.148, ...), custom_call_target="tpu_custom_call" | custom-call | flops 6442450944 | bytes 18874368 | tf_op jit(solution)/shard_map/right_product/pallas_call | solution.py:89
  359.3 1.9 dynamic-slice_bitcast_fusion.8
  361.9 3.5 collective-permute-start.23
  367.5 2.6 collective-permute-done.44
  370.1 5.9 %collective-permute-start.50 = (bf16[256,512]{1,0:T(8,128)(2,1)S(1)}, bf16[256,512]{1,0:T(8,128)(2,1)S(1)}, u32[]{:S(2)}, u32[]{:S(2)}) collective-permute-start(bf16[256,512]{1,0:T(8,128)(2,1)S(1)} %reshape.89), channel_id=1, source_target_pairs={{0,16},{4,20},{8,24},{12,28},{16,0},{20,4},{24,8},{28,12},{1,17},{... | collective-permute-start | bytes 786440 | tf_op jit(solution)/shard_map/ppermute | solution.py:18
  378.2 10.6 %collective-permute-done.23 = bf16[1024,128]{1,0:T(8,128)(2,1)} collective-permute-done((bf16[1024,128]{1,0:T(8,128)(2,1)}, bf16[1024,128]{1,0:T(8,128)(2,1)}, u32[]{:S(2)}, u32[]{:S(2)}) %collective-permute-start.23) | collective-permute-done | bytes 262176 | tf_op jit(solution)/shard_map/ppermute | solution.py:23
  396.9 2.8 collective-permute-start.51
  400.7 1.7 collective-permute-start.54
  403.4 9.1 %collective-permute-done.51 = bf16[256,512]{1,0:T(8,128)(2,1)S(1)} collective-permute-done((bf16[256,512]{1,0:T(8,128)(2,1)S(1)}, bf16[256,512]{1,0:T(8,128)(2,1)S(1)}, u32[]{:S(2)}, u32[]{:S(2)}) %collective-permute-start.51) | collective-permute-done | bytes 262176 | tf_op jit(solution)/shard_map/ppermute | solution.py:18
  413.0 5.1 %collective-permute-done.49 = bf16[256,512]{1,0:T(8,128)(2,1)S(1)} collective-permute-done((bf16[256,512]{1,0:T(8,128)(2,1)S(1)}, bf16[256,512]{1,0:T(8,128)(2,1)S(1)}, u32[]{:S(2)}, u32[]{:S(2)}) %collective-permute-start.49) | collective-permute-done | bytes 262176 | tf_op jit(solution)/shard_map/ppermute | solution.py:18
  419.3 3.9 collective-permute-done.53
  423.4 1.9 collective-permute-done.52
  425.8 3.0 collective-permute-start.55
  431.6 2.6 collective-permute-start.60
  437.7 2.8 collective-permute-done.61
  (194 shorter events, 74.0 us)
Async XLA Ops:
  4.5 29.3 %collective-permute-start.1 = (bf16[192,3072]{1,0:T(8,128)(2,1)}, bf16[192,3072]{1,0:T(8,128)(2,1)}, u32[]{:S(2)}, u32[]{:S(2)}) collective-permute-start(bf16[192,3072]{1,0:T(8,128)(2,1)} %bitcast.56), channel_id=1, source_target_pairs={{0,16},{4,20},{8,24},{12,28},{16,0},{20,4},{24,8},{28,12},{1,17},{... | collective-permute-start | bytes 3538952 | tf_op jit(solution)/shard_map/ppermute | solution.py:18
  7.5 32.8 %collective-permute-start = (bf16[192,3072]{1,0:T(8,128)(2,1)}, bf16[192,3072]{1,0:T(8,128)(2,1)}, u32[]{:S(2)}, u32[]{:S(2)}) collective-permute-start(bf16[192,3072]{1,0:T(8,128)(2,1)} %bitcast.56), channel_id=1, source_target_pairs={{0,4},{4,0},{8,12},{12,8},{16,20},{20,16},{24,28},{28,24},{1,5},{5... | collective-permute-start | bytes 3538952 | tf_op jit(solution)/shard_map/ppermute | solution.py:18
  7.5 34.4 %collective-permute-start.3 = (bf16[192,3072]{1,0:T(8,128)(2,1)}, bf16[192,3072]{1,0:T(8,128)(2,1)}, u32[]{:S(2)}, u32[]{:S(2)}) collective-permute-start(bf16[192,3072]{1,0:T(8,128)(2,1)} %bitcast.56), channel_id=1, source_target_pairs={{0,8},{4,12},{8,0},{12,4},{16,24},{20,28},{24,16},{28,20},{1,9},{5... | collective-permute-start | bytes 3538952 | tf_op jit(solution)/shard_map/ppermute | solution.py:18
  10.1 51.8 %collective-permute-start.8 = (bf16[192,3072]{1,0:T(8,128)(2,1)}, bf16[192,3072]{1,0:T(8,128)(2,1)}, u32[]{:S(2)}, u32[]{:S(2)}) collective-permute-start(bf16[192,3072]{1,0:T(8,128)(2,1)} %bitcast.58), channel_id=1, source_target_pairs={{0,8},{4,12},{8,0},{12,4},{16,24},{20,28},{24,16},{28,20},{1,9},{5... | collective-permute-start | bytes 3538952 | tf_op jit(solution)/shard_map/ppermute | solution.py:18
  33.7 31.0 %collective-permute-start.2 = (bf16[192,3072]{1,0:T(8,128)(2,1)}, bf16[192,3072]{1,0:T(8,128)(2,1)}, u32[]{:S(2)}, u32[]{:S(2)}) collective-permute-start(bf16[192,3072]{1,0:T(8,128)(2,1)} %collective-permute-done.1), channel_id=1, source_target_pairs={{0,4},{4,0},{8,12},{12,8},{16,20},{20,16},{24,28},{28,24},{1,5},{5... | collective-permute-start | bytes 3538952 | tf_op jit(solution)/shard_map/ppermute | solution.py:18
  33.7 53.0 %collective-permute-start.5 = (bf16[192,3072]{1,0:T(8,128)(2,1)}, bf16[192,3072]{1,0:T(8,128)(2,1)}, u32[]{:S(2)}, u32[]{:S(2)}) collective-permute-start(bf16[192,3072]{1,0:T(8,128)(2,1)} %collective-permute-done.1), channel_id=1, source_target_pairs={{0,8},{4,12},{8,0},{12,4},{16,24},{20,28},{24,16},{28,20},{1,9},{5... | collective-permute-start | bytes 3538952 | tf_op jit(solution)/shard_map/ppermute | solution.py:18
  40.2 49.3 %collective-permute-start.10 = (bf16[192,3072]{1,0:T(8,128)(2,1)}, bf16[192,3072]{1,0:T(8,128)(2,1)S(1)}, u32[]{:S(2)}, u32[]{:S(2)}) collective-permute-start(bf16[192,3072]{1,0:T(8,128)(2,1)} %bitcast.58), channel_id=1, source_target_pairs={{0,16},{4,20},{8,24},{12,28},{16,0},{20,4},{24,8},{28,12},{1,17},{... | collective-permute-start | bytes 3538952 | tf_op jit(solution)/shard_map/ppermute | solution.py:18
  41.8 48.3 %collective-permute-start.4 = (bf16[192,3072]{1,0:T(8,128)(2,1)}, bf16[192,3072]{1,0:T(8,128)(2,1)S(1)}, u32[]{:S(2)}, u32[]{:S(2)}) collective-permute-start(bf16[192,3072]{1,0:T(8,128)(2,1)} %collective-permute-done.3), channel_id=1, source_target_pairs={{0,4},{4,0},{8,12},{12,8},{16,20},{20,16},{24,28},{28,24},{1,5},{5... | collective-permute-start | bytes 3538952 | tf_op jit(solution)/shard_map/ppermute | solution.py:18
  61.9 32.0 %collective-permute-start.12 = (bf16[192,3072]{1,0:T(8,128)(2,1)}, bf16[192,3072]{1,0:T(8,128)(2,1)S(1)}, u32[]{:S(2)}, u32[]{:S(2)}) collective-permute-start(bf16[192,3072]{1,0:T(8,128)(2,1)} %collective-permute-done.8), channel_id=1, source_target_pairs={{0,16},{4,20},{8,24},{12,28},{16,0},{20,4},{24,8},{28,12},{1,17},{... | collective-permute-start | bytes 3538952 | tf_op jit(solution)/shard_map/ppermute | solution.py:18
  64.7 32.3 %collective-permute-start.7 = (bf16[192,3072]{1,0:T(8,128)(2,1)}, bf16[192,3072]{1,0:T(8,128)(2,1)S(1)}, u32[]{:S(2)}, u32[]{:S(2)}) collective-permute-start(bf16[192,3072]{1,0:T(8,128)(2,1)} %bitcast.58), channel_id=1, source_target_pairs={{0,4},{4,0},{8,12},{12,8},{16,20},{20,16},{24,28},{28,24},{1,5},{5... | collective-permute-start | bytes 3538952 | tf_op jit(solution)/shard_map/ppermute | solution.py:18
  89.5 9.0 %collective-permute-start.9 = (bf16[192,3072]{1,0:T(8,128)(2,1)}, bf16[192,3072]{1,0:T(8,128)(2,1)S(1)}, u32[]{:S(2)}, u32[]{:S(2)}) collective-permute-start(bf16[192,3072]{1,0:T(8,128)(2,1)} %collective-permute-done.8), channel_id=1, source_target_pairs={{0,4},{4,0},{8,12},{12,8},{16,20},{20,16},{24,28},{28,24},{1,5},{5... | collective-permute-start | bytes 3538952 | tf_op jit(solution)/shard_map/ppermute | solution.py:18
  143.2 130.6 %collective-permute-start.14 = (bf16[256,6144]{1,0:T(8,128)(2,1)}, bf16[256,6144]{1,0:T(8,128)(2,1)}, u32[]{:S(2)}, u32[]{:S(2)}) collective-permute-start(bf16[256,6144]{1,0:T(8,128)(2,1)} %bitcast.62.refs_0_), channel_id=1, source_target_pairs={{0,4},{4,0},{8,12},{12,8},{16,20},{20,16},{24,28},{28,24},{1,5},{5... | collective-permute-start | bytes 9437192 | tf_op jit(solution)/shard_map/ppermute | solution.py:18
  175.0 100.5 %collective-permute-start.15 = (bf16[256,6144]{1,0:T(8,128)(2,1)S(1)}, bf16[256,6144]{1,0:T(8,128)(2,1)}, u32[]{:S(2)}, u32[]{:S(2)}) collective-permute-start(bf16[256,6144]{1,0:T(8,128)(2,1)S(1)} %bitcast.138), channel_id=1, source_target_pairs={{0,4},{4,0},{8,12},{12,8},{16,20},{20,16},{24,28},{28,24},{1,5},{5... | collective-permute-start | bytes 9437192 | tf_op jit(solution)/shard_map/ppermute | solution.py:18
  180.0 19.6 %collective-permute-start.27 = (bf16[3072,128]{1,0:T(8,128)(2,1)S(1)}, bf16[3072,128]{1,0:T(8,128)(2,1)}, u32[]{:S(2)}, u32[]{:S(2)}) collective-permute-start(bf16[3072,128]{1,0:T(8,128)(2,1)S(1)} %bitcast.156), channel_id=1, source_target_pairs={{0,16},{4,20},{8,24},{12,28},{16,0},{20,4},{24,8},{28,12},{1,17},{... | collective-permute-start | bytes 2359304 | tf_op jit(solution)/shard_map/ppermute | solution.py:18
  181.6 20.5 %collective-permute-start.29 = (bf16[3072,128]{1,0:T(8,128)(2,1)S(1)}, bf16[3072,128]{1,0:T(8,128)(2,1)}, u32[]{:S(2)}, u32[]{:S(2)}) collective-permute-start(bf16[3072,128]{1,0:T(8,128)(2,1)S(1)} %bitcast.153), channel_id=1, source_target_pairs={{0,8},{4,12},{8,0},{12,4},{16,24},{20,28},{24,16},{28,20},{1,9},{5... | collective-permute-start | bytes 2359304 | tf_op jit(solution)/shard_map/ppermute | solution.py:18
  182.1 35.4 %collective-permute-start.26 = (bf16[3072,128]{1,0:T(8,128)(2,1)S(1)}, bf16[3072,128]{1,0:T(8,128)(2,1)S(1)}, u32[]{:S(2)}, u32[]{:S(2)}) collective-permute-start(bf16[3072,128]{1,0:T(8,128)(2,1)S(1)} %bitcast.157), channel_id=1, source_target_pairs={{0,8},{4,12},{8,0},{12,4},{16,24},{20,28},{24,16},{28,20},{1,9},{5... | collective-permute-start | bytes 2359304 | tf_op jit(solution)/shard_map/ppermute | solution.py:18
  199.6 20.4 %collective-permute-start.30 = (bf16[3072,128]{1,0:T(8,128)(2,1)S(1)}, bf16[3072,128]{1,0:T(8,128)(2,1)S(1)}, u32[]{:S(2)}, u32[]{:S(2)}) collective-permute-start(bf16[3072,128]{1,0:T(8,128)(2,1)S(1)} %bitcast.154), channel_id=1, source_target_pairs={{0,16},{4,20},{8,24},{12,28},{16,0},{20,4},{24,8},{28,12},{1,17},{... | collective-permute-start | bytes 2359304 | tf_op jit(solution)/shard_map/ppermute | solution.py:18
  202.1 34.8 %collective-permute-start.17 = (bf16[3072,128]{1,0:T(8,128)(2,1)S(1)}, bf16[3072,128]{1,0:T(8,128)(2,1)}, u32[]{:S(2)}, u32[]{:S(2)}) collective-permute-start(bf16[3072,128]{1,0:T(8,128)(2,1)S(1)} %bitcast.147), channel_id=1, source_target_pairs={{0,16},{4,20},{8,24},{12,28},{16,0},{20,4},{24,8},{28,12},{1,17},{... | collective-permute-start | bytes 2359304 | tf_op jit(solution)/shard_map/ppermute | solution.py:18
  218.5 33.4 %collective-permute-start.37 = (bf16[3072,128]{1,0:T(8,128)(2,1)S(1)}, bf16[3072,128]{1,0:T(8,128)(2,1)S(1)}, u32[]{:S(2)}, u32[]{:S(2)}) collective-permute-start(bf16[3072,128]{1,0:T(8,128)(2,1)S(1)} %bitcast.150), channel_id=1, source_target_pairs={{0,16},{4,20},{8,24},{12,28},{16,0},{20,4},{24,8},{28,12},{1,17},{... | collective-permute-start | bytes 2359304 | tf_op jit(solution)/shard_map/ppermute | solution.py:18
  220.0 35.6 %collective-permute-start.39 = (bf16[3072,128]{1,0:T(8,128)(2,1)}, bf16[3072,128]{1,0:T(8,128)(2,1)}, u32[]{:S(2)}, u32[]{:S(2)}) collective-permute-start(bf16[3072,128]{1,0:T(8,128)(2,1)} %bitcast.31.refs_8_), channel_id=1, source_target_pairs={{0,8},{4,12},{8,0},{12,4},{16,24},{20,28},{24,16},{28,20},{1,9},{5... | collective-permute-start | bytes 2359304 | tf_op jit(solution)/shard_map/ppermute | solution.py:18
  237.0 19.2 %collective-permute-start.28 = (bf16[3072,128]{1,0:T(8,128)(2,1)}, bf16[3072,128]{1,0:T(8,128)(2,1)}, u32[]{:S(2)}, u32[]{:S(2)}) collective-permute-start(bf16[3072,128]{1,0:T(8,128)(2,1)} %collective-permute-done.27.refs_6_), channel_id=1, source_target_pairs={{0,8},{4,12},{8,0},{12,4},{16,24},{20,28},{24,16},{28,20},{1,9},{5... | collective-permute-start | bytes 2359304 | tf_op jit(solution)/shard_map/ppermute | solution.py:18
  252.7 20.7 %collective-permute-start.31 = (bf16[3072,128]{1,0:T(8,128)(2,1)}, bf16[3072,128]{1,0:T(8,128)(2,1)}, u32[]{:S(2)}, u32[]{:S(2)}) collective-permute-start(bf16[3072,128]{1,0:T(8,128)(2,1)} %collective-permute-done.29.refs_9_), channel_id=1, source_target_pairs={{0,16},{4,20},{8,24},{12,28},{16,0},{20,4},{24,8},{28,12},{1,17},{... | collective-permute-start | bytes 2359304 | tf_op jit(solution)/shard_map/ppermute | solution.py:18
  255.6 39.0 %collective-permute-start.36 = (bf16[3072,128]{1,0:T(8,128)(2,1)}, bf16[3072,128]{1,0:T(8,128)(2,1)}, u32[]{:S(2)}, u32[]{:S(2)}) collective-permute-start(bf16[3072,128]{1,0:T(8,128)(2,1)} %bitcast.151), channel_id=1, source_target_pairs={{0,8},{4,12},{8,0},{12,4},{16,24},{20,28},{24,16},{28,20},{1,9},{5... | collective-permute-start | bytes 2359304 | tf_op jit(solution)/shard_map/ppermute | solution.py:18
  256.1 40.1 %collective-permute-start.40 = (bf16[3072,128]{1,0:T(8,128)(2,1)}, bf16[3072,128]{1,0:T(8,128)(2,1)}, u32[]{:S(2)}, u32[]{:S(2)}) collective-permute-start(bf16[3072,128]{1,0:T(8,128)(2,1)} %bitcast.31.refs_8_), channel_id=1, source_target_pairs={{0,16},{4,20},{8,24},{12,28},{16,0},{20,4},{24,8},{28,12},{1,17},{... | collective-permute-start | bytes 2359304 | tf_op jit(solution)/shard_map/ppermute | solution.py:18
  273.5 20.7 %collective-permute-start.19 = (bf16[3072,128]{1,0:T(8,128)(2,1)}, bf16[3072,128]{1,0:T(8,128)(2,1)}, u32[]{:S(2)}, u32[]{:S(2)}) collective-permute-start(bf16[3072,128]{1,0:T(8,128)(2,1)} %bitcast.144), channel_id=1, source_target_pairs={{0,8},{4,12},{8,0},{12,4},{16,24},{20,28},{24,16},{28,20},{1,9},{5... | collective-permute-start | bytes 2359304 | tf_op jit(solution)/shard_map/ppermute | solution.py:18
  273.8 37.3 %collective-permute-start.38 = (bf16[3072,128]{1,0:T(8,128)(2,1)}, bf16[3072,128]{1,0:T(8,128)(2,1)}, u32[]{:S(2)}, u32[]{:S(2)}) collective-permute-start(bf16[3072,128]{1,0:T(8,128)(2,1)} %copy-done.15), channel_id=1, source_target_pairs={{0,8},{4,12},{8,0},{12,4},{16,24},{20,28},{24,16},{28,20},{1,9},{5... | collective-permute-start | bytes 2359304 | tf_op jit(solution)/shard_map/ppermute | solution.py:18
  275.5 38.2 %collective-permute-start.41 = (bf16[3072,128]{1,0:T(8,128)(2,1)}, bf16[3072,128]{1,0:T(8,128)(2,1)S(1)}, u32[]{:S(2)}, u32[]{:S(2)}) collective-permute-start(bf16[3072,128]{1,0:T(8,128)(2,1)} %collective-permute-done.39.refs_9_), channel_id=1, source_target_pairs={{0,16},{4,20},{8,24},{12,28},{16,0},{20,4},{24,8},{28,12},{1,17},{... | collective-permute-start | bytes 2359304 | tf_op jit(solution)/shard_map/ppermute | solution.py:18
  294.2 37.0 %collective-permute-start.16 = (bf16[3072,128]{1,0:T(8,128)(2,1)S(1)}, bf16[3072,128]{1,0:T(8,128)(2,1)}, u32[]{:S(2)}, u32[]{:S(2)}) collective-permute-start(bf16[3072,128]{1,0:T(8,128)(2,1)S(1)} %bitcast.149), channel_id=1, source_target_pairs={{0,8},{4,12},{8,0},{12,4},{16,24},{20,28},{24,16},{28,20},{1,9},{5... | collective-permute-start | bytes 2359304 | tf_op jit(solution)/shard_map/ppermute | solution.py:18
  294.5 39.4 %collective-permute-start.20 = (bf16[3072,128]{1,0:T(8,128)(2,1)S(1)}, bf16[3072,128]{1,0:T(8,128)(2,1)}, u32[]{:S(2)}, u32[]{:S(2)}) collective-permute-start(bf16[3072,128]{1,0:T(8,128)(2,1)S(1)} %bitcast.146), channel_id=1, source_target_pairs={{0,16},{4,20},{8,24},{12,28},{16,0},{20,4},{24,8},{28,12},{1,17},{... | collective-permute-start | bytes 2359304 | tf_op jit(solution)/shard_map/ppermute | solution.py:18
  296.3 44.6 %collective-permute-start.18 = (bf16[3072,128]{1,0:T(8,128)(2,1)}, bf16[3072,128]{1,0:T(8,128)(2,1)}, u32[]{:S(2)}, u32[]{:S(2)}) collective-permute-start(bf16[3072,128]{1,0:T(8,128)(2,1)} %collective-permute-done.17.refs_6_), channel_id=1, source_target_pairs={{0,8},{4,12},{8,0},{12,4},{16,24},{20,28},{24,16},{28,20},{1,9},{5... | collective-permute-start | bytes 2359304 | tf_op jit(solution)/shard_map/ppermute | solution.py:18
  311.0 31.3 %collective-permute-start.21 = (bf16[3072,128]{1,0:T(8,128)(2,1)}, bf16[3072,128]{1,0:T(8,128)(2,1)}, u32[]{:S(2)}, u32[]{:S(2)}) collective-permute-start(bf16[3072,128]{1,0:T(8,128)(2,1)} %collective-permute-done.19.refs_9_), channel_id=1, source_target_pairs={{0,16},{4,20},{8,24},{12,28},{16,0},{20,4},{24,8},{28,12},{1,17},{... | collective-permute-start | bytes 2359304 | tf_op jit(solution)/shard_map/ppermute | solution.py:18
  314.6 44.3 %collective-permute-start.32 = (bf16[1024,128]{1,0:T(8,128)(2,1)S(1)}, bf16[1024,128]{1,0:T(8,128)(2,1)S(1)}, u32[]{:S(2)}, u32[]{:S(2)}) collective-permute-start(bf16[1024,128]{1,0:T(8,128)(2,1)S(1)} %get-tuple-element.19), channel_id=1, source_target_pairs={{0,1},{1,0},{2,3},{3,2},{4,5},{5,4},{6,7},{7,6},{8,9},{9,8},{10,11... | collective-permute-start | bytes 786440 | tf_op jit(solution)/shard_map/ppermute | solution.py:23
  331.2 30.0 %collective-permute-start.33 = (bf16[1024,128]{1,0:T(8,128)(2,1)S(1)}, bf16[1024,128]{1,0:T(8,128)(2,1)S(1)}, u32[]{:S(2)}, u32[]{:S(2)}) collective-permute-start(bf16[1024,128]{1,0:T(8,128)(2,1)S(1)} %get-tuple-element.21), channel_id=1, source_target_pairs={{0,2},{1,3},{2,0},{3,1},{4,6},{5,7},{6,4},{7,5},{8,10},{9,11},{10,... | collective-permute-start | bytes 786440 | tf_op jit(solution)/shard_map/ppermute | solution.py:23
  333.9 28.0 %collective-permute-start.34 = (bf16[1024,128]{1,0:T(8,128)(2,1)S(1)}, bf16[1024,128]{1,0:T(8,128)(2,1)S(1)}, u32[]{:S(2)}, u32[]{:S(2)}) collective-permute-start(bf16[1024,128]{1,0:T(8,128)(2,1)S(1)} %get-tuple-element.20), channel_id=1, source_target_pairs={{0,3},{1,2},{2,1},{3,0},{4,7},{5,6},{6,5},{7,4},{8,11},{9,10},{10,... | collective-permute-start | bytes 786440 | tf_op jit(solution)/shard_map/ppermute | solution.py:23
  340.8 25.8 %collective-permute-start.42 = (bf16[1024,128]{1,0:T(8,128)(2,1)S(1)}, bf16[1024,128]{1,0:T(8,128)(2,1)S(1)}, u32[]{:S(2)}, u32[]{:S(2)}) collective-permute-start(bf16[1024,128]{1,0:T(8,128)(2,1)S(1)} %get-tuple-element.16), channel_id=1, source_target_pairs={{0,1},{1,0},{2,3},{3,2},{4,5},{5,4},{6,7},{7,6},{8,9},{9,8},{10,11... | collective-permute-start | bytes 786440 | tf_op jit(solution)/shard_map/ppermute | solution.py:23
  342.4 24.6 %collective-permute-start.43 = (bf16[1024,128]{1,0:T(8,128)(2,1)S(1)}, bf16[1024,128]{1,0:T(8,128)(2,1)S(1)}, u32[]{:S(2)}, u32[]{:S(2)}) collective-permute-start(bf16[1024,128]{1,0:T(8,128)(2,1)S(1)} %get-tuple-element.18), channel_id=1, source_target_pairs={{0,2},{1,3},{2,0},{3,1},{4,6},{5,7},{6,4},{7,5},{8,10},{9,11},{10,... | collective-permute-start | bytes 786440 | tf_op jit(solution)/shard_map/ppermute | solution.py:23
  359.0 11.1 %collective-permute-start.44 = (bf16[1024,128]{1,0:T(8,128)(2,1)S(1)}, bf16[1024,128]{1,0:T(8,128)(2,1)S(1)}, u32[]{:S(2)}, u32[]{:S(2)}) collective-permute-start(bf16[1024,128]{1,0:T(8,128)(2,1)S(1)} %get-tuple-element.17), channel_id=1, source_target_pairs={{0,3},{1,2},{2,1},{3,0},{4,7},{5,6},{6,5},{7,4},{8,11},{9,10},{10,... | collective-permute-start | bytes 786440 | tf_op jit(solution)/shard_map/ppermute | solution.py:23
  361.2 17.0 %collective-permute-start.22 = (bf16[1024,128]{1,0:T(8,128)(2,1)}, bf16[1024,128]{1,0:T(8,128)(2,1)S(1)}, u32[]{:S(2)}, u32[]{:S(2)}) collective-permute-start(bf16[1024,128]{1,0:T(8,128)(2,1)} %get-tuple-element.22), channel_id=1, source_target_pairs={{0,1},{1,0},{2,3},{3,2},{4,5},{5,4},{6,7},{7,6},{8,9},{9,8},{10,11... | collective-permute-start | bytes 786440 | tf_op jit(solution)/shard_map/ppermute | solution.py:23
  361.9 26.9 %collective-permute-start.23 = (bf16[1024,128]{1,0:T(8,128)(2,1)}, bf16[1024,128]{1,0:T(8,128)(2,1)}, u32[]{:S(2)}, u32[]{:S(2)}) collective-permute-start(bf16[1024,128]{1,0:T(8,128)(2,1)} %get-tuple-element.24), channel_id=1, source_target_pairs={{0,2},{1,3},{2,0},{3,1},{4,6},{5,7},{6,4},{7,5},{8,10},{9,11},{10,... | collective-permute-start | bytes 786440 | tf_op jit(solution)/shard_map/ppermute | solution.py:23
  366.7 22.2 %collective-permute-start.24 = (bf16[1024,128]{1,0:T(8,128)(2,1)S(1)}, bf16[1024,128]{1,0:T(8,128)(2,1)S(1)}, u32[]{:S(2)}, u32[]{:S(2)}) collective-permute-start(bf16[1024,128]{1,0:T(8,128)(2,1)S(1)} %get-tuple-element.23), channel_id=1, source_target_pairs={{0,3},{1,2},{2,1},{3,0},{4,7},{5,6},{6,5},{7,4},{8,11},{9,10},{10,... | collective-permute-start | bytes 786440 | tf_op jit(solution)/shard_map/ppermute | solution.py:23
  366.9 32.9 %collective-permute-start.47 = (bf16[256,512]{1,0:T(8,128)(2,1)S(1)}, bf16[256,512]{1,0:T(8,128)(2,1)S(1)}, u32[]{:S(2)}, u32[]{:S(2)}) collective-permute-start(bf16[256,512]{1,0:T(8,128)(2,1)S(1)} %reshape.89), channel_id=1, source_target_pairs={{0,8},{4,12},{8,0},{12,4},{16,24},{20,28},{24,16},{28,20},{1,9},{5... | collective-permute-start | bytes 786440 | tf_op jit(solution)/shard_map/ppermute | solution.py:18
  370.1 32.6 %collective-permute-start.50 = (bf16[256,512]{1,0:T(8,128)(2,1)S(1)}, bf16[256,512]{1,0:T(8,128)(2,1)S(1)}, u32[]{:S(2)}, u32[]{:S(2)}) collective-permute-start(bf16[256,512]{1,0:T(8,128)(2,1)S(1)} %reshape.89), channel_id=1, source_target_pairs={{0,16},{4,20},{8,24},{12,28},{16,0},{20,4},{24,8},{28,12},{1,17},{... | collective-permute-start | bytes 786440 | tf_op jit(solution)/shard_map/ppermute | solution.py:18
  390.2 28.8 %collective-permute-start.46 = (bf16[256,512]{1,0:T(8,128)(2,1)S(1)}, bf16[256,512]{1,0:T(8,128)(2,1)S(1)}, u32[]{:S(2)}, u32[]{:S(2)}) collective-permute-start(bf16[256,512]{1,0:T(8,128)(2,1)S(1)} %reshape.88), channel_id=1, source_target_pairs={{0,8},{4,12},{8,0},{12,4},{16,24},{20,28},{24,16},{28,20},{1,9},{5... | collective-permute-start | bytes 786440 | tf_op jit(solution)/shard_map/ppermute | solution.py:18
  391.3 9.5 %collective-permute-start.48 = (bf16[256,512]{1,0:T(8,128)(2,1)S(1)}, bf16[256,512]{1,0:T(8,128)(2,1)S(1)}, u32[]{:S(2)}, u32[]{:S(2)}) collective-permute-start(bf16[256,512]{1,0:T(8,128)(2,1)S(1)} %reshape.90), channel_id=1, source_target_pairs={{0,8},{4,12},{8,0},{12,4},{16,24},{20,28},{24,16},{28,20},{1,9},{5... | collective-permute-start | bytes 786440 | tf_op jit(solution)/shard_map/ppermute | solution.py:18
  396.9 15.6 %collective-permute-start.51 = (bf16[256,512]{1,0:T(8,128)(2,1)S(1)}, bf16[256,512]{1,0:T(8,128)(2,1)S(1)}, u32[]{:S(2)}, u32[]{:S(2)}) collective-permute-start(bf16[256,512]{1,0:T(8,128)(2,1)S(1)} %reshape.90), channel_id=1, source_target_pairs={{0,16},{4,20},{8,24},{12,28},{16,0},{20,4},{24,8},{28,12},{1,17},{... | collective-permute-start | bytes 786440 | tf_op jit(solution)/shard_map/ppermute | solution.py:18
  399.9 18.2 %collective-permute-start.49 = (bf16[256,512]{1,0:T(8,128)(2,1)S(1)}, bf16[256,512]{1,0:T(8,128)(2,1)S(1)}, u32[]{:S(2)}, u32[]{:S(2)}) collective-permute-start(bf16[256,512]{1,0:T(8,128)(2,1)S(1)} %reshape.88), channel_id=1, source_target_pairs={{0,16},{4,20},{8,24},{12,28},{16,0},{20,4},{24,8},{28,12},{1,17},{... | collective-permute-start | bytes 786440 | tf_op jit(solution)/shard_map/ppermute | solution.py:18
  400.7 12.0 %collective-permute-start.54 = (bf16[256,512]{1,0:T(8,128)(2,1)S(1)}, bf16[256,512]{1,0:T(8,128)(2,1)S(1)}, u32[]{:S(2)}, u32[]{:S(2)}) collective-permute-start(bf16[256,512]{1,0:T(8,128)(2,1)S(1)} %reshape.90), channel_id=1, source_target_pairs={{0,24},{4,28},{8,16},{12,20},{16,8},{20,12},{24,0},{28,4},{1,25},{... | collective-permute-start | bytes 786440 | tf_op jit(solution)/shard_map/ppermute | solution.py:18
  402.7 20.5 %collective-permute-start.53 = (bf16[256,512]{1,0:T(8,128)(2,1)S(1)}, bf16[256,512]{1,0:T(8,128)(2,1)S(1)}, u32[]{:S(2)}, u32[]{:S(2)}) collective-permute-start(bf16[256,512]{1,0:T(8,128)(2,1)S(1)} %collective-permute-done.47), channel_id=1, source_target_pairs={{0,16},{4,20},{8,24},{12,28},{16,0},{20,4},{24,8},{28,12},{1,17},{... | collective-permute-start | bytes 786440 | tf_op jit(solution)/shard_map/ppermute | solution.py:18
  (33 other events, 564.8 us)

commit v2 on v1

v2 whole, which is shorter than its diff:
```python
import functools
import math

import jax
import jax.numpy as jnp
from jax import lax
from jax.experimental import pallas as pl
from jax.experimental.pallas import tpu as pltpu
from jax.sharding import PartitionSpec as P


BOND_WIDTH = 3072
SECTOR_TILES = 4
GROUP = 8
CUTS = (0, 2, 4, 5, 6)
CHUNKS = len(CUTS) - 1


def hop(value, mask):
    devices = lax.axis_size("lb")
    return lax.ppermute(value, "lb", [(i, i ^ mask) for i in range(devices)])


def rb_hop(value, mask):
    devices = lax.axis_size("rb")
    return lax.ppermute(value, "rb", [(i, i ^ mask) for i in range(devices)])


def spread(piece, bits):
    held = {0: piece}
    for bit in bits:
        for q in list(held):
            held[q | bit] = hop(held[q], 2 * bit)
    return held


def combine_operators(operator_left, operator_right):
    channels = operator_left.shape[0]
    joined = jnp.einsum(
        "aups,uvqt->avpqst", operator_left, operator_right, precision=lax.Precision.HIGHEST
    )
    return joined.reshape(channels, channels, 4, 4)


def left_kernel(states, channels, group_rows, left_ref, mix_ref, *refs):
    waves, out_ref, parts = refs[:states], refs[states], refs[states + 1]
    for x in range(states):
        parts[x] = jnp.dot(
            left_ref[...], waves[x][...], preferred_element_type=jnp.float32
        ).astype(parts.dtype)
    rows = GROUP * channels
    for pair in range(group_rows // (2 * GROUP)):
        values = []
        for g in (2 * pair, 2 * pair + 1):
            stacked = jnp.concatenate(
                [parts[x, g * rows : (g + 1) * rows, :] for x in range(states)], axis=0
            )
            values.append(jnp.dot(mix_ref[...], stacked, preferred_element_type=jnp.float32))
        here = slice(2 * pair * GROUP, 2 * (pair + 1) * GROUP)
        for v in range(channels):
            for y in range(states):
                at = (v * states + y) * GROUP
                both = jnp.concatenate([value[at : at + GROUP] for value in values], axis=0)
                out_ref[v, y, here, :] = both.astype(out_ref.dtype)


def left_mix(left, mix, state, channels, states, group_rows):
    rows, depth = left.shape
    row_count = rows // channels
    local_right = state.shape[1] // states
    width = 256 if local_right % 256 == 0 else 128
    across = local_right // width
    wave_specs = [
        pl.BlockSpec((depth, width), lambda r, i, x=x: (0, x * across + r)) for x in range(states)
    ]
    return pl.pallas_call(
        functools.partial(left_kernel, states, channels, group_rows),
        out_shape=jax.ShapeDtypeStruct((channels, states, row_count, local_right), jnp.bfloat16),
        grid=(across, row_count // group_rows),
        in_specs=[
            pl.BlockSpec((group_rows * channels, depth), lambda r, i: (i, 0)),
            pl.BlockSpec(mix.shape, lambda r, i: (0, 0)),
            *wave_specs,
        ],
        out_specs=pl.BlockSpec((channels, states, group_rows, width), lambda r, i: (0, 0, i, r)),
        scratch_shapes=[pltpu.VMEM((states, group_rows * channels, width), jnp.bfloat16)],
        compiler_params=pltpu.CompilerParams(vmem_limit_bytes=60 << 20),
        cost_estimate=pl.CostEstimate(
            flops=2 * rows * depth * state.shape[1],
            bytes_accessed=2 * (depth * state.shape[1] + across * rows * depth),
            transcendentals=0,
        ),
        name="left_mix",
    )(left, mix, *([state] * states)).reshape(channels, states * row_count, local_right)


def right_kernel(chips, steps, per, own_ref, sib_ref, *refs):
    first, second = refs[:chips], refs[chips : 2 * chips]
    out_ref, rhs, total = refs[2 * chips :]
    step = pl.program_id(0)
    width = first[0].shape[0]
    rows = own_ref.shape[1]

    def load(pieces):
        for q in range(chips):
            rhs[q * width : (q + 1) * width, :] = pieces[q][...]

    pl.when(step < steps // 2)(lambda: load(first))
    pl.when(step >= steps // 2)(lambda: load(second))
    for e, ref in enumerate((own_ref, sib_ref)):
        here = slice(e * rows, (e + 1) * rows)
        left = jnp.concatenate([ref[v] for v in range(per)], axis=1)
        value = lax.dot_general(
            rhs[...], left, (((1,), (1,)), ((), ())), preferred_element_type=jnp.float32
        )

        @pl.when(step == 0)
        def _():
            total[:, here] = value

        @pl.when(jnp.logical_and(step > 0, step < steps - 1))
        def _():
            total[:, here] += value

        @pl.when(step == steps - 1)
        def _():
            final = (total[:, here] + value).astype(out_ref.dtype)
            for q in range(chips):
                out_ref[q, :, here] = final[q * width : (q + 1) * width]


def right_product(own, sib, first, second):
    chips = len(first)
    channels, rows, depth = own.shape
    width = first[0].shape[0]
    per = 2 if channels % 4 == 0 else 1
    steps = channels // per
    half = steps // 2
    lhs_spec = pl.BlockSpec((per, rows, depth), lambda k: (k, 0, 0))
    first_spec = pl.BlockSpec((width, per * depth), lambda k: (0, jnp.minimum(k, half - 1)))
    second_spec = pl.BlockSpec((width, per * depth), lambda k: (0, jnp.maximum(k - half, 0)))
    shape = (chips, width, 2 * rows)
    return pl.pallas_call(
        functools.partial(right_kernel, chips, steps, per),
        out_shape=jax.ShapeDtypeStruct(shape, jnp.bfloat16),
        grid=(steps,),
        in_specs=[lhs_spec] * 2 + [first_spec] * chips + [second_spec] * chips,
        out_specs=pl.BlockSpec(shape, lambda k: (0, 0, 0)),
        scratch_shapes=[
            pltpu.VMEM((chips * width, per * depth), jnp.bfloat16),
            pltpu.VMEM((chips * width, 2 * rows), jnp.float32),
        ],
        compiler_params=pltpu.CompilerParams(vmem_limit_bytes=60 << 20),
        cost_estimate=pl.CostEstimate(
            flops=4 * rows * depth * channels * chips * width,
            bytes_accessed=2 * depth * channels * (2 * rows + chips * width),
            transcendentals=0,
        ),
        name="right_product",
    )(own, sib, *first, *second)


def gram_kernel(chips, states, rows, start, *refs):
    tiles, out_ref = refs[:chips], refs[-1]

    def stacked(ref):
        parts = []
        for y in range(states):
            both = [ref[:, (e * states + y) * rows : (e * states + y + 1) * rows] for e in range(2)]
            parts.append(jnp.concatenate(both, axis=1))
        return jnp.concatenate(parts, axis=0)

    own = stacked(tiles[0])
    for q in range(chips):
        other = own if q == 0 else stacked(tiles[q])
        value = lax.dot_general(
            own, other, (((0,), (0,)), ((), ())), preferred_element_type=jnp.float32
        )
        out_ref[q] = value if start else refs[chips][q] + value


def add_gram(gram, tiles, states, rows):
    chips = len(tiles)
    shape = (chips, 2 * rows, 2 * rows)
    before = [] if gram is None else [gram]
    whole = pl.BlockSpec(memory_space=pltpu.VMEM)
    return pl.pallas_call(
        functools.partial(gram_kernel, chips, states, rows, gram is None),
        out_shape=jax.ShapeDtypeStruct(shape, jnp.float32),
        in_specs=[whole] * (chips + len(before)),
        out_specs=whole,
        compiler_params=pltpu.CompilerParams(vmem_limit_bytes=32 << 20),
        cost_estimate=pl.CostEstimate(
            flops=2 * chips * (2 * rows) ** 2 * states * tiles[0].shape[0],
            bytes_accessed=8 * chips * (2 * rows) ** 2,
            transcendentals=0,
        ),
        name="add_gram",
    )(*tiles, *before)


def exchange(parts, own_slot):
    z = lax.axis_index("rb")

    def slot(target):
        return lax.dynamic_index_in_dim(parts, target ^ own_slot, 0, keepdims=False)

    total = slot(z).astype(jnp.float32)
    for mask in range(1, lax.axis_size("rb")):
        total = total + rb_hop(slot(z ^ mask), mask).astype(jnp.float32)
    return total


def fetch(value, q):
    tiles = lax.axis_size("lb")
    near = [i for i in range(tiles) if 2 * abs(i // 2 - (i // 2 ^ q)) - 1 < SECTOR_TILES]
    return lax.ppermute(value, "lb", [(i ^ (2 * q), i) for i in near])


def shards(
    wavefunction, left_environment, operator_left, operator_right, right_environment, row_sector
):
    channels, row_count, full_bond = left_environment.shape
    piece_rows, states, local_right = wavefunction.shape
    tile_width = right_environment.shape[2]
    tiles = lax.axis_size("lb")
    chips = tiles // 2
    me = lax.axis_index("lb")
    z = lax.axis_index("rb")
    chip, core = me // 2, me % 2
    first_core = core == 0
    bits = [1 << i for i in range(chips.bit_length() - 1)]
    orders = (bits[::-1], bits)

    flat = wavefunction.reshape(piece_rows, states * local_right)
    half_rows = piece_rows // 2
    state = jnp.zeros((full_bond, states * local_right), wavefunction.dtype)
    for half in range(2):
        held = spread(flat[half * half_rows : (half + 1) * half_rows], orders[half])
        for q, piece in held.items():
            for e in range(2):
                value = piece if e == 0 else hop(piece, 1)
                start = (me ^ (2 * q + e)) * piece_rows + half * half_rows
                state = lax.dynamic_update_slice(state, value, (start, jnp.int32(0)))

    combined = combine_operators(operator_left, operator_right)
    mix = combined.transpose(1, 2, 3, 0)[:, :, None, :, None, :]
    mix = mix * jnp.eye(GROUP, dtype=jnp.float32)[None, None, :, None, :, None]
    mix = mix.reshape(channels * GROUP * states, states * GROUP * channels).astype(jnp.bfloat16)
    left = left_environment.transpose(1, 0, 2).reshape(row_count * channels, full_bond)
    mixed = left_mix(left, mix, state, channels, states, row_count // 2)
    mixed_sibling = hop(mixed, 1)

    half = channels // 2
    flipped = right_environment.transpose(2, 0, 1).reshape(tile_width, channels * local_right)
    mine, theirs = [], []
    gram = None
    for j in range(CHUNKS):
        here = slice(CUTS[j] * tile_width // CUTS[-1], CUTS[j + 1] * tile_width // CUTS[-1])
        pieces = []
        for h in range(2):
            part = flipped[here, h * half * local_right : (h + 1) * half * local_right]
            held = spread(part, orders[h])
            pieces.append([held[q] for q in range(chips)])
        parts = right_product(mixed, mixed_sibling, *pieces)
        applied = exchange(parts, chip).astype(jnp.bfloat16)
        own_rows = row_count * states
        mine.append(applied[:, :own_rows])
        theirs.append(hop(applied[:, own_rows:], 1))
        if j < CHUNKS // 2:
            held = spread(applied, orders[j % 2])
        else:
            held = {q: fetch(applied, q) if q else applied for q in range(chips)}
        gram = add_gram(gram, [held[q] for q in range(chips)], states, row_count)

    def ordered(value, other):
        return (jnp.where(first_core, value, other), jnp.where(first_core, other, value))

    gram = jnp.concatenate(ordered(gram[:, :, :row_count], gram[:, :, row_count:]), axis=2)
    gram = gram.astype(jnp.bfloat16)
    rb_size = lax.axis_size("rb")
    block = 0.0
    for e in range(2):
        for mask in range(rb_size):
            part = lax.dynamic_index_in_dim(gram, (z ^ mask) ^ chip, 0, keepdims=False)
            part = part[e * row_count : (e + 1) * row_count]
            if e or mask:
                pairs = [
                    (b * rb_size + i, (b ^ e) * rb_size + (i ^ mask))
                    for b in range(tiles)
                    for i in range(rb_size)
                ]
                part = lax.ppermute(part, ("lb", "rb"), pairs)
            block = block + part.astype(jnp.float32)
    columns = [ordered(a, b) for a, b in zip(mine, theirs)]
    applied = jnp.concatenate([c[0] for c in columns] + [c[1] for c in columns], axis=0)
    applied = applied.reshape(2 * tile_width, states, row_count).transpose(2, 1, 0)
    own_label = lax.dynamic_index_in_dim(row_sector, me, keepdims=False)
    labels = lax.dynamic_slice_in_dim(row_sector, 2 * z, 2)
    keep = jnp.repeat(labels == own_label, row_count)[None, :]
    density = jnp.where(keep, block, jnp.float32(0.0)) * (1.0 / math.sqrt(4.0 * BOND_WIDTH))
    return (applied, density)


def solution(mesh):
    placed = (P("lb", None, "rb"), P(None, "lb", None), P(), P(), P(None, "rb", "lb"), P())
    return jax.shard_map(
        shards,
        mesh=mesh,
        in_specs=placed,
        out_specs=(P("lb", None, "rb"), P("lb", "rb")),
        check_vma=False,
    )
```

time: 445 us -> 444 us (level)
  matrix products: 35.7 us -> 0.41 us
  Pallas kernels: 41.8 us -> 75.3 us
  local copies, waits for them, and re-layouts: 82.4 us -> 68.4 us
  waiting for transfers between devices: 210 us -> 217 us
  starting transfers between devices: 65.1 us -> 70.3 us
    dot_general x16 -> x0, matrix products: 35.3 us -> none  [the longest x2 28.9 us: shards(): jnp.dot(rows.reshape(channels * block_rows, full_bond), state, preferred_...]
    pallas_call x3 -> x9, Pallas kernels: 41.8 us -> 75.3 us  [the longest x4 45.5 us: right_product(): pl.pallas_call(functools.partial(right_kernel, chips, steps, per), out_sh...]
    reshape x8 -> x2, local copies, waits for them, and re-layouts: 34.6 us -> 1.52 us  [shards(): applied.reshape(2 * tile_width, states, row_count).transpose(2, 1, 0)]
    ppermute x9 -> x12, waiting for transfers between devices: 13.3 us -> 41.4 us  [rb_hop(): return lax.ppermute(value, 'rb', [(i, i ^ mask) for i in range(devices)])]
    ppermute x46 -> x49, waiting for transfers between devices: 193 us -> 172 us  [hop(): return lax.ppermute(value, 'lb', [(i, i ^ mask) for i in range(devices)])]
    dynamic_update_slice x16, local copies, waits for them, and re-layouts: 12.3 us -> 26.8 us  [shards(): state = lax.dynamic_update_slice(state, value, (start, jnp.int32(0)))]
    transpose x0 -> x3, local copies, waits for them, and re-layouts: none -> 9.05 us  [the longest x1 8.86 us: shards(): left_environment.transpose(1, 0, 2).reshape(row_count * channels, full_bond)]
    unnamed x43 -> x42, local copies, waits for them, and re-layouts: 15.8 us -> 7.54 us
  transfers between devices with their start and end apart: 62 -> 74, of which waited for: 28 -> 26; matrix products, arithmetic and copies ran while one was open for 16% -> 16% of each run, Pallas kernels for 9% -> 11%
where the time goes in v2:
time: 444 us; the launch traced here: 438 us
  waiting for transfers between devices  217 us (49%)
  Pallas kernels  75.3 us (17%)
  starting transfers between devices  70.3 us (16%)
  local copies, waits for them, and re-layouts  68.4 us (15%)
  other arithmetic  5.67 us (1%)
    ppermute x49, waiting for transfers between devices, hop(): return lax.ppermute(value, 'lb', [(i, i ^ mask) for i in range(devices)])  172 us
    pallas_call x4, Pallas kernels, right_product(): pl.pallas_call(functools.partial(right_kernel, chips, steps, per), out_sh...  45.5 us
    ppermute x12, waiting for transfers between devices, rb_hop(): return lax.ppermute(value, 'rb', [(i, i ^ mask) for i in range(devices)])  41.4 us
    ppermute x49, starting transfers between devices, hop(): return lax.ppermute(value, 'lb', [(i, i ^ mask) for i in range(devices)])  36.1 us
    pallas_call x1, Pallas kernels, left_mix(): pl.pallas_call(functools.partial(left_kernel, states, channels, group_row...  28.2 us
    dynamic_update_slice x16, local copies, waits for them, and re-layouts, shards(): state = lax.dynamic_update_slice(state, value, (start, jnp.int32(0)))  26.8 us
    ppermute x12, starting transfers between devices, rb_hop(): return lax.ppermute(value, 'rb', [(i, i ^ mask) for i in range(devices)])  17.7 us
    ppermute x7, starting transfers between devices, shards(): part = lax.ppermute(part, ('lb', 'rb'), pairs)  9.81 us
  transfers between devices with their start and end apart: 74, of which 26 were waited for; matrix products, arithmetic and copies ran while one was open for 16% of the time, Pallas kernels for 11%

profile of v2, /device:TPU:0, one launch (start us, length us, event | category | flops | bytes accessed | tf_op | source)
XLA Modules:
  0.0 438.5 jit_solution(15893595108573360174)
XLA Ops:
  0.7 2.4 fusion.29
  4.3 3.0 collective-permute-start.1
  10.2 23.4 %collective-permute-done.1 = bf16[192,3072]{1,0:T(8,128)(2,1)} collective-permute-done((bf16[192,3072]{1,0:T(8,128)(2,1)}, bf16[192,3072]{1,0:T(8,128)(2,1)}, u32[]{:S(2)}, u32[]{:S(2)}) %collective-permute-start.1) | collective-permute-done | bytes 1179680 | tf_op jit(solution)/shard_map/ppermute | solution.py:21
  36.0 8.9 %copy.42 = bf16[128,8,3072]{2,1,0:T(8,128)(2,1)} copy(bf16[128,8,3072]{2,0,1:T(8,128)(2,1)} %bitcast.89) | data formatting | bytes 12582912 | tf_op jit(solution)/shard_map/transpose | solution.py:250
  44.8 3.5 convert_element_type.114.mix_ref
  48.3 6.7 %broadcast_in_dim.22 = bf16[3072,3072]{1,0:T(8,128)(2,1)} broadcast(bf16[]{:T(256)} %constant.111.clone.1), dimensions={} | broadcast | bytes 18874370 | tf_op jit(solution)/shard_map/broadcast_in_dim | solution.py:237
  55.0 2.4 constant_dynamic-update-slice_fusion.15
  58.9 2.9 collective-permute-done.8
  61.8 2.4 constant_dynamic-update-slice_fusion.14
  64.2 2.4 constant_dynamic-update-slice_fusion.13
  66.5 20.1 %collective-permute-done.5 = bf16[192,3072]{1,0:T(8,128)(2,1)} collective-permute-done((bf16[192,3072]{1,0:T(8,128)(2,1)}, bf16[192,3072]{1,0:T(8,128)(2,1)}, u32[]{:S(2)}, u32[]{:S(2)}) %collective-permute-start.5) | collective-permute-done | bytes 1179680 | tf_op jit(solution)/shard_map/ppermute | solution.py:21
  86.6 2.4 constant_dynamic-update-slice_fusion.12
  89.0 2.4 constant_dynamic-update-slice_fusion.11
  92.0 18.7 %collective-permute-done.12 = bf16[192,3072]{1,0:T(8,128)(2,1)S(1)} collective-permute-done((bf16[192,3072]{1,0:T(8,128)(2,1)}, bf16[192,3072]{1,0:T(8,128)(2,1)S(1)}, u32[]{:S(2)}, u32[]{:S(2)}) %collective-permute-start.12) | collective-permute-done | bytes 1179680 | tf_op jit(solution)/shard_map/ppermute | solution.py:21
  111.9 2.4 constant_dynamic-update-slice_fusion.9
  117.6 2.4 constant_dynamic-update-slice_fusion.5
  125.7 28.2 %left_mix.1 = bf16[8,4,128,768]{3,2,1,0:T(8,128)(2,1)} custom-call(bf16[1024,3072]{1,0:T(8,128)(2,1)} %bitcast.86, bf16[256,256]{1,0:T(8,128)(2,1)} %convert_element_type.114.mix_ref, bf16[3072,3072]{1,0:T(8,128)(2,1)} %constant_dynamic-update-slice_fusion.refs_0_.refs_1_.refs_2_.refs_3_, ...), custom_call_target="tpu_custom_call" | custom-call | flops 19327352832 | bytes 37748736 | tf_op jit(solution)/shard_map/left_mix/pallas_call | solution.py:76
  154.3 2.7 fusion.27
  164.5 5.8 %collective-permute-done.36.refs_2_ = bf16[64,3072]{1,0:T(8,128)(2,1)S(1)} collective-permute-done((bf16[64,3072]{1,0:T(8,128)(2,1)}, bf16[64,3072]{1,0:T(8,128)(2,1)S(1)}, u32[]{:S(2)}, u32[]{:S(2)}) %collective-permute-start.36) | collective-permute-done | bytes 393248 | tf_op jit(solution)/shard_map/ppermute | solution.py:21
  174.1 2.1 fusion.28
  177.7 3.8 collective-permute-done.35.refs_1_
  182.2 5.0 %collective-permute-done.46.refs_2_ = bf16[64,3072]{1,0:T(8,128)(2,1)} collective-permute-done((bf16[64,3072]{1,0:T(8,128)(2,1)S(1)}, bf16[64,3072]{1,0:T(8,128)(2,1)}, u32[]{:S(2)}, u32[]{:S(2)}) %collective-permute-start.46) | collective-permute-done | bytes 393248 | tf_op jit(solution)/shard_map/ppermute | solution.py:21
  187.6 2.3 collective-permute-done.48.refs_5_
  190.3 23.5 %collective-permute-done.45.refs_1_ = bf16[64,3072]{1,0:T(8,128)(2,1)S(1)} collective-permute-done((bf16[64,3072]{1,0:T(8,128)(2,1)S(1)}, bf16[64,3072]{1,0:T(8,128)(2,1)S(1)}, u32[]{:S(2)}, u32[]{:S(2)}) %collective-permute-start.45) | collective-permute-done | bytes 393248 | tf_op jit(solution)/shard_map/ppermute | solution.py:21
  219.9 14.6 %collective-permute-done.15.refs_1_ = bf16[128,3072]{1,0:T(8,128)(2,1)} collective-permute-done((bf16[128,3072]{1,0:T(8,128)(2,1)}, bf16[128,3072]{1,0:T(8,128)(2,1)}, u32[]{:S(2)}, u32[]{:S(2)}) %collective-permute-start.15) | collective-permute-done | bytes 786464 | tf_op jit(solution)/shard_map/ppermute | solution.py:21
  237.0 14.4 %collective-permute-done.17.refs_3_ = bf16[128,3072]{1,0:T(8,128)(2,1)} collective-permute-done((bf16[128,3072]{1,0:T(8,128)(2,1)}, bf16[128,3072]{1,0:T(8,128)(2,1)}, u32[]{:S(2)}, u32[]{:S(2)}) %collective-permute-start.17) | collective-permute-done | bytes 786464 | tf_op jit(solution)/shard_map/ppermute | solution.py:21
  253.9 13.5 %right_product.4 = bf16[4,128,1024]{2,1,0:T(8,128)(2,1)} custom-call(bf16[8,512,768]{2,1,0:T(8,128)(2,1)} %bitcast.82, bf16[8,512,768]{2,1,0:T(8,128)(2,1)} %collective-permute-done.14.sib_ref, bf16[128,3072]{1,0:T(8,128)(2,1)} %copy.27.refs_0_, bf16[128,3072]{1,0:T(8,128)(2,1)} %collective-permute-done.15.refs_1_, ...), custom_call_target="tpu_custom_call" | custom-call | flops 6442450944 | bytes 18874368 | tf_op jit(solution)/shard_map/right_product/pallas_call | solution.py:143
  270.6 6.1 %collective-permute-done.37.refs_3_ = bf16[64,3072]{1,0:T(8,128)(2,1)} collective-permute-done((bf16[64,3072]{1,0:T(8,128)(2,1)}, bf16[64,3072]{1,0:T(8,128)(2,1)}, u32[]{:S(2)}, u32[]{:S(2)}) %collective-permute-start.37) | collective-permute-done | bytes 393248 | tf_op jit(solution)/shard_map/ppermute | solution.py:21
  278.5 6.5 %collective-permute-done.47.refs_3_ = bf16[64,3072]{1,0:T(8,128)(2,1)S(1)} collective-permute-done((bf16[64,3072]{1,0:T(8,128)(2,1)}, bf16[64,3072]{1,0:T(8,128)(2,1)S(1)}, u32[]{:S(2)}, u32[]{:S(2)}) %collective-permute-start.47) | collective-permute-done | bytes 393248 | tf_op jit(solution)/shard_map/ppermute | solution.py:21
  285.5 9.3 %right_product.6 = bf16[4,64,1024]{2,1,0:T(8,128)(2,1)} custom-call(bf16[8,512,768]{2,1,0:T(8,128)(2,1)} %bitcast.83, bf16[8,512,768]{2,1,0:T(8,128)(2,1)} %collective-permute-done.14.sib_ref, bf16[64,3072]{1,0:T(8,128)(2,1)} %copy.31.refs_0_, bf16[64,3072]{1,0:T(8,128)(2,1)} %collective-permute-done.35.refs_1_, bf16[64,3072]{1,0:T(8,128)(2,1)} %copy-done.7, ...), custom_call_target="tpu_custom_call" | custom-call | flops 3221225472 | bytes 15728640 | tf_op jit(solution)/shard_map/right_product/pallas_call | solution.py:143
  296.7 5.4 %collective-permute-done.50.refs_7_ = bf16[64,3072]{1,0:T(8,128)(2,1)S(1)} collective-permute-done((bf16[64,3072]{1,0:T(8,128)(2,1)}, bf16[64,3072]{1,0:T(8,128)(2,1)S(1)}, u32[]{:S(2)}, u32[]{:S(2)}) %collective-permute-start.50) | collective-permute-done | bytes 393248 | tf_op jit(solution)/shard_map/ppermute | solution.py:21
  303.7 9.4 %right_product.7 = bf16[4,64,1024]{2,1,0:T(8,128)(2,1)} custom-call(bf16[8,512,768]{2,1,0:T(8,128)(2,1)} %bitcast.84, bf16[8,512,768]{2,1,0:T(8,128)(2,1)} %collective-permute-done.14.sib_ref, bf16[64,3072]{1,0:T(8,128)(2,1)} %copy-done.2, bf16[64,3072]{1,0:T(8,128)(2,1)} %copy-done.9, bf16[64,3072]{1,0:T(8,128)(2,1)} %collective-permute-done.46.refs_2_, ...), custom_call_target="tpu_custom_call" | custom-call | flops 3221225472 | bytes 15728640 | tf_op jit(solution)/shard_map/right_product/pallas_call | solution.py:143
  315.5 2.6 collective-permute-start.42
  318.1 2.2 collective-permute-start.43
  320.3 13.3 %right_product.5 = bf16[4,128,1024]{2,1,0:T(8,128)(2,1)} custom-call(bf16[8,512,768]{2,1,0:T(8,128)(2,1)} %bitcast.85, bf16[8,512,768]{2,1,0:T(8,128)(2,1)} %collective-permute-done.14.sib_ref, bf16[128,3072]{1,0:T(8,128)(2,1)} %copy-done.5, bf16[128,3072]{1,0:T(8,128)(2,1)} %collective-permute-done.25.refs_1_, ...), custom_call_target="tpu_custom_call" | custom-call | flops 6442450944 | bytes 18874368 | tf_op jit(solution)/shard_map/right_product/pallas_call | solution.py:143
  334.8 2.2 collective-permute-start.22
  337.0 2.2 collective-permute-start.23
  341.9 26.3 %collective-permute-done.52 = bf16[64,1024]{1,0:T(8,128)(2,1)S(1)} collective-permute-done((bf16[64,1024]{1,0:T(8,128)(2,1)S(1)}, bf16[64,1024]{1,0:T(8,128)(2,1)S(1)}, u32[]{:S(2)}, u32[]{:S(2)}) %collective-permute-start.52) | collective-permute-done | bytes 131104 | tf_op jit(solution)/shard_map/ppermute | solution.py:26
  368.2 2.1 collective-permute-start.32
  370.3 2.4 collective-permute-start.33
  374.4 3.4 collective-permute-done.31
  377.8 11.7 %collective-permute-done.32 = bf16[128,1024]{1,0:T(8,128)(2,1)S(1)} collective-permute-done((bf16[128,1024]{1,0:T(8,128)(2,1)S(1)}, bf16[128,1024]{1,0:T(8,128)(2,1)S(1)}, u32[]{:S(2)}, u32[]{:S(2)}) %collective-permute-start.32) | collective-permute-done | bytes 262176 | tf_op jit(solution)/shard_map/ppermute | solution.py:26
  396.7 10.9 %collective-permute-done.61.refs_1_ = bf16[128,1024]{1,0:T(8,128)(2,1)S(1)} collective-permute-done((bf16[128,1024]{1,0:T(8,128)(2,1)S(1)}, bf16[128,1024]{1,0:T(8,128)(2,1)S(1)}, u32[]{:S(2)}, u32[]{:S(2)}) %collective-permute-start.61) | collective-permute-done | bytes 262176 | tf_op jit(solution)/shard_map/ppermute | solution.py:21
  410.5 4.2 collective-permute-start.55
  414.7 5.1 %collective-permute-done.63.refs_3_ = bf16[128,1024]{1,0:T(8,128)(2,1)S(1)} collective-permute-done((bf16[128,1024]{1,0:T(8,128)(2,1)S(1)}, bf16[128,1024]{1,0:T(8,128)(2,1)S(1)}, u32[]{:S(2)}, u32[]{:S(2)}) %collective-permute-start.63) | collective-permute-done | bytes 262176 | tf_op jit(solution)/shard_map/ppermute | solution.py:21
  424.0 3.0 collective-permute-start.67
  427.3 2.3 collective-permute-start.69
  435.4 2.3 collective-permute-done.73
  (210 shorter events, 82.2 us)
Async XLA Ops:
  4.3 29.3 %collective-permute-start.1 = (bf16[192,3072]{1,0:T(8,128)(2,1)}, bf16[192,3072]{1,0:T(8,128)(2,1)}, u32[]{:S(2)}, u32[]{:S(2)}) collective-permute-start(bf16[192,3072]{1,0:T(8,128)(2,1)} %bitcast.46), channel_id=1, source_target_pairs={{0,16},{4,20},{8,24},{12,28},{16,0},{20,4},{24,8},{28,12},{1,17},{... | collective-permute-start | bytes 3538952 | tf_op jit(solution)/shard_map/ppermute | solution.py:21
  7.3 50.0 %collective-permute-start = (bf16[192,3072]{1,0:T(8,128)(2,1)}, bf16[192,3072]{1,0:T(8,128)(2,1)}, u32[]{:S(2)}, u32[]{:S(2)}) collective-permute-start(bf16[192,3072]{1,0:T(8,128)(2,1)} %bitcast.46), channel_id=1, source_target_pairs={{0,4},{4,0},{8,12},{12,8},{16,20},{20,16},{24,28},{28,24},{1,5},{5... | collective-permute-start | bytes 3538952 | tf_op jit(solution)/shard_map/ppermute | solution.py:21
  7.3 51.5 %collective-permute-start.3 = (bf16[192,3072]{1,0:T(8,128)(2,1)}, bf16[192,3072]{1,0:T(8,128)(2,1)}, u32[]{:S(2)}, u32[]{:S(2)}) collective-permute-start(bf16[192,3072]{1,0:T(8,128)(2,1)} %bitcast.46), channel_id=1, source_target_pairs={{0,8},{4,12},{8,0},{12,4},{16,24},{20,28},{24,16},{28,20},{1,9},{5... | collective-permute-start | bytes 3538952 | tf_op jit(solution)/shard_map/ppermute | solution.py:21
  9.0 52.8 %collective-permute-start.8 = (bf16[192,3072]{1,0:T(8,128)(2,1)S(1)}, bf16[192,3072]{1,0:T(8,128)(2,1)}, u32[]{:S(2)}, u32[]{:S(2)}) collective-permute-start(bf16[192,3072]{1,0:T(8,128)(2,1)S(1)} %bitcast.90), channel_id=1, source_target_pairs={{0,8},{4,12},{8,0},{12,4},{16,24},{20,28},{24,16},{28,20},{1,9},{5... | collective-permute-start | bytes 3538952 | tf_op jit(solution)/shard_map/ppermute | solution.py:21
  33.6 32.9 %collective-permute-start.2 = (bf16[192,3072]{1,0:T(8,128)(2,1)}, bf16[192,3072]{1,0:T(8,128)(2,1)}, u32[]{:S(2)}, u32[]{:S(2)}) collective-permute-start(bf16[192,3072]{1,0:T(8,128)(2,1)} %collective-permute-done.1), channel_id=1, source_target_pairs={{0,4},{4,0},{8,12},{12,8},{16,20},{20,16},{24,28},{28,24},{1,5},{5... | collective-permute-start | bytes 3538952 | tf_op jit(solution)/shard_map/ppermute | solution.py:21
  33.6 53.0 %collective-permute-start.5 = (bf16[192,3072]{1,0:T(8,128)(2,1)}, bf16[192,3072]{1,0:T(8,128)(2,1)}, u32[]{:S(2)}, u32[]{:S(2)}) collective-permute-start(bf16[192,3072]{1,0:T(8,128)(2,1)} %collective-permute-done.1), channel_id=1, source_target_pairs={{0,8},{4,12},{8,0},{12,4},{16,24},{20,28},{24,16},{28,20},{1,9},{5... | collective-permute-start | bytes 3538952 | tf_op jit(solution)/shard_map/ppermute | solution.py:21
  57.4 34.0 %collective-permute-start.10 = (bf16[192,3072]{1,0:T(8,128)(2,1)S(1)}, bf16[192,3072]{1,0:T(8,128)(2,1)S(1)}, u32[]{:S(2)}, u32[]{:S(2)}) collective-permute-start(bf16[192,3072]{1,0:T(8,128)(2,1)S(1)} %bitcast.91), channel_id=1, source_target_pairs={{0,16},{4,20},{8,24},{12,28},{16,0},{20,4},{24,8},{28,12},{1,17},{... | collective-permute-start | bytes 3538952 | tf_op jit(solution)/shard_map/ppermute | solution.py:21
  58.9 33.0 %collective-permute-start.4 = (bf16[192,3072]{1,0:T(8,128)(2,1)}, bf16[192,3072]{1,0:T(8,128)(2,1)S(1)}, u32[]{:S(2)}, u32[]{:S(2)}) collective-permute-start(bf16[192,3072]{1,0:T(8,128)(2,1)} %collective-permute-done.3), channel_id=1, source_target_pairs={{0,4},{4,0},{8,12},{12,8},{16,20},{20,16},{24,28},{28,24},{1,5},{5... | collective-permute-start | bytes 3538952 | tf_op jit(solution)/shard_map/ppermute | solution.py:21
  61.8 49.0 %collective-permute-start.12 = (bf16[192,3072]{1,0:T(8,128)(2,1)}, bf16[192,3072]{1,0:T(8,128)(2,1)S(1)}, u32[]{:S(2)}, u32[]{:S(2)}) collective-permute-start(bf16[192,3072]{1,0:T(8,128)(2,1)} %collective-permute-done.8), channel_id=1, source_target_pairs={{0,16},{4,20},{8,24},{12,28},{16,0},{20,4},{24,8},{28,12},{1,17},{... | collective-permute-start | bytes 3538952 | tf_op jit(solution)/shard_map/ppermute | solution.py:21
  66.5 49.9 %collective-permute-start.7 = (bf16[192,3072]{1,0:T(8,128)(2,1)S(1)}, bf16[192,3072]{1,0:T(8,128)(2,1)S(1)}, u32[]{:S(2)}, u32[]{:S(2)}) collective-permute-start(bf16[192,3072]{1,0:T(8,128)(2,1)S(1)} %bitcast.92), channel_id=1, source_target_pairs={{0,4},{4,0},{8,12},{12,8},{16,20},{20,16},{24,28},{28,24},{1,5},{5... | collective-permute-start | bytes 3538952 | tf_op jit(solution)/shard_map/ppermute | solution.py:21
  86.6 27.7 %collective-permute-start.6 = (bf16[192,3072]{1,0:T(8,128)(2,1)}, bf16[192,3072]{1,0:T(8,128)(2,1)S(1)}, u32[]{:S(2)}, u32[]{:S(2)}) collective-permute-start(bf16[192,3072]{1,0:T(8,128)(2,1)} %collective-permute-done.5), channel_id=1, source_target_pairs={{0,4},{4,0},{8,12},{12,8},{16,20},{20,16},{24,28},{28,24},{1,5},{5... | collective-permute-start | bytes 3538952 | tf_op jit(solution)/shard_map/ppermute | solution.py:21
  91.3 28.7 %collective-permute-start.9 = (bf16[192,3072]{1,0:T(8,128)(2,1)}, bf16[192,3072]{1,0:T(8,128)(2,1)S(1)}, u32[]{:S(2)}, u32[]{:S(2)}) collective-permute-start(bf16[192,3072]{1,0:T(8,128)(2,1)} %collective-permute-done.8), channel_id=1, source_target_pairs={{0,4},{4,0},{8,12},{12,8},{16,20},{20,16},{24,28},{28,24},{1,5},{5... | collective-permute-start | bytes 3538952 | tf_op jit(solution)/shard_map/ppermute | solution.py:21
  91.9 30.4 %collective-permute-start.11 = (bf16[192,3072]{1,0:T(8,128)(2,1)S(1)}, bf16[192,3072]{1,0:T(8,128)(2,1)S(1)}, u32[]{:S(2)}, u32[]{:S(2)}) collective-permute-start(bf16[192,3072]{1,0:T(8,128)(2,1)S(1)} %collective-permute-done.10), channel_id=1, source_target_pairs={{0,4},{4,0},{8,12},{12,8},{16,20},{20,16},{24,28},{28,24},{1,5},{5... | collective-permute-start | bytes 3538952 | tf_op jit(solution)/shard_map/ppermute | solution.py:21
  153.9 98.3 %collective-permute-start.14 = (bf16[8,512,768]{2,1,0:T(8,128)(2,1)}, bf16[8,512,768]{2,1,0:T(8,128)(2,1)}, u32[]{:S(2)}, u32[]{:S(2)}) collective-permute-start(bf16[8,512,768]{2,1,0:T(8,128)(2,1)} %bitcast.81), channel_id=1, source_target_pairs={{0,4},{4,0},{8,12},{12,8},{16,20},{20,16},{24,28},{28,24},{1,5},{5... | collective-permute-start | bytes 18874376 | tf_op jit(solution)/shard_map/ppermute | solution.py:21
  161.2 20.3 %collective-permute-start.35 = (bf16[64,3072]{1,0:T(8,128)(2,1)}, bf16[64,3072]{1,0:T(8,128)(2,1)}, u32[]{:S(2)}, u32[]{:S(2)}) collective-permute-start(bf16[64,3072]{1,0:T(8,128)(2,1)} %copy.31.refs_0_), channel_id=1, source_target_pairs={{0,8},{4,12},{8,0},{12,4},{16,24},{20,28},{24,16},{28,20},{1,9},{5... | collective-permute-start | bytes 1179656 | tf_op jit(solution)/shard_map/ppermute | solution.py:21
  162.7 19.1 %collective-permute-start.39 = (bf16[64,3072]{1,0:T(8,128)(2,1)}, bf16[64,3072]{1,0:T(8,128)(2,1)}, u32[]{:S(2)}, u32[]{:S(2)}) collective-permute-start(bf16[64,3072]{1,0:T(8,128)(2,1)} %copy.32.refs_4_), channel_id=1, source_target_pairs={{0,16},{4,20},{8,24},{12,28},{16,0},{20,4},{24,8},{28,12},{1,17},{... | collective-permute-start | bytes 1179656 | tf_op jit(solution)/shard_map/ppermute | solution.py:21
  181.4 33.2 %collective-permute-start.16 = (bf16[128,3072]{1,0:T(8,128)(2,1)}, bf16[128,3072]{1,0:T(8,128)(2,1)}, u32[]{:S(2)}, u32[]{:S(2)}) collective-permute-start(bf16[128,3072]{1,0:T(8,128)(2,1)} %copy.27.refs_0_), channel_id=1, source_target_pairs={{0,16},{4,20},{8,24},{12,28},{16,0},{20,4},{24,8},{28,12},{1,17},{... | collective-permute-start | bytes 2359304 | tf_op jit(solution)/shard_map/ppermute | solution.py:21
  181.9 34.5 %collective-permute-start.18 = (bf16[128,3072]{1,0:T(8,128)(2,1)S(1)}, bf16[128,3072]{1,0:T(8,128)(2,1)}, u32[]{:S(2)}, u32[]{:S(2)}) collective-permute-start(bf16[128,3072]{1,0:T(8,128)(2,1)S(1)} %copy.28.refs_4_), channel_id=1, source_target_pairs={{0,8},{4,12},{8,0},{12,4},{16,24},{20,28},{24,16},{28,20},{1,9},{5... | collective-permute-start | bytes 2359304 | tf_op jit(solution)/shard_map/ppermute | solution.py:21
  187.2 26.6 %collective-permute-start.45 = (bf16[64,3072]{1,0:T(8,128)(2,1)S(1)}, bf16[64,3072]{1,0:T(8,128)(2,1)S(1)}, u32[]{:S(2)}, u32[]{:S(2)}) collective-permute-start(bf16[64,3072]{1,0:T(8,128)(2,1)S(1)} %copy.33.refs_0_), channel_id=1, source_target_pairs={{0,8},{4,12},{8,0},{12,4},{16,24},{20,28},{24,16},{28,20},{1,9},{5... | collective-permute-start | bytes 1179656 | tf_op jit(solution)/shard_map/ppermute | solution.py:21
  189.9 24.4 %collective-permute-start.49 = (bf16[64,3072]{1,0:T(8,128)(2,1)}, bf16[64,3072]{1,0:T(8,128)(2,1)S(1)}, u32[]{:S(2)}, u32[]{:S(2)}) collective-permute-start(bf16[64,3072]{1,0:T(8,128)(2,1)} %copy.34.refs_4_), channel_id=1, source_target_pairs={{0,16},{4,20},{8,24},{12,28},{16,0},{20,4},{24,8},{28,12},{1,17},{... | collective-permute-start | bytes 1179656 | tf_op jit(solution)/shard_map/ppermute | solution.py:21
  213.8 20.7 %collective-permute-start.15 = (bf16[128,3072]{1,0:T(8,128)(2,1)}, bf16[128,3072]{1,0:T(8,128)(2,1)}, u32[]{:S(2)}, u32[]{:S(2)}) collective-permute-start(bf16[128,3072]{1,0:T(8,128)(2,1)} %copy.27.refs_0_), channel_id=1, source_target_pairs={{0,8},{4,12},{8,0},{12,4},{16,24},{20,28},{24,16},{28,20},{1,9},{5... | collective-permute-start | bytes 2359304 | tf_op jit(solution)/shard_map/ppermute | solution.py:21
  214.3 20.8 %collective-permute-start.19 = (bf16[128,3072]{1,0:T(8,128)(2,1)S(1)}, bf16[128,3072]{1,0:T(8,128)(2,1)}, u32[]{:S(2)}, u32[]{:S(2)}) collective-permute-start(bf16[128,3072]{1,0:T(8,128)(2,1)S(1)} %copy.28.refs_4_), channel_id=1, source_target_pairs={{0,16},{4,20},{8,24},{12,28},{16,0},{20,4},{24,8},{28,12},{1,17},{... | collective-permute-start | bytes 2359304 | tf_op jit(solution)/shard_map/ppermute | solution.py:21
  214.6 36.8 %collective-permute-start.17 = (bf16[128,3072]{1,0:T(8,128)(2,1)}, bf16[128,3072]{1,0:T(8,128)(2,1)}, u32[]{:S(2)}, u32[]{:S(2)}) collective-permute-start(bf16[128,3072]{1,0:T(8,128)(2,1)} %collective-permute-done.16.refs_2_), channel_id=1, source_target_pairs={{0,8},{4,12},{8,0},{12,4},{16,24},{20,28},{24,16},{28,20},{1,9},{5... | collective-permute-start | bytes 2359304 | tf_op jit(solution)/shard_map/ppermute | solution.py:21
  216.3 35.5 %collective-permute-start.20 = (bf16[128,3072]{1,0:T(8,128)(2,1)}, bf16[128,3072]{1,0:T(8,128)(2,1)}, u32[]{:S(2)}, u32[]{:S(2)}) collective-permute-start(bf16[128,3072]{1,0:T(8,128)(2,1)} %collective-permute-done.18.refs_5_), channel_id=1, source_target_pairs={{0,16},{4,20},{8,24},{12,28},{16,0},{20,4},{24,8},{28,12},{1,17},{... | collective-permute-start | bytes 2359304 | tf_op jit(solution)/shard_map/ppermute | solution.py:21
  234.5 34.0 %collective-permute-start.26 = (bf16[128,3072]{1,0:T(8,128)(2,1)S(1)}, bf16[128,3072]{1,0:T(8,128)(2,1)}, u32[]{:S(2)}, u32[]{:S(2)}) collective-permute-start(bf16[128,3072]{1,0:T(8,128)(2,1)S(1)} %copy.29.refs_0_), channel_id=1, source_target_pairs={{0,16},{4,20},{8,24},{12,28},{16,0},{20,4},{24,8},{28,12},{1,17},{... | collective-permute-start | bytes 2359304 | tf_op jit(solution)/shard_map/ppermute | solution.py:21
  235.0 35.0 %collective-permute-start.28 = (bf16[128,3072]{1,0:T(8,128)(2,1)S(1)}, bf16[128,3072]{1,0:T(8,128)(2,1)}, u32[]{:S(2)}, u32[]{:S(2)}) collective-permute-start(bf16[128,3072]{1,0:T(8,128)(2,1)S(1)} %copy.30.refs_4_), channel_id=1, source_target_pairs={{0,8},{4,12},{8,0},{12,4},{16,24},{20,28},{24,16},{28,20},{1,9},{5... | collective-permute-start | bytes 2359304 | tf_op jit(solution)/shard_map/ppermute | solution.py:21
  251.4 25.3 %collective-permute-start.37 = (bf16[64,3072]{1,0:T(8,128)(2,1)}, bf16[64,3072]{1,0:T(8,128)(2,1)}, u32[]{:S(2)}, u32[]{:S(2)}) collective-permute-start(bf16[64,3072]{1,0:T(8,128)(2,1)} %copy-done.7), channel_id=1, source_target_pairs={{0,8},{4,12},{8,0},{12,4},{16,24},{20,28},{24,16},{28,20},{1,9},{5... | collective-permute-start | bytes 1179656 | tf_op jit(solution)/shard_map/ppermute | solution.py:21
  251.8 25.3 %collective-permute-start.40 = (bf16[64,3072]{1,0:T(8,128)(2,1)}, bf16[64,3072]{1,0:T(8,128)(2,1)}, u32[]{:S(2)}, u32[]{:S(2)}) collective-permute-start(bf16[64,3072]{1,0:T(8,128)(2,1)} %copy-done.8), channel_id=1, source_target_pairs={{0,16},{4,20},{8,24},{12,28},{16,0},{20,4},{24,8},{28,12},{1,17},{... | collective-permute-start | bytes 1179656 | tf_op jit(solution)/shard_map/ppermute | solution.py:21
  252.2 32.8 %collective-permute-start.47 = (bf16[64,3072]{1,0:T(8,128)(2,1)}, bf16[64,3072]{1,0:T(8,128)(2,1)S(1)}, u32[]{:S(2)}, u32[]{:S(2)}) collective-permute-start(bf16[64,3072]{1,0:T(8,128)(2,1)} %collective-permute-done.46.refs_2_), channel_id=1, source_target_pairs={{0,8},{4,12},{8,0},{12,4},{16,24},{20,28},{24,16},{28,20},{1,9},{5... | collective-permute-start | bytes 1179656 | tf_op jit(solution)/shard_map/ppermute | solution.py:21
  268.5 46.3 %collective-permute-start.25 = (bf16[128,3072]{1,0:T(8,128)(2,1)S(1)}, bf16[128,3072]{1,0:T(8,128)(2,1)}, u32[]{:S(2)}, u32[]{:S(2)}) collective-permute-start(bf16[128,3072]{1,0:T(8,128)(2,1)S(1)} %copy.29.refs_0_), channel_id=1, source_target_pairs={{0,8},{4,12},{8,0},{12,4},{16,24},{20,28},{24,16},{28,20},{1,9},{5... | collective-permute-start | bytes 2359304 | tf_op jit(solution)/shard_map/ppermute | solution.py:21
  270.1 45.4 %collective-permute-start.29 = (bf16[128,3072]{1,0:T(8,128)(2,1)S(1)}, bf16[128,3072]{1,0:T(8,128)(2,1)}, u32[]{:S(2)}, u32[]{:S(2)}) collective-permute-start(bf16[128,3072]{1,0:T(8,128)(2,1)S(1)} %copy.30.refs_4_), channel_id=1, source_target_pairs={{0,16},{4,20},{8,24},{12,28},{16,0},{20,4},{24,8},{28,12},{1,17},{... | collective-permute-start | bytes 2359304 | tf_op jit(solution)/shard_map/ppermute | solution.py:21
  276.7 25.4 %collective-permute-start.50 = (bf16[64,3072]{1,0:T(8,128)(2,1)}, bf16[64,3072]{1,0:T(8,128)(2,1)S(1)}, u32[]{:S(2)}, u32[]{:S(2)}) collective-permute-start(bf16[64,3072]{1,0:T(8,128)(2,1)} %collective-permute-done.48.refs_5_), channel_id=1, source_target_pairs={{0,16},{4,20},{8,24},{12,28},{16,0},{20,4},{24,8},{28,12},{1,17},{... | collective-permute-start | bytes 1179656 | tf_op jit(solution)/shard_map/ppermute | solution.py:21
  277.2 40.9 %collective-permute-start.27 = (bf16[128,3072]{1,0:T(8,128)(2,1)}, bf16[128,3072]{1,0:T(8,128)(2,1)}, u32[]{:S(2)}, u32[]{:S(2)}) collective-permute-start(bf16[128,3072]{1,0:T(8,128)(2,1)} %collective-permute-done.26.refs_2_), channel_id=1, source_target_pairs={{0,8},{4,12},{8,0},{12,4},{16,24},{20,28},{24,16},{28,20},{1,9},{5... | collective-permute-start | bytes 2359304 | tf_op jit(solution)/shard_map/ppermute | solution.py:21
  285.0 35.3 %collective-permute-start.30 = (bf16[128,3072]{1,0:T(8,128)(2,1)}, bf16[128,3072]{1,0:T(8,128)(2,1)}, u32[]{:S(2)}, u32[]{:S(2)}) collective-permute-start(bf16[128,3072]{1,0:T(8,128)(2,1)} %collective-permute-done.28.refs_5_), channel_id=1, source_target_pairs={{0,16},{4,20},{8,24},{12,28},{16,0},{20,4},{24,8},{28,12},{1,17},{... | collective-permute-start | bytes 2359304 | tf_op jit(solution)/shard_map/ppermute | solution.py:21
  302.1 68.2 %collective-permute-start.21 = (bf16[128,1024]{1,0:T(8,128)(2,1)S(1)}, bf16[128,1024]{1,0:T(8,128)(2,1)S(1)}, u32[]{:S(2)}, u32[]{:S(2)}) collective-permute-start(bf16[128,1024]{1,0:T(8,128)(2,1)S(1)} %get-tuple-element.17), channel_id=1, source_target_pairs={{0,1},{1,0},{2,3},{3,2},{4,5},{5,4},{6,7},{7,6},{8,9},{9,8},{10,11... | collective-permute-start | bytes 786440 | tf_op jit(solution)/shard_map/ppermute | solution.py:26
  314.7 20.0 %collective-permute-start.41 = (bf16[64,1024]{1,0:T(8,128)(2,1)}, bf16[64,1024]{1,0:T(8,128)(2,1)S(1)}, u32[]{:S(2)}, u32[]{:S(2)}) collective-permute-start(bf16[64,1024]{1,0:T(8,128)(2,1)} %get-tuple-element.27), channel_id=1, source_target_pairs={{0,1},{1,0},{2,3},{3,2},{4,5},{5,4},{6,7},{7,6},{8,9},{9,8},{10,11... | collective-permute-start | bytes 393224 | tf_op jit(solution)/shard_map/ppermute | solution.py:26
  315.5 21.5 %collective-permute-start.42 = (bf16[64,1024]{1,0:T(8,128)(2,1)}, bf16[64,1024]{1,0:T(8,128)(2,1)S(1)}, u32[]{:S(2)}, u32[]{:S(2)}) collective-permute-start(bf16[64,1024]{1,0:T(8,128)(2,1)} %get-tuple-element.29), channel_id=1, source_target_pairs={{0,2},{1,3},{2,0},{3,1},{4,6},{5,7},{6,4},{7,5},{8,10},{9,11},{10,... | collective-permute-start | bytes 393224 | tf_op jit(solution)/shard_map/ppermute | solution.py:26
  318.1 21.1 %collective-permute-start.43 = (bf16[64,1024]{1,0:T(8,128)(2,1)}, bf16[64,1024]{1,0:T(8,128)(2,1)}, u32[]{:S(2)}, u32[]{:S(2)}) collective-permute-start(bf16[64,1024]{1,0:T(8,128)(2,1)} %get-tuple-element.28), channel_id=1, source_target_pairs={{0,3},{1,2},{2,1},{3,0},{4,7},{5,6},{6,5},{7,4},{8,11},{9,10},{10,... | collective-permute-start | bytes 393224 | tf_op jit(solution)/shard_map/ppermute | solution.py:26
  320.3 18.9 %collective-permute-start.51 = (bf16[64,1024]{1,0:T(8,128)(2,1)}, bf16[64,1024]{1,0:T(8,128)(2,1)S(1)}, u32[]{:S(2)}, u32[]{:S(2)}) collective-permute-start(bf16[64,1024]{1,0:T(8,128)(2,1)} %get-tuple-element.24), channel_id=1, source_target_pairs={{0,1},{1,0},{2,3},{3,2},{4,5},{5,4},{6,7},{7,6},{8,9},{9,8},{10,11... | collective-permute-start | bytes 393224 | tf_op jit(solution)/shard_map/ppermute | solution.py:26
  334.8 38.9 %collective-permute-start.22 = (bf16[128,1024]{1,0:T(8,128)(2,1)S(1)}, bf16[128,1024]{1,0:T(8,128)(2,1)S(1)}, u32[]{:S(2)}, u32[]{:S(2)}) collective-permute-start(bf16[128,1024]{1,0:T(8,128)(2,1)S(1)} %get-tuple-element.19), channel_id=1, source_target_pairs={{0,2},{1,3},{2,0},{3,1},{4,6},{5,7},{6,4},{7,5},{8,10},{9,11},{10,... | collective-permute-start | bytes 786440 | tf_op jit(solution)/shard_map/ppermute | solution.py:26
  337.0 37.2 %collective-permute-start.23 = (bf16[128,1024]{1,0:T(8,128)(2,1)S(1)}, bf16[128,1024]{1,0:T(8,128)(2,1)S(1)}, u32[]{:S(2)}, u32[]{:S(2)}) collective-permute-start(bf16[128,1024]{1,0:T(8,128)(2,1)S(1)} %get-tuple-element.18), channel_id=1, source_target_pairs={{0,3},{1,2},{2,1},{3,0},{4,7},{5,6},{6,5},{7,4},{8,11},{9,10},{10,... | collective-permute-start | bytes 786440 | tf_op jit(solution)/shard_map/ppermute | solution.py:26
  339.2 29.0 %collective-permute-start.52 = (bf16[64,1024]{1,0:T(8,128)(2,1)S(1)}, bf16[64,1024]{1,0:T(8,128)(2,1)S(1)}, u32[]{:S(2)}, u32[]{:S(2)}) collective-permute-start(bf16[64,1024]{1,0:T(8,128)(2,1)S(1)} %get-tuple-element.26), channel_id=1, source_target_pairs={{0,2},{1,3},{2,0},{3,1},{4,6},{5,7},{6,4},{7,5},{8,10},{9,11},{10,... | collective-permute-start | bytes 393224 | tf_op jit(solution)/shard_map/ppermute | solution.py:26
  339.2 29.0 %collective-permute-start.53 = (bf16[64,1024]{1,0:T(8,128)(2,1)S(1)}, bf16[64,1024]{1,0:T(8,128)(2,1)S(1)}, u32[]{:S(2)}, u32[]{:S(2)}) collective-permute-start(bf16[64,1024]{1,0:T(8,128)(2,1)S(1)} %get-tuple-element.25), channel_id=1, source_target_pairs={{0,3},{1,2},{2,1},{3,0},{4,7},{5,6},{6,5},{7,4},{8,11},{9,10},{10,... | collective-permute-start | bytes 393224 | tf_op jit(solution)/shard_map/ppermute | solution.py:26
  368.2 21.3 %collective-permute-start.32 = (bf16[128,1024]{1,0:T(8,128)(2,1)S(1)}, bf16[128,1024]{1,0:T(8,128)(2,1)S(1)}, u32[]{:S(2)}, u32[]{:S(2)}) collective-permute-start(bf16[128,1024]{1,0:T(8,128)(2,1)S(1)} %get-tuple-element.16), channel_id=1, source_target_pairs={{0,2},{1,3},{2,0},{3,1},{4,6},{5,7},{6,4},{7,5},{8,10},{9,11},{10,... | collective-permute-start | bytes 786440 | tf_op jit(solution)/shard_map/ppermute | solution.py:26
  370.3 19.8 %collective-permute-start.33 = (bf16[128,1024]{1,0:T(8,128)(2,1)S(1)}, bf16[128,1024]{1,0:T(8,128)(2,1)S(1)}, u32[]{:S(2)}, u32[]{:S(2)}) collective-permute-start(bf16[128,1024]{1,0:T(8,128)(2,1)S(1)} %get-tuple-element.15), channel_id=1, source_target_pairs={{0,3},{1,2},{2,1},{3,0},{4,7},{5,6},{6,5},{7,4},{8,11},{9,10},{10,... | collective-permute-start | bytes 786440 | tf_op jit(solution)/shard_map/ppermute | solution.py:26
  373.7 35.4 %collective-permute-start.58 = (bf16[64,1024]{1,0:T(8,128)(2,1)S(1)}, bf16[64,1024]{1,0:T(8,128)(2,1)S(1)}, u32[]{:S(2)}, u32[]{:S(2)}) collective-permute-start(bf16[64,1024]{1,0:T(8,128)(2,1)S(1)} %fusion.11.refs_0_), channel_id=1, source_target_pairs={{8,0},{12,4},{0,8},{4,12},{24,16},{28,20},{16,24},{20,28},{9,1},{1... | collective-permute-start | bytes 393224 | tf_op jit(solution)/shard_map/ppermute | solution.py:217
  374.2 20.8 %collective-permute-start.54 = (bf16[64,512]{1,0:T(8,128)(2,1)S(1)}, bf16[64,512]{1,0:T(8,128)(2,1)S(1)}, u32[]{:S(2)}, u32[]{:S(2)}) collective-permute-start(bf16[64,512]{1,0:T(8,128)(2,1)S(1)} %slice.164), channel_id=1, source_target_pairs={{0,4},{4,0},{8,12},{12,8},{16,20},{20,16},{24,28},{28,24},{1,5},{5... | collective-permute-start | bytes 196616 | tf_op jit(solution)/shard_map/ppermute | solution.py:21
  396.5 18.2 %collective-permute-start.66 = (bf16[128,1024]{1,0:T(8,128)(2,1)S(1)}, bf16[128,1024]{1,0:T(8,128)(2,1)S(1)}, u32[]{:S(2)}, u32[]{:S(2)}) collective-permute-start(bf16[128,1024]{1,0:T(8,128)(2,1)S(1)} %collective-permute-done.65.refs_2_), channel_id=1, source_target_pairs={{0,8},{4,12},{8,0},{12,4},{16,24},{20,28},{24,16},{28,20},{1,9},{5... | collective-permute-start | bytes 786440 | tf_op jit(solution)/shard_map/ppermute | solution.py:21
  (42 other events, 649.7 us)

commit v3 on v2

--- a/solution.py
+++ b/solution.py
@@ -94,9 +94,10 @@
     )(left, mix, *([state] * states)).reshape(channels, states * row_count, local_right)
 
 
-def right_kernel(chips, steps, per, own_ref, sib_ref, *refs):
+def right_kernel(chips, steps, per, turn_ref, own_ref, sib_ref, *refs):
     first, second = refs[:chips], refs[chips : 2 * chips]
-    out_ref, rhs, total = refs[2 * chips :]
+    outs = refs[2 * chips : 3 * chips]
+    rhs, total = refs[3 * chips :]
     step = pl.program_id(0)
     width = first[0].shape[0]
     rows = own_ref.shape[1]
@@ -118,38 +119,42 @@
         def _():
             total[:, here] = value
 
-        @pl.when(jnp.logical_and(step > 0, step < steps - 1))
+        @pl.when(step > 0)
         def _():
             total[:, here] += value
 
-        @pl.when(step == steps - 1)
-        def _():
-            final = (total[:, here] + value).astype(out_ref.dtype)
-            for q in range(chips):
-                out_ref[q, :, here] = final[q * width : (q + 1) * width]
-
-
-def right_product(own, sib, first, second):
+    @pl.when(step == steps - 1)
+    def _():
+        for m in range(chips):
+            at = pl.multiple_of((turn_ref[0] ^ m) * width, 16)
+            outs[m][...] = total[pl.ds(at, width), :].astype(outs[m].dtype)
+
+
+def right_product(turn, own, sib, first, second):
     chips = len(first)
     channels, rows, depth = own.shape
     width = first[0].shape[0]
     per = 2 if channels % 4 == 0 else 1
     steps = channels // per
     half = steps // 2
-    lhs_spec = pl.BlockSpec((per, rows, depth), lambda k: (k, 0, 0))
-    first_spec = pl.BlockSpec((width, per * depth), lambda k: (0, jnp.minimum(k, half - 1)))
-    second_spec = pl.BlockSpec((width, per * depth), lambda k: (0, jnp.maximum(k - half, 0)))
-    shape = (chips, width, 2 * rows)
+    shape = (width, 2 * rows)
     return pl.pallas_call(
         functools.partial(right_kernel, chips, steps, per),
-        out_shape=jax.ShapeDtypeStruct(shape, jnp.bfloat16),
-        grid=(steps,),
-        in_specs=[lhs_spec] * 2 + [first_spec] * chips + [second_spec] * chips,
-        out_specs=pl.BlockSpec(shape, lambda k: (0, 0, 0)),
-        scratch_shapes=[
-            pltpu.VMEM((chips * width, per * depth), jnp.bfloat16),
-            pltpu.VMEM((chips * width, 2 * rows), jnp.float32),
-        ],
+        out_shape=[jax.ShapeDtypeStruct(shape, jnp.bfloat16)] * chips,
+        grid_spec=pltpu.PrefetchScalarGridSpec(
+            num_scalar_prefetch=1,
+            grid=(steps,),
+            in_specs=[pl.BlockSpec((per, rows, depth), lambda k, t: (k, 0, 0))] * 2
+            + [pl.BlockSpec((width, per * depth), lambda k, t: (0, jnp.minimum(k, half - 1)))]
+            * chips
+            + [pl.BlockSpec((width, per * depth), lambda k, t: (0, jnp.maximum(k - half, 0)))]
+            * chips,
+            out_specs=[pl.BlockSpec(shape, lambda k, t: (0, 0))] * chips,
+            scratch_shapes=[
+                pltpu.VMEM((chips * width, per * depth), jnp.bfloat16),
+                pltpu.VMEM((chips * width, 2 * rows), jnp.float32),
+            ],
+        ),
         compiler_params=pltpu.CompilerParams(vmem_limit_bytes=60 << 20),
         cost_estimate=pl.CostEstimate(
             flops=4 * rows * depth * channels * chips * width,
@@ -157,7 +162,7 @@
             transcendentals=0,
         ),
         name="right_product",
-    )(own, sib, *first, *second)
+    )(turn, own, sib, *first, *second)
 
 
 def gram_kernel(chips, states, rows, start, *refs):
@@ -199,15 +204,10 @@
     )(*tiles, *before)
 
 
-def exchange(parts, own_slot):
-    z = lax.axis_index("rb")
-
-    def slot(target):
-        return lax.dynamic_index_in_dim(parts, target ^ own_slot, 0, keepdims=False)
-
-    total = slot(z).astype(jnp.float32)
-    for mask in range(1, lax.axis_size("rb")):
-        total = total + rb_hop(slot(z ^ mask), mask).astype(jnp.float32)
+def exchange(parts):
+    total = parts[0].astype(jnp.float32)
+    for m in range(1, len(parts)):
+        total = total + rb_hop(parts[m], m).astype(jnp.float32)
     return total
 
 
@@ -232,11 +232,12 @@
     bits = [1 << i for i in range(chips.bit_length() - 1)]
     orders = (bits[::-1], bits)
 
-    flat = wavefunction.reshape(piece_rows, states * local_right)
     half_rows = piece_rows // 2
     state = jnp.zeros((full_bond, states * local_right), wavefunction.dtype)
     for half in range(2):
-        held = spread(flat[half * half_rows : (half + 1) * half_rows], orders[half])
+        source = wavefunction if half == 0 else lax.optimization_barrier(wavefunction)
+        piece = source[half * half_rows : (half + 1) * half_rows]
+        held = spread(piece.reshape(half_rows, states * local_right), orders[half])
         for q, piece in held.items():
             for e in range(2):
                 value = piece if e == 0 else hop(piece, 1)
@@ -253,6 +254,7 @@
 
     half = channels // 2
     flipped = right_environment.transpose(2, 0, 1).reshape(tile_width, channels * local_right)
+    turn = (chip ^ z).astype(jnp.int32).reshape(1)
     mine, theirs = [], []
     gram = None
     for j in range(CHUNKS):
@@ -262,36 +264,29 @@
             part = flipped[here, h * half * local_right : (h + 1) * half * local_right]
             held = spread(part, orders[h])
             pieces.append([held[q] for q in range(chips)])
-        parts = right_product(mixed, mixed_sibling, *pieces)
-        applied = exchange(parts, chip).astype(jnp.bfloat16)
+        parts = right_product(turn, mixed, mixed_sibling, *pieces)
+        applied = exchange(parts).astype(jnp.bfloat16)
         own_rows = row_count * states
         mine.append(applied[:, :own_rows])
         theirs.append(hop(applied[:, own_rows:], 1))
         if j < CHUNKS // 2:
             held = spread(applied, orders[j % 2])
         else:
-            held = {q: fetch(applied, q) if q else applied for q in range(chips)}
+            held = {0: applied}
+            for q in range(chips - 1, 0, -1):
+                held[q] = fetch(applied, q)
         gram = add_gram(gram, [held[q] for q in range(chips)], states, row_count)
 
     def ordered(value, other):
         return (jnp.where(first_core, value, other), jnp.where(first_core, other, value))
 
     gram = jnp.concatenate(ordered(gram[:, :, :row_count], gram[:, :, row_count:]), axis=2)
-    gram = gram.astype(jnp.bfloat16)
-    rb_size = lax.axis_size("rb")
-    block = 0.0
-    for e in range(2):
-        for mask in range(rb_size):
-            part = lax.dynamic_index_in_dim(gram, (z ^ mask) ^ chip, 0, keepdims=False)
-            part = part[e * row_count : (e + 1) * row_count]
-            if e or mask:
-                pairs = [
-                    (b * rb_size + i, (b ^ e) * rb_size + (i ^ mask))
-                    for b in range(tiles)
-                    for i in range(rb_size)
-                ]
-                part = lax.ppermute(part, ("lb", "rb"), pairs)
-            block = block + part.astype(jnp.float32)
+    received = hop(gram[:, row_count:].astype(jnp.bfloat16), 1)
+    gram = (gram[:, :row_count] + received.astype(jnp.float32)).astype(jnp.bfloat16)
+    blocks = [
+        lax.dynamic_index_in_dim(gram, turn[0] ^ m, 0, keepdims=False) for m in range(chips)
+    ]
+    block = exchange(blocks)
     columns = [ordered(a, b) for a, b in zip(mine, theirs)]
     applied = jnp.concatenate([c[0] for c in columns] + [c[1] for c in columns], axis=0)
     applied = applied.reshape(2 * tile_width, states, row_count).transpose(2, 1, 0)

time: 444 us -> 441 us (level)
  waiting for transfers between devices: 217 us -> 225 us
    ppermute x6, waiting for transfers between devices: 1.72 us -> 16 us  [fetch(): return lax.ppermute(value, 'lb', [(i ^ 2 * q, i) for i in near])]
    ppermute x7 -> x0, starting transfers between devices: 9.81 us -> none  [shards(): part = lax.ppermute(part, ('lb', 'rb'), pairs)]
    ppermute x12 -> x15, starting transfers between devices: 17.7 us -> 23 us  [rb_hop(): return lax.ppermute(value, 'rb', [(i, i ^ mask) for i in range(devices)])]
    squeeze x4 -> x1, local copies, waits for them, and re-layouts: 4.68 us -> 0.02 us  [shards(): lax.dynamic_index_in_dim(gram, turn[0] ^ m, 0, keepdims=False)]
    ppermute x49 -> x50, waiting for transfers between devices: 172 us -> 169 us  [hop(): return lax.ppermute(value, 'lb', [(i, i ^ mask) for i in range(devices)])]
    ppermute x12 -> x15, waiting for transfers between devices: 41.4 us -> 39.5 us  [rb_hop(): return lax.ppermute(value, 'rb', [(i, i ^ mask) for i in range(devices)])]
    ppermute x49 -> x50, starting transfers between devices: 36.1 us -> 35.7 us  [hop(): return lax.ppermute(value, 'lb', [(i, i ^ mask) for i in range(devices)])]
  transfers between devices with their start and end apart: 74 -> 71, of which waited for: 26 -> 27; matrix products, arithmetic and copies ran while one was open for 16% -> 15% of each run, Pallas kernels for 11% -> 11%
where the time goes in v3:
time: 441 us; the launch traced here: 439 us
  waiting for transfers between devices  225 us (51%)
  Pallas kernels  75.7 us (17%)
  local copies, waits for them, and re-layouts  66.8 us (15%)
  starting transfers between devices  65.9 us (15%)
    ppermute x50, waiting for transfers between devices, hop(): return lax.ppermute(value, 'lb', [(i, i ^ mask) for i in range(devices)])  169 us
    pallas_call x4, Pallas kernels, right_product(): pl.pallas_call(functools.partial(right_kernel, chips, steps, per), out_sh...  45.8 us
    ppermute x15, waiting for transfers between devices, rb_hop(): return lax.ppermute(value, 'rb', [(i, i ^ mask) for i in range(devices)])  39.5 us
    ppermute x50, starting transfers between devices, hop(): return lax.ppermute(value, 'lb', [(i, i ^ mask) for i in range(devices)])  35.7 us
    pallas_call x1, Pallas kernels, left_mix(): pl.pallas_call(functools.partial(left_kernel, states, channels, group_row...  28.4 us
    dynamic_update_slice x16, local copies, waits for them, and re-layouts, shards(): state = lax.dynamic_update_slice(state, value, (start, jnp.int32(0)))  26.7 us
    ppermute x15, starting transfers between devices, rb_hop(): return lax.ppermute(value, 'rb', [(i, i ^ mask) for i in range(devices)])  23 us
    ppermute x6, waiting for transfers between devices, fetch(): return lax.ppermute(value, 'lb', [(i ^ 2 * q, i) for i in near])  16 us
  transfers between devices with their start and end apart: 71, of which 27 were waited for; matrix products, arithmetic and copies ran while one was open for 15% of the time, Pallas kernels for 11%

profile of v3, /device:TPU:0, one launch (start us, length us, event | category | flops | bytes accessed | tf_op | source)
XLA Modules:
  0.0 439.1 jit_solution(2170629185946316257)
XLA Ops:
  3.6 3.0 collective-permute-start.1
  11.9 21.0 %collective-permute-done.1 = bf16[192,3072]{1,0:T(8,128)(2,1)} collective-permute-done((bf16[192,3072]{1,0:T(8,128)(2,1)}, bf16[192,3072]{1,0:T(8,128)(2,1)}, u32[]{:S(2)}, u32[]{:S(2)}) %collective-permute-start.1) | collective-permute-done | bytes 1179680 | tf_op jit(solution)/shard_map/ppermute | solution.py:21
  35.2 8.9 %copy.42 = bf16[128,8,3072]{2,1,0:T(8,128)(2,1)} copy(bf16[128,8,3072]{2,0,1:T(8,128)(2,1)} %bitcast.44) | data formatting | bytes 12582912 | tf_op jit(solution)/shard_map/transpose | solution.py:251
  44.0 3.5 convert_element_type.96.mix_ref
  47.5 6.8 %broadcast_in_dim.22 = bf16[3072,3072]{1,0:T(8,128)(2,1)} broadcast(bf16[]{:T(256)} %constant.69.clone.1), dimensions={} | broadcast | bytes 18874370 | tf_op jit(solution)/shard_map/broadcast_in_dim | solution.py:236
  54.3 2.4 constant_dynamic-update-slice_fusion.15
  58.2 2.8 collective-permute-done.8
  61.0 2.4 constant_dynamic-update-slice_fusion.14
  63.4 2.4 constant_dynamic-update-slice_fusion.13
  65.8 20.1 %collective-permute-done.5 = bf16[192,3072]{1,0:T(8,128)(2,1)} collective-permute-done((bf16[192,3072]{1,0:T(8,128)(2,1)}, bf16[192,3072]{1,0:T(8,128)(2,1)}, u32[]{:S(2)}, u32[]{:S(2)}) %collective-permute-start.5) | collective-permute-done | bytes 1179680 | tf_op jit(solution)/shard_map/ppermute | solution.py:21
  85.8 2.4 constant_dynamic-update-slice_fusion.12
  88.2 2.4 constant_dynamic-update-slice_fusion.11
  91.2 18.8 %collective-permute-done.12 = bf16[192,3072]{1,0:T(8,128)(2,1)S(1)} collective-permute-done((bf16[192,3072]{1,0:T(8,128)(2,1)}, bf16[192,3072]{1,0:T(8,128)(2,1)S(1)}, u32[]{:S(2)}, u32[]{:S(2)}) %collective-permute-start.12) | collective-permute-done | bytes 1179680 | tf_op jit(solution)/shard_map/ppermute | solution.py:21
  111.3 2.4 constant_dynamic-update-slice_fusion.9
  116.9 2.4 constant_dynamic-update-slice_fusion.5
  125.0 28.4 %left_mix.1 = bf16[8,4,128,768]{3,2,1,0:T(8,128)(2,1)} custom-call(bf16[1024,3072]{1,0:T(8,128)(2,1)} %bitcast.41, bf16[256,256]{1,0:T(8,128)(2,1)} %convert_element_type.96.mix_ref, bf16[3072,3072]{1,0:T(8,128)(2,1)} %constant_dynamic-update-slice_fusion.refs_0_.refs_1_.refs_2_.refs_3_, ...), custom_call_target="tpu_custom_call" | custom-call | flops 19327352832 | bytes 37748736 | tf_op jit(solution)/shard_map/left_mix/pallas_call | solution.py:76
  153.8 2.7 fusion.11
  163.0 3.0 fusion.12
  166.0 3.0 collective-permute-done.36.refs_2_
  171.6 6.2 %collective-permute-done.38.refs_5_ = bf16[64,3072]{1,0:T(8,128)(2,1)} collective-permute-done((bf16[64,3072]{1,0:T(8,128)(2,1)}, bf16[64,3072]{1,0:T(8,128)(2,1)}, u32[]{:S(2)}, u32[]{:S(2)}) %collective-permute-start.38) | collective-permute-done | bytes 393248 | tf_op jit(solution)/shard_map/ppermute | solution.py:21
  178.2 2.3 copy.27.refs_0_
  183.8 2.1 collective-permute-done.46.refs_2_
  186.2 3.8 collective-permute-done.48.refs_5_
  190.5 7.9 %collective-permute-done.45.refs_1_ = bf16[64,3072]{1,0:T(8,128)(2,1)S(1)} collective-permute-done((bf16[64,3072]{1,0:T(8,128)(2,1)}, bf16[64,3072]{1,0:T(8,128)(2,1)S(1)}, u32[]{:S(2)}, u32[]{:S(2)}) %collective-permute-start.45) | collective-permute-done | bytes 393248 | tf_op jit(solution)/shard_map/ppermute | solution.py:21
  199.2 11.0 %collective-permute-done.49.refs_6_ = bf16[64,3072]{1,0:T(8,128)(2,1)S(1)} collective-permute-done((bf16[64,3072]{1,0:T(8,128)(2,1)}, bf16[64,3072]{1,0:T(8,128)(2,1)S(1)}, u32[]{:S(2)}, u32[]{:S(2)}) %collective-permute-start.49) | collective-permute-done | bytes 393248 | tf_op jit(solution)/shard_map/ppermute | solution.py:21
  212.5 2.9 collective-permute-done.18.refs_5_
  215.8 16.4 %collective-permute-done.15.refs_1_ = bf16[128,3072]{1,0:T(8,128)(2,1)} collective-permute-done((bf16[128,3072]{1,0:T(8,128)(2,1)}, bf16[128,3072]{1,0:T(8,128)(2,1)}, u32[]{:S(2)}, u32[]{:S(2)}) %collective-permute-start.15) | collective-permute-done | bytes 786464 | tf_op jit(solution)/shard_map/ppermute | solution.py:21
  234.3 11.8 %collective-permute-done.26.refs_2_ = bf16[128,3072]{1,0:T(8,128)(2,1)} collective-permute-done((bf16[128,3072]{1,0:T(8,128)(2,1)S(1)}, bf16[128,3072]{1,0:T(8,128)(2,1)}, u32[]{:S(2)}, u32[]{:S(2)}) %collective-permute-start.26) | collective-permute-done | bytes 786464 | tf_op jit(solution)/shard_map/ppermute | solution.py:21
  249.5 7.9 %collective-permute-done.37.refs_3_ = bf16[64,3072]{1,0:T(8,128)(2,1)S(1)} collective-permute-done((bf16[64,3072]{1,0:T(8,128)(2,1)}, bf16[64,3072]{1,0:T(8,128)(2,1)S(1)}, u32[]{:S(2)}, u32[]{:S(2)}) %collective-permute-start.37) | collective-permute-done | bytes 393248 | tf_op jit(solution)/shard_map/ppermute | solution.py:21
  259.8 12.9 %collective-permute-done.40.refs_7_ = bf16[64,3072]{1,0:T(8,128)(2,1)} collective-permute-done((bf16[64,3072]{1,0:T(8,128)(2,1)}, bf16[64,3072]{1,0:T(8,128)(2,1)}, u32[]{:S(2)}, u32[]{:S(2)}) %collective-permute-start.40) | collective-permute-done | bytes 393248 | tf_op jit(solution)/shard_map/ppermute | solution.py:21
  272.9 9.7 %collective-permute-done.47.refs_3_ = bf16[64,3072]{1,0:T(8,128)(2,1)S(1)} collective-permute-done((bf16[64,3072]{1,0:T(8,128)(2,1)}, bf16[64,3072]{1,0:T(8,128)(2,1)S(1)}, u32[]{:S(2)}, u32[]{:S(2)}) %collective-permute-start.47) | collective-permute-done | bytes 393248 | tf_op jit(solution)/shard_map/ppermute | solution.py:21
  285.5 13.5 %right_product.4 = (bf16[128,1024]{1,0:T(8,128)(2,1)}, bf16[128,1024]{1,0:T(8,128)(2,1)}, bf16[128,1024]{1,0:T(8,128)(2,1)}, bf16[128,1024]{1,0:T(8,128)(2,1)}) custom-call(s32[1]{0:T(128)} %bitcast.turn_ref, bf16[8,512,768]{2,1,0:T(8,128)(2,1)} %bitcast.37, bf16[8,512,768]{2,1,0:T(8,128)(2,1)} %collective-permute-done.14.sib_ref, ...), custom_call_target="tpu_custom_call" | custom-call | flops 6442450944 | bytes 18874368 | tf_op jit(solution)/shard_map/right_product/pallas_call | solution.py:141
  299.1 9.4 %right_product.6 = (bf16[64,1024]{1,0:T(8,128)(2,1)}, bf16[64,1024]{1,0:T(8,128)(2,1)}, bf16[64,1024]{1,0:T(8,128)(2,1)}, bf16[64,1024]{1,0:T(8,128)(2,1)}) custom-call(s32[1]{0:T(128)} %bitcast.turn_ref, bf16[8,512,768]{2,1,0:T(8,128)(2,1)} %bitcast.38, bf16[8,512,768]{2,1,0:T(8,128)(2,1)} %collective-permute-done.14.sib_ref, bf16[64,3072]{1,0:T(8,128)(2,1)} %copy-done.2, ...), custom_call_target="tpu_custom_call" | custom-call | flops 3221225472 | bytes 15728640 | tf_op jit(solution)/shard_map/right_product/pallas_call | solution.py:141
  308.6 3.0 collective-permute-done.50.refs_7_
  313.2 9.5 %right_product.7 = (bf16[64,1024]{1,0:T(8,128)(2,1)}, bf16[64,1024]{1,0:T(8,128)(2,1)}, bf16[64,1024]{1,0:T(8,128)(2,1)}, bf16[64,1024]{1,0:T(8,128)(2,1)}) custom-call(s32[1]{0:T(128)} %bitcast.turn_ref, bf16[8,512,768]{2,1,0:T(8,128)(2,1)} %bitcast.39, bf16[8,512,768]{2,1,0:T(8,128)(2,1)} %collective-permute-done.14.sib_ref, ...), custom_call_target="tpu_custom_call" | custom-call | flops 3221225472 | bytes 15728640 | tf_op jit(solution)/shard_map/right_product/pallas_call | solution.py:141
  323.4 2.6 collective-permute-start.42
  327.5 13.3 %right_product.5 = (bf16[128,1024]{1,0:T(8,128)(2,1)}, bf16[128,1024]{1,0:T(8,128)(2,1)}, bf16[128,1024]{1,0:T(8,128)(2,1)}, bf16[128,1024]{1,0:T(8,128)(2,1)}) custom-call(s32[1]{0:T(128)} %bitcast.turn_ref, bf16[8,512,768]{2,1,0:T(8,128)(2,1)} %bitcast.40, bf16[8,512,768]{2,1,0:T(8,128)(2,1)} %collective-permute-done.14.sib_ref, ...), custom_call_target="tpu_custom_call" | custom-call | flops 6442450944 | bytes 18874368 | tf_op jit(solution)/shard_map/right_product/pallas_call | solution.py:141
  340.8 3.0 collective-permute-start.22
  345.8 2.0 collective-permute-start.53
  347.8 20.2 %collective-permute-done.52 = bf16[64,1024]{1,0:T(8,128)(2,1)S(1)} collective-permute-done((bf16[64,1024]{1,0:T(8,128)(2,1)S(1)}, bf16[64,1024]{1,0:T(8,128)(2,1)S(1)}, u32[]{:S(2)}, u32[]{:S(2)}) %collective-permute-start.52) | collective-permute-done | bytes 131104 | tf_op jit(solution)/shard_map/ppermute | solution.py:26
  368.4 3.6 collective-permute-start.32
  374.1 5.2 %collective-permute-done.31 = bf16[128,1024]{1,0:T(8,128)(2,1)S(1)} collective-permute-done((bf16[128,1024]{1,0:T(8,128)(2,1)}, bf16[128,1024]{1,0:T(8,128)(2,1)S(1)}, u32[]{:S(2)}, u32[]{:S(2)}) %collective-permute-start.31) | collective-permute-done | bytes 262176 | tf_op jit(solution)/shard_map/ppermute | solution.py:26
  380.3 10.3 %collective-permute-done.32 = bf16[128,1024]{1,0:T(8,128)(2,1)S(1)} collective-permute-done((bf16[128,1024]{1,0:T(8,128)(2,1)}, bf16[128,1024]{1,0:T(8,128)(2,1)S(1)}, u32[]{:S(2)}, u32[]{:S(2)}) %collective-permute-start.32) | collective-permute-done | bytes 262176 | tf_op jit(solution)/shard_map/ppermute | solution.py:26
  397.1 3.7 collective-permute-done.61.refs_1_
  402.9 11.6 %collective-permute-done.58.refs_1_ = bf16[64,1024]{1,0:T(8,128)(2,1)S(1)} collective-permute-done((bf16[64,1024]{1,0:T(8,128)(2,1)S(1)}, bf16[64,1024]{1,0:T(8,128)(2,1)S(1)}, u32[]{:S(2)}, u32[]{:S(2)}) %collective-permute-start.58) | collective-permute-done | bytes 131104 | tf_op jit(solution)/shard_map/ppermute | solution.py:217
  416.0 4.0 collective-permute-start.55
  422.0 4.4 %collective-permute-done.55.refs_1_ = bf16[64,1024]{1,0:T(8,128)(2,1)S(1)} collective-permute-done((bf16[64,1024]{1,0:T(8,128)(2,1)S(1)}, bf16[64,1024]{1,0:T(8,128)(2,1)S(1)}, u32[]{:S(2)}, u32[]{:S(2)}) %collective-permute-start.55) | collective-permute-done | bytes 131104 | tf_op jit(solution)/shard_map/ppermute | solution.py:217
  434.5 3.9 collective-permute-done.69
  (209 shorter events, 81.3 us)
Async XLA Ops:
  3.6 29.3 %collective-permute-start.1 = (bf16[192,3072]{1,0:T(8,128)(2,1)}, bf16[192,3072]{1,0:T(8,128)(2,1)}, u32[]{:S(2)}, u32[]{:S(2)}) collective-permute-start(bf16[192,3072]{1,0:T(8,128)(2,1)} %bitcast.23), channel_id=1, source_target_pairs={{0,16},{4,20},{8,24},{12,28},{16,0},{20,4},{24,8},{28,12},{1,17},{... | collective-permute-start | bytes 3538952 | tf_op jit(solution)/shard_map/ppermute | solution.py:21
  6.6 50.1 %collective-permute-start = (bf16[192,3072]{1,0:T(8,128)(2,1)}, bf16[192,3072]{1,0:T(8,128)(2,1)}, u32[]{:S(2)}, u32[]{:S(2)}) collective-permute-start(bf16[192,3072]{1,0:T(8,128)(2,1)} %bitcast.23), channel_id=1, source_target_pairs={{0,4},{4,0},{8,12},{12,8},{16,20},{20,16},{24,28},{28,24},{1,5},{5... | collective-permute-start | bytes 3538952 | tf_op jit(solution)/shard_map/ppermute | solution.py:21
  6.6 51.6 %collective-permute-start.3 = (bf16[192,3072]{1,0:T(8,128)(2,1)}, bf16[192,3072]{1,0:T(8,128)(2,1)}, u32[]{:S(2)}, u32[]{:S(2)}) collective-permute-start(bf16[192,3072]{1,0:T(8,128)(2,1)} %bitcast.23), channel_id=1, source_target_pairs={{0,8},{4,12},{8,0},{12,4},{16,24},{20,28},{24,16},{28,20},{1,9},{5... | collective-permute-start | bytes 3538952 | tf_op jit(solution)/shard_map/ppermute | solution.py:21
  9.9 51.1 %collective-permute-start.8 = (bf16[192,3072]{1,0:T(8,128)(2,1)S(1)}, bf16[192,3072]{1,0:T(8,128)(2,1)}, u32[]{:S(2)}, u32[]{:S(2)}) collective-permute-start(bf16[192,3072]{1,0:T(8,128)(2,1)S(1)} %bitcast.45), channel_id=1, source_target_pairs={{0,8},{4,12},{8,0},{12,4},{16,24},{20,28},{24,16},{28,20},{1,9},{5... | collective-permute-start | bytes 3538952 | tf_op jit(solution)/shard_map/ppermute | solution.py:21
  32.8 32.9 %collective-permute-start.2 = (bf16[192,3072]{1,0:T(8,128)(2,1)}, bf16[192,3072]{1,0:T(8,128)(2,1)}, u32[]{:S(2)}, u32[]{:S(2)}) collective-permute-start(bf16[192,3072]{1,0:T(8,128)(2,1)} %collective-permute-done.1), channel_id=1, source_target_pairs={{0,4},{4,0},{8,12},{12,8},{16,20},{20,16},{24,28},{28,24},{1,5},{5... | collective-permute-start | bytes 3538952 | tf_op jit(solution)/shard_map/ppermute | solution.py:21
  32.8 53.0 %collective-permute-start.5 = (bf16[192,3072]{1,0:T(8,128)(2,1)}, bf16[192,3072]{1,0:T(8,128)(2,1)}, u32[]{:S(2)}, u32[]{:S(2)}) collective-permute-start(bf16[192,3072]{1,0:T(8,128)(2,1)} %collective-permute-done.1), channel_id=1, source_target_pairs={{0,8},{4,12},{8,0},{12,4},{16,24},{20,28},{24,16},{28,20},{1,9},{5... | collective-permute-start | bytes 3538952 | tf_op jit(solution)/shard_map/ppermute | solution.py:21
  56.7 33.9 %collective-permute-start.10 = (bf16[192,3072]{1,0:T(8,128)(2,1)S(1)}, bf16[192,3072]{1,0:T(8,128)(2,1)S(1)}, u32[]{:S(2)}, u32[]{:S(2)}) collective-permute-start(bf16[192,3072]{1,0:T(8,128)(2,1)S(1)} %bitcast.46), channel_id=1, source_target_pairs={{0,16},{4,20},{8,24},{12,28},{16,0},{20,4},{24,8},{28,12},{1,17},{... | collective-permute-start | bytes 3538952 | tf_op jit(solution)/shard_map/ppermute | solution.py:21
  58.2 33.0 %collective-permute-start.4 = (bf16[192,3072]{1,0:T(8,128)(2,1)}, bf16[192,3072]{1,0:T(8,128)(2,1)S(1)}, u32[]{:S(2)}, u32[]{:S(2)}) collective-permute-start(bf16[192,3072]{1,0:T(8,128)(2,1)} %collective-permute-done.3), channel_id=1, source_target_pairs={{0,4},{4,0},{8,12},{12,8},{16,20},{20,16},{24,28},{28,24},{1,5},{5... | collective-permute-start | bytes 3538952 | tf_op jit(solution)/shard_map/ppermute | solution.py:21
  61.0 49.1 %collective-permute-start.12 = (bf16[192,3072]{1,0:T(8,128)(2,1)}, bf16[192,3072]{1,0:T(8,128)(2,1)S(1)}, u32[]{:S(2)}, u32[]{:S(2)}) collective-permute-start(bf16[192,3072]{1,0:T(8,128)(2,1)} %collective-permute-done.8), channel_id=1, source_target_pairs={{0,16},{4,20},{8,24},{12,28},{16,0},{20,4},{24,8},{28,12},{1,17},{... | collective-permute-start | bytes 3538952 | tf_op jit(solution)/shard_map/ppermute | solution.py:21
  65.8 50.1 %collective-permute-start.7 = (bf16[192,3072]{1,0:T(8,128)(2,1)S(1)}, bf16[192,3072]{1,0:T(8,128)(2,1)S(1)}, u32[]{:S(2)}, u32[]{:S(2)}) collective-permute-start(bf16[192,3072]{1,0:T(8,128)(2,1)S(1)} %bitcast.47), channel_id=1, source_target_pairs={{0,4},{4,0},{8,12},{12,8},{16,20},{20,16},{24,28},{28,24},{1,5},{5... | collective-permute-start | bytes 3538952 | tf_op jit(solution)/shard_map/ppermute | solution.py:21
  85.8 27.8 %collective-permute-start.6 = (bf16[192,3072]{1,0:T(8,128)(2,1)}, bf16[192,3072]{1,0:T(8,128)(2,1)S(1)}, u32[]{:S(2)}, u32[]{:S(2)}) collective-permute-start(bf16[192,3072]{1,0:T(8,128)(2,1)} %collective-permute-done.5), channel_id=1, source_target_pairs={{0,4},{4,0},{8,12},{12,8},{16,20},{20,16},{24,28},{28,24},{1,5},{5... | collective-permute-start | bytes 3538952 | tf_op jit(solution)/shard_map/ppermute | solution.py:21
  90.6 28.8 %collective-permute-start.9 = (bf16[192,3072]{1,0:T(8,128)(2,1)}, bf16[192,3072]{1,0:T(8,128)(2,1)S(1)}, u32[]{:S(2)}, u32[]{:S(2)}) collective-permute-start(bf16[192,3072]{1,0:T(8,128)(2,1)} %collective-permute-done.8), channel_id=1, source_target_pairs={{0,4},{4,0},{8,12},{12,8},{16,20},{20,16},{24,28},{28,24},{1,5},{5... | collective-permute-start | bytes 3538952 | tf_op jit(solution)/shard_map/ppermute | solution.py:21
  91.2 30.5 %collective-permute-start.11 = (bf16[192,3072]{1,0:T(8,128)(2,1)S(1)}, bf16[192,3072]{1,0:T(8,128)(2,1)S(1)}, u32[]{:S(2)}, u32[]{:S(2)}) collective-permute-start(bf16[192,3072]{1,0:T(8,128)(2,1)S(1)} %collective-permute-done.10), channel_id=1, source_target_pairs={{0,4},{4,0},{8,12},{12,8},{16,20},{20,16},{24,28},{28,24},{1,5},{5... | collective-permute-start | bytes 3538952 | tf_op jit(solution)/shard_map/ppermute | solution.py:21
  153.4 131.8 %collective-permute-start.14 = (bf16[8,512,768]{2,1,0:T(8,128)(2,1)}, bf16[8,512,768]{2,1,0:T(8,128)(2,1)}, u32[]{:S(2)}, u32[]{:S(2)}) collective-permute-start(bf16[8,512,768]{2,1,0:T(8,128)(2,1)} %bitcast.36), channel_id=1, source_target_pairs={{0,4},{4,0},{8,12},{12,8},{16,20},{20,16},{24,28},{28,24},{1,5},{5... | collective-permute-start | bytes 18874376 | tf_op jit(solution)/shard_map/ppermute | solution.py:21
  158.5 22.0 %collective-permute-start.35 = (bf16[64,3072]{1,0:T(8,128)(2,1)S(1)}, bf16[64,3072]{1,0:T(8,128)(2,1)}, u32[]{:S(2)}, u32[]{:S(2)}) collective-permute-start(bf16[64,3072]{1,0:T(8,128)(2,1)S(1)} %copy.31.refs_0_), channel_id=1, source_target_pairs={{0,8},{4,12},{8,0},{12,4},{16,24},{20,28},{24,16},{28,20},{1,9},{5... | collective-permute-start | bytes 1179656 | tf_op jit(solution)/shard_map/ppermute | solution.py:21
  161.6 20.5 %collective-permute-start.39 = (bf16[64,3072]{1,0:T(8,128)(2,1)}, bf16[64,3072]{1,0:T(8,128)(2,1)}, u32[]{:S(2)}, u32[]{:S(2)}) collective-permute-start(bf16[64,3072]{1,0:T(8,128)(2,1)} %copy.32.refs_4_), channel_id=1, source_target_pairs={{0,16},{4,20},{8,24},{12,28},{16,0},{20,4},{24,8},{28,12},{1,17},{... | collective-permute-start | bytes 1179656 | tf_op jit(solution)/shard_map/ppermute | solution.py:21
  180.5 31.1 %collective-permute-start.16 = (bf16[128,3072]{1,0:T(8,128)(2,1)}, bf16[128,3072]{1,0:T(8,128)(2,1)}, u32[]{:S(2)}, u32[]{:S(2)}) collective-permute-start(bf16[128,3072]{1,0:T(8,128)(2,1)} %copy.27.refs_0_), channel_id=1, source_target_pairs={{0,16},{4,20},{8,24},{12,28},{16,0},{20,4},{24,8},{28,12},{1,17},{... | collective-permute-start | bytes 2359304 | tf_op jit(solution)/shard_map/ppermute | solution.py:21
  185.8 29.5 %collective-permute-start.18 = (bf16[128,3072]{1,0:T(8,128)(2,1)}, bf16[128,3072]{1,0:T(8,128)(2,1)}, u32[]{:S(2)}, u32[]{:S(2)}) collective-permute-start(bf16[128,3072]{1,0:T(8,128)(2,1)} %copy.28.refs_4_), channel_id=1, source_target_pairs={{0,8},{4,12},{8,0},{12,4},{16,24},{20,28},{24,16},{28,20},{1,9},{5... | collective-permute-start | bytes 2359304 | tf_op jit(solution)/shard_map/ppermute | solution.py:21
  190.0 20.2 %collective-permute-start.49 = (bf16[64,3072]{1,0:T(8,128)(2,1)}, bf16[64,3072]{1,0:T(8,128)(2,1)S(1)}, u32[]{:S(2)}, u32[]{:S(2)}) collective-permute-start(bf16[64,3072]{1,0:T(8,128)(2,1)} %copy.34.refs_4_), channel_id=1, source_target_pairs={{0,16},{4,20},{8,24},{12,28},{16,0},{20,4},{24,8},{28,12},{1,17},{... | collective-permute-start | bytes 1179656 | tf_op jit(solution)/shard_map/ppermute | solution.py:21
  198.4 33.8 %collective-permute-start.15 = (bf16[128,3072]{1,0:T(8,128)(2,1)}, bf16[128,3072]{1,0:T(8,128)(2,1)}, u32[]{:S(2)}, u32[]{:S(2)}) collective-permute-start(bf16[128,3072]{1,0:T(8,128)(2,1)} %copy.27.refs_0_), channel_id=1, source_target_pairs={{0,8},{4,12},{8,0},{12,4},{16,24},{20,28},{24,16},{28,20},{1,9},{5... | collective-permute-start | bytes 2359304 | tf_op jit(solution)/shard_map/ppermute | solution.py:21
  210.1 22.5 %collective-permute-start.19 = (bf16[128,3072]{1,0:T(8,128)(2,1)}, bf16[128,3072]{1,0:T(8,128)(2,1)}, u32[]{:S(2)}, u32[]{:S(2)}) collective-permute-start(bf16[128,3072]{1,0:T(8,128)(2,1)} %copy.28.refs_4_), channel_id=1, source_target_pairs={{0,16},{4,20},{8,24},{12,28},{16,0},{20,4},{24,8},{28,12},{1,17},{... | collective-permute-start | bytes 2359304 | tf_op jit(solution)/shard_map/ppermute | solution.py:21
  211.7 34.4 %collective-permute-start.26 = (bf16[128,3072]{1,0:T(8,128)(2,1)S(1)}, bf16[128,3072]{1,0:T(8,128)(2,1)}, u32[]{:S(2)}, u32[]{:S(2)}) collective-permute-start(bf16[128,3072]{1,0:T(8,128)(2,1)S(1)} %copy.29.refs_0_), channel_id=1, source_target_pairs={{0,16},{4,20},{8,24},{12,28},{16,0},{20,4},{24,8},{28,12},{1,17},{... | collective-permute-start | bytes 2359304 | tf_op jit(solution)/shard_map/ppermute | solution.py:21
  215.4 33.6 %collective-permute-start.28 = (bf16[128,3072]{1,0:T(8,128)(2,1)S(1)}, bf16[128,3072]{1,0:T(8,128)(2,1)S(1)}, u32[]{:S(2)}, u32[]{:S(2)}) collective-permute-start(bf16[128,3072]{1,0:T(8,128)(2,1)S(1)} %copy.30.refs_4_), channel_id=1, source_target_pairs={{0,8},{4,12},{8,0},{12,4},{16,24},{20,28},{24,16},{28,20},{1,9},{5... | collective-permute-start | bytes 2359304 | tf_op jit(solution)/shard_map/ppermute | solution.py:21
  232.2 25.2 %collective-permute-start.37 = (bf16[64,3072]{1,0:T(8,128)(2,1)}, bf16[64,3072]{1,0:T(8,128)(2,1)S(1)}, u32[]{:S(2)}, u32[]{:S(2)}) collective-permute-start(bf16[64,3072]{1,0:T(8,128)(2,1)} %collective-permute-done.36.refs_2_), channel_id=1, source_target_pairs={{0,8},{4,12},{8,0},{12,4},{16,24},{20,28},{24,16},{28,20},{1,9},{5... | collective-permute-start | bytes 1179656 | tf_op jit(solution)/shard_map/ppermute | solution.py:21
  232.7 50.5 %collective-permute-start.17 = (bf16[128,3072]{1,0:T(8,128)(2,1)}, bf16[128,3072]{1,0:T(8,128)(2,1)}, u32[]{:S(2)}, u32[]{:S(2)}) collective-permute-start(bf16[128,3072]{1,0:T(8,128)(2,1)} %collective-permute-done.16.refs_2_), channel_id=1, source_target_pairs={{0,8},{4,12},{8,0},{12,4},{16,24},{20,28},{24,16},{28,20},{1,9},{5... | collective-permute-start | bytes 2359304 | tf_op jit(solution)/shard_map/ppermute | solution.py:21
  246.1 38.6 %collective-permute-start.20 = (bf16[128,3072]{1,0:T(8,128)(2,1)}, bf16[128,3072]{1,0:T(8,128)(2,1)}, u32[]{:S(2)}, u32[]{:S(2)}) collective-permute-start(bf16[128,3072]{1,0:T(8,128)(2,1)} %collective-permute-done.18.refs_5_), channel_id=1, source_target_pairs={{0,16},{4,20},{8,24},{12,28},{16,0},{20,4},{24,8},{28,12},{1,17},{... | collective-permute-start | bytes 2359304 | tf_op jit(solution)/shard_map/ppermute | solution.py:21
  249.0 23.8 %collective-permute-start.40 = (bf16[64,3072]{1,0:T(8,128)(2,1)}, bf16[64,3072]{1,0:T(8,128)(2,1)}, u32[]{:S(2)}, u32[]{:S(2)}) collective-permute-start(bf16[64,3072]{1,0:T(8,128)(2,1)} %collective-permute-done.38.refs_5_), channel_id=1, source_target_pairs={{0,16},{4,20},{8,24},{12,28},{16,0},{20,4},{24,8},{28,12},{1,17},{... | collective-permute-start | bytes 1179656 | tf_op jit(solution)/shard_map/ppermute | solution.py:21
  257.4 25.3 %collective-permute-start.47 = (bf16[64,3072]{1,0:T(8,128)(2,1)}, bf16[64,3072]{1,0:T(8,128)(2,1)S(1)}, u32[]{:S(2)}, u32[]{:S(2)}) collective-permute-start(bf16[64,3072]{1,0:T(8,128)(2,1)} %collective-permute-done.46.refs_2_), channel_id=1, source_target_pairs={{0,8},{4,12},{8,0},{12,4},{16,24},{20,28},{24,16},{28,20},{1,9},{5... | collective-permute-start | bytes 1179656 | tf_op jit(solution)/shard_map/ppermute | solution.py:21
  272.8 49.9 %collective-permute-start.25 = (bf16[128,3072]{1,0:T(8,128)(2,1)S(1)}, bf16[128,3072]{1,0:T(8,128)(2,1)}, u32[]{:S(2)}, u32[]{:S(2)}) collective-permute-start(bf16[128,3072]{1,0:T(8,128)(2,1)S(1)} %copy.29.refs_0_), channel_id=1, source_target_pairs={{0,8},{4,12},{8,0},{12,4},{16,24},{20,28},{24,16},{28,20},{1,9},{5... | collective-permute-start | bytes 2359304 | tf_op jit(solution)/shard_map/ppermute | solution.py:21
  282.7 40.8 %collective-permute-start.29 = (bf16[128,3072]{1,0:T(8,128)(2,1)S(1)}, bf16[128,3072]{1,0:T(8,128)(2,1)}, u32[]{:S(2)}, u32[]{:S(2)}) collective-permute-start(bf16[128,3072]{1,0:T(8,128)(2,1)S(1)} %copy.30.refs_4_), channel_id=1, source_target_pairs={{0,16},{4,20},{8,24},{12,28},{16,0},{20,4},{24,8},{28,12},{1,17},{... | collective-permute-start | bytes 2359304 | tf_op jit(solution)/shard_map/ppermute | solution.py:21
  283.2 28.3 %collective-permute-start.50 = (bf16[64,3072]{1,0:T(8,128)(2,1)}, bf16[64,3072]{1,0:T(8,128)(2,1)S(1)}, u32[]{:S(2)}, u32[]{:S(2)}) collective-permute-start(bf16[64,3072]{1,0:T(8,128)(2,1)} %copy-done.5), channel_id=1, source_target_pairs={{0,16},{4,20},{8,24},{12,28},{16,0},{20,4},{24,8},{28,12},{1,17},{... | collective-permute-start | bytes 1179656 | tf_op jit(solution)/shard_map/ppermute | solution.py:21
  284.7 41.3 %collective-permute-start.27 = (bf16[128,3072]{1,0:T(8,128)(2,1)}, bf16[128,3072]{1,0:T(8,128)(2,1)}, u32[]{:S(2)}, u32[]{:S(2)}) collective-permute-start(bf16[128,3072]{1,0:T(8,128)(2,1)} %collective-permute-done.26.refs_2_), channel_id=1, source_target_pairs={{0,8},{4,12},{8,0},{12,4},{16,24},{20,28},{24,16},{28,20},{1,9},{5... | collective-permute-start | bytes 2359304 | tf_op jit(solution)/shard_map/ppermute | solution.py:21
  285.2 42.0 %collective-permute-start.30 = (bf16[128,3072]{1,0:T(8,128)(2,1)}, bf16[128,3072]{1,0:T(8,128)(2,1)}, u32[]{:S(2)}, u32[]{:S(2)}) collective-permute-start(bf16[128,3072]{1,0:T(8,128)(2,1)} %copy-done.16), channel_id=1, source_target_pairs={{0,16},{4,20},{8,24},{12,28},{16,0},{20,4},{24,8},{28,12},{1,17},{... | collective-permute-start | bytes 2359304 | tf_op jit(solution)/shard_map/ppermute | solution.py:21
  311.5 60.4 %collective-permute-start.21 = (bf16[128,1024]{1,0:T(8,128)(2,1)}, bf16[128,1024]{1,0:T(8,128)(2,1)S(1)}, u32[]{:S(2)}, u32[]{:S(2)}) collective-permute-start(bf16[128,1024]{1,0:T(8,128)(2,1)} %get-tuple-element.19), channel_id=1, source_target_pairs={{0,1},{1,0},{2,3},{3,2},{4,5},{5,4},{6,7},{7,6},{8,9},{9,8},{10,11... | collective-permute-start | bytes 786440 | tf_op jit(solution)/shard_map/ppermute | solution.py:26
  323.4 20.4 %collective-permute-start.42 = (bf16[64,1024]{1,0:T(8,128)(2,1)}, bf16[64,1024]{1,0:T(8,128)(2,1)S(1)}, u32[]{:S(2)}, u32[]{:S(2)}) collective-permute-start(bf16[64,1024]{1,0:T(8,128)(2,1)} %get-tuple-element.28), channel_id=1, source_target_pairs={{0,2},{1,3},{2,0},{3,1},{4,6},{5,7},{6,4},{7,5},{8,10},{9,11},{10,... | collective-permute-start | bytes 393224 | tf_op jit(solution)/shard_map/ppermute | solution.py:26
  326.0 18.9 %collective-permute-start.43 = (bf16[64,1024]{1,0:T(8,128)(2,1)}, bf16[64,1024]{1,0:T(8,128)(2,1)S(1)}, u32[]{:S(2)}, u32[]{:S(2)}) collective-permute-start(bf16[64,1024]{1,0:T(8,128)(2,1)} %get-tuple-element.29), channel_id=1, source_target_pairs={{0,3},{1,2},{2,1},{3,0},{4,7},{5,6},{6,5},{7,4},{8,11},{9,10},{10,... | collective-permute-start | bytes 393224 | tf_op jit(solution)/shard_map/ppermute | solution.py:26
  327.2 18.6 %collective-permute-start.51 = (bf16[64,1024]{1,0:T(8,128)(2,1)}, bf16[64,1024]{1,0:T(8,128)(2,1)S(1)}, u32[]{:S(2)}, u32[]{:S(2)}) collective-permute-start(bf16[64,1024]{1,0:T(8,128)(2,1)} %get-tuple-element.31), channel_id=1, source_target_pairs={{0,1},{1,0},{2,3},{3,2},{4,5},{5,4},{6,7},{7,6},{8,9},{9,8},{10,11... | collective-permute-start | bytes 393224 | tf_op jit(solution)/shard_map/ppermute | solution.py:26
  340.8 32.5 %collective-permute-start.22 = (bf16[128,1024]{1,0:T(8,128)(2,1)S(1)}, bf16[128,1024]{1,0:T(8,128)(2,1)S(1)}, u32[]{:S(2)}, u32[]{:S(2)}) collective-permute-start(bf16[128,1024]{1,0:T(8,128)(2,1)S(1)} %copy-done.18), channel_id=1, source_target_pairs={{0,2},{1,3},{2,0},{3,1},{4,6},{5,7},{6,4},{7,5},{8,10},{9,11},{10,... | collective-permute-start | bytes 786440 | tf_op jit(solution)/shard_map/ppermute | solution.py:26
  343.8 29.6 %collective-permute-start.23 = (bf16[128,1024]{1,0:T(8,128)(2,1)S(1)}, bf16[128,1024]{1,0:T(8,128)(2,1)S(1)}, u32[]{:S(2)}, u32[]{:S(2)}) collective-permute-start(bf16[128,1024]{1,0:T(8,128)(2,1)S(1)} %copy-done.17), channel_id=1, source_target_pairs={{0,3},{1,2},{2,1},{3,0},{4,7},{5,6},{6,5},{7,4},{8,11},{9,10},{10,... | collective-permute-start | bytes 786440 | tf_op jit(solution)/shard_map/ppermute | solution.py:26
  345.0 23.0 %collective-permute-start.52 = (bf16[64,1024]{1,0:T(8,128)(2,1)S(1)}, bf16[64,1024]{1,0:T(8,128)(2,1)S(1)}, u32[]{:S(2)}, u32[]{:S(2)}) collective-permute-start(bf16[64,1024]{1,0:T(8,128)(2,1)S(1)} %copy-done.20), channel_id=1, source_target_pairs={{0,2},{1,3},{2,0},{3,1},{4,6},{5,7},{6,4},{7,5},{8,10},{9,11},{10,... | collective-permute-start | bytes 393224 | tf_op jit(solution)/shard_map/ppermute | solution.py:26
  345.8 22.6 %collective-permute-start.53 = (bf16[64,1024]{1,0:T(8,128)(2,1)S(1)}, bf16[64,1024]{1,0:T(8,128)(2,1)S(1)}, u32[]{:S(2)}, u32[]{:S(2)}) collective-permute-start(bf16[64,1024]{1,0:T(8,128)(2,1)S(1)} %copy-done.19), channel_id=1, source_target_pairs={{0,3},{1,2},{2,1},{3,0},{4,7},{5,6},{6,5},{7,4},{8,11},{9,10},{10,... | collective-permute-start | bytes 393224 | tf_op jit(solution)/shard_map/ppermute | solution.py:26
  368.4 22.2 %collective-permute-start.32 = (bf16[128,1024]{1,0:T(8,128)(2,1)}, bf16[128,1024]{1,0:T(8,128)(2,1)S(1)}, u32[]{:S(2)}, u32[]{:S(2)}) collective-permute-start(bf16[128,1024]{1,0:T(8,128)(2,1)} %get-tuple-element.24), channel_id=1, source_target_pairs={{0,2},{1,3},{2,0},{3,1},{4,6},{5,7},{6,4},{7,5},{8,10},{9,11},{10,... | collective-permute-start | bytes 786440 | tf_op jit(solution)/shard_map/ppermute | solution.py:26
  373.3 28.4 %collective-permute-start.54 = (bf16[64,512]{1,0:T(8,128)(2,1)S(1)}, bf16[64,512]{1,0:T(8,128)(2,1)S(1)}, u32[]{:S(2)}, u32[]{:S(2)}) collective-permute-start(bf16[64,512]{1,0:T(8,128)(2,1)S(1)} %slice.105), channel_id=1, source_target_pairs={{0,4},{4,0},{8,12},{12,8},{16,20},{20,16},{24,28},{28,24},{1,5},{5... | collective-permute-start | bytes 196616 | tf_op jit(solution)/shard_map/ppermute | solution.py:21
  373.4 21.8 %collective-permute-start.44 = (bf16[64,512]{1,0:T(8,128)(2,1)S(1)}, bf16[64,512]{1,0:T(8,128)(2,1)S(1)}, u32[]{:S(2)}, u32[]{:S(2)}) collective-permute-start(bf16[64,512]{1,0:T(8,128)(2,1)S(1)} %slice.101), channel_id=1, source_target_pairs={{0,4},{4,0},{8,12},{12,8},{16,20},{20,16},{24,28},{28,24},{1,5},{5... | collective-permute-start | bytes 196616 | tf_op jit(solution)/shard_map/ppermute | solution.py:21
  393.6 21.7 %collective-permute-start.64 = (bf16[128,1024]{1,0:T(8,128)(2,1)S(1)}, bf16[128,1024]{1,0:T(8,128)(2,1)S(1)}, u32[]{:S(2)}, u32[]{:S(2)}) collective-permute-start(bf16[128,1024]{1,0:T(8,128)(2,1)S(1)} %add_convert_fusion.1.refs_0_), channel_id=1, source_target_pairs={{0,8},{4,12},{8,0},{12,4},{16,24},{20,28},{24,16},{28,20},{1,9},{5... | collective-permute-start | bytes 786440 | tf_op jit(solution)/shard_map/ppermute | solution.py:21
  395.2 20.8 %collective-permute-start.62 = (bf16[128,1024]{1,0:T(8,128)(2,1)S(1)}, bf16[128,1024]{1,0:T(8,128)(2,1)S(1)}, u32[]{:S(2)}, u32[]{:S(2)}) collective-permute-start(bf16[128,1024]{1,0:T(8,128)(2,1)S(1)} %add_convert_fusion.refs_0_), channel_id=1, source_target_pairs={{0,16},{4,20},{8,24},{12,28},{16,0},{20,4},{24,8},{28,12},{1,17},{... | collective-permute-start | bytes 786440 | tf_op jit(solution)/shard_map/ppermute | solution.py:21
  396.1 23.8 %collective-permute-start.66 = (bf16[128,1024]{1,0:T(8,128)(2,1)S(1)}, bf16[128,1024]{1,0:T(8,128)(2,1)S(1)}, u32[]{:S(2)}, u32[]{:S(2)}) collective-permute-start(bf16[128,1024]{1,0:T(8,128)(2,1)S(1)} %collective-permute-done.65.refs_2_), channel_id=1, source_target_pairs={{0,8},{4,12},{8,0},{12,4},{16,24},{20,28},{24,16},{28,20},{1,9},{5... | collective-permute-start | bytes 786440 | tf_op jit(solution)/shard_map/ppermute | solution.py:21
  400.9 19.1 %collective-permute-start.63 = (bf16[128,1024]{1,0:T(8,128)(2,1)S(1)}, bf16[128,1024]{1,0:T(8,128)(2,1)S(1)}, u32[]{:S(2)}, u32[]{:S(2)}) collective-permute-start(bf16[128,1024]{1,0:T(8,128)(2,1)S(1)} %collective-permute-done.61.refs_1_), channel_id=1, source_target_pairs={{0,16},{4,20},{8,24},{12,28},{16,0},{20,4},{24,8},{28,12},{1,17},{... | collective-permute-start | bytes 786440 | tf_op jit(solution)/shard_map/ppermute | solution.py:21
  (44 other events, 1460.8 us)

commit v4 on v3

--- a/solution.py
+++ b/solution.py
@@ -134,7 +134,7 @@
     chips = len(first)
     channels, rows, depth = own.shape
     width = first[0].shape[0]
-    per = 2 if channels % 4 == 0 else 1
+    per = (2 if width % 128 == 0 else 4) if channels % 8 == 0 else 1
     steps = channels // per
     half = steps // 2
     shape = (width, 2 * rows)
@@ -207,7 +207,8 @@
 def exchange(parts):
     total = parts[0].astype(jnp.float32)
     for m in range(1, len(parts)):
-        total = total + rb_hop(parts[m], m).astype(jnp.float32)
+        part = rb_hop(parts[m], m)
+        total = total + part.astype(jnp.float32)
     return total
 
 
@@ -255,7 +256,7 @@
     half = channels // 2
     flipped = right_environment.transpose(2, 0, 1).reshape(tile_width, channels * local_right)
     turn = (chip ^ z).astype(jnp.int32).reshape(1)
-    mine, theirs = [], []
+    applied_parts = []
     gram = None
     for j in range(CHUNKS):
         here = slice(CUTS[j] * tile_width // CUTS[-1], CUTS[j + 1] * tile_width // CUTS[-1])
@@ -266,9 +267,7 @@
             pieces.append([held[q] for q in range(chips)])
         parts = right_product(turn, mixed, mixed_sibling, *pieces)
         applied = exchange(parts).astype(jnp.bfloat16)
-        own_rows = row_count * states
-        mine.append(applied[:, :own_rows])
-        theirs.append(hop(applied[:, own_rows:], 1))
+        applied_parts.append(applied)
         if j < CHUNKS // 2:
             held = spread(applied, orders[j % 2])
         else:
@@ -280,6 +279,10 @@
     def ordered(value, other):
         return (jnp.where(first_core, value, other), jnp.where(first_core, other, value))
 
+    own_rows = row_count * states
+    theirs = jnp.concatenate([part[:, own_rows:] for part in applied_parts], axis=0)
+    theirs = hop(theirs, 1)
+
     gram = jnp.concatenate(ordered(gram[:, :, :row_count], gram[:, :, row_count:]), axis=2)
     received = hop(gram[:, row_count:].astype(jnp.bfloat16), 1)
     gram = (gram[:, :row_count] + received.astype(jnp.float32)).astype(jnp.bfloat16)
@@ -287,8 +290,8 @@
         lax.dynamic_index_in_dim(gram, turn[0] ^ m, 0, keepdims=False) for m in range(chips)
     ]
     block = exchange(blocks)
-    columns = [ordered(a, b) for a, b in zip(mine, theirs)]
-    applied = jnp.concatenate([c[0] for c in columns] + [c[1] for c in columns], axis=0)
+    mine = jnp.concatenate([part[:, :own_rows] for part in applied_parts], axis=0)
+    applied = jnp.concatenate(ordered(mine, theirs), axis=0)
     applied = applied.reshape(2 * tile_width, states, row_count).transpose(2, 1, 0)
     own_label = lax.dynamic_index_in_dim(row_sector, me, keepdims=False)
     labels = lax.dynamic_slice_in_dim(row_sector, 2 * z, 2)

time: 441 us -> 435 us (0.986)
    ppermute x6, waiting for transfers between devices: 16 us -> 2.9 us  [fetch(): return lax.ppermute(value, 'lb', [(i ^ 2 * q, i) for i in near])]
    ppermute x50 -> x47, waiting for transfers between devices: 169 us -> 178 us  [hop(): return lax.ppermute(value, 'lb', [(i, i ^ mask) for i in range(devices)])]
    ppermute x50 -> x47, starting transfers between devices: 35.7 us -> 33.4 us  [hop(): return lax.ppermute(value, 'lb', [(i, i ^ mask) for i in range(devices)])]
    unnamed x52 -> x62, local copies, waits for them, and re-layouts: 8.83 us -> 8.85 us
  transfers between devices with their start and end apart: 71 -> 68, of which waited for: 27 -> 28; matrix products, arithmetic and copies ran while one was open for 15% -> 15% of each run, Pallas kernels for 11% -> 11%
where the time goes in v4:
time: 435 us; the launch traced here: 433 us
  waiting for transfers between devices  221 us (51%)
  Pallas kernels  74.8 us (17%)
  starting transfers between devices  66.2 us (15%)
  local copies, waits for them, and re-layouts  64.5 us (15%)
    ppermute x47, waiting for transfers between devices, hop(): return lax.ppermute(value, 'lb', [(i, i ^ mask) for i in range(devices)])  178 us
    pallas_call x4, Pallas kernels, right_product(): pl.pallas_call(functools.partial(right_kernel, chips, steps, per), out_sh...  44.8 us
    ppermute x15, waiting for transfers between devices, rb_hop(): return lax.ppermute(value, 'rb', [(i, i ^ mask) for i in range(devices)])  40.5 us
    ppermute x47, starting transfers between devices, hop(): return lax.ppermute(value, 'lb', [(i, i ^ mask) for i in range(devices)])  33.4 us
    pallas_call x1, Pallas kernels, left_mix(): pl.pallas_call(functools.partial(left_kernel, states, channels, group_row...  28.4 us
    dynamic_update_slice x16, local copies, waits for them, and re-layouts, shards(): state = lax.dynamic_update_slice(state, value, (start, jnp.int32(0)))  26.7 us
    ppermute x15, starting transfers between devices, rb_hop(): return lax.ppermute(value, 'rb', [(i, i ^ mask) for i in range(devices)])  26 us
    unnamed x62, local copies, waits for them, and re-layouts  8.85 us
  transfers between devices with their start and end apart: 68, of which 28 were waited for; matrix products, arithmetic and copies ran while one was open for 15% of the time, Pallas kernels for 11%

profile of v4, /device:TPU:0, one launch (start us, length us, event | category | flops | bytes accessed | tf_op | source)
XLA Modules:
  0.0 432.9 jit_solution(17396526075581320707)
XLA Ops:
  3.7 3.0 collective-permute-start.1
  9.6 23.4 %collective-permute-done.1 = bf16[192,3072]{1,0:T(8,128)(2,1)} collective-permute-done((bf16[192,3072]{1,0:T(8,128)(2,1)}, bf16[192,3072]{1,0:T(8,128)(2,1)}, u32[]{:S(2)}, u32[]{:S(2)}) %collective-permute-start.1) | collective-permute-done | bytes 1179680 | tf_op jit(solution)/shard_map/ppermute | solution.py:21
  35.3 8.8 %copy.42 = bf16[128,8,3072]{2,1,0:T(8,128)(2,1)} copy(bf16[128,8,3072]{2,0,1:T(8,128)(2,1)} %bitcast.44) | data formatting | bytes 12582912 | tf_op jit(solution)/shard_map/transpose | solution.py:252
  44.1 3.5 convert_element_type.96.mix_ref
  47.6 6.8 %broadcast_in_dim.22 = bf16[3072,3072]{1,0:T(8,128)(2,1)} broadcast(bf16[]{:T(256)} %constant.69.clone.1), dimensions={} | broadcast | bytes 18874370 | tf_op jit(solution)/shard_map/broadcast_in_dim | solution.py:237
  54.4 2.4 constant_dynamic-update-slice_fusion.15
  58.2 2.9 collective-permute-done.8
  61.1 2.4 constant_dynamic-update-slice_fusion.14
  63.5 2.3 constant_dynamic-update-slice_fusion.13
  65.8 20.1 %collective-permute-done.5 = bf16[192,3072]{1,0:T(8,128)(2,1)} collective-permute-done((bf16[192,3072]{1,0:T(8,128)(2,1)}, bf16[192,3072]{1,0:T(8,128)(2,1)}, u32[]{:S(2)}, u32[]{:S(2)}) %collective-permute-start.5) | collective-permute-done | bytes 1179680 | tf_op jit(solution)/shard_map/ppermute | solution.py:21
  85.9 2.4 constant_dynamic-update-slice_fusion.12
  88.3 2.4 constant_dynamic-update-slice_fusion.11
  91.3 18.8 %collective-permute-done.12 = bf16[192,3072]{1,0:T(8,128)(2,1)S(1)} collective-permute-done((bf16[192,3072]{1,0:T(8,128)(2,1)}, bf16[192,3072]{1,0:T(8,128)(2,1)S(1)}, u32[]{:S(2)}, u32[]{:S(2)}) %collective-permute-start.12) | collective-permute-done | bytes 1179680 | tf_op jit(solution)/shard_map/ppermute | solution.py:21
  111.3 2.4 constant_dynamic-update-slice_fusion.9
  117.0 2.5 constant_dynamic-update-slice_fusion.5
  125.1 28.4 %left_mix.1 = bf16[8,4,128,768]{3,2,1,0:T(8,128)(2,1)} custom-call(bf16[1024,3072]{1,0:T(8,128)(2,1)} %bitcast.41, bf16[256,256]{1,0:T(8,128)(2,1)} %convert_element_type.96.mix_ref, bf16[3072,3072]{1,0:T(8,128)(2,1)} %constant_dynamic-update-slice_fusion.refs_0_.refs_1_.refs_2_.refs_3_, ...), custom_call_target="tpu_custom_call" | custom-call | flops 19327352832 | bytes 37748736 | tf_op jit(solution)/shard_map/left_mix/pallas_call | solution.py:76
  153.9 2.7 fusion.12
  163.1 3.0 fusion.11
  166.0 3.0 collective-permute-done.34.refs_2_
  171.7 6.2 %collective-permute-done.36.refs_5_ = bf16[64,3072]{1,0:T(8,128)(2,1)} collective-permute-done((bf16[64,3072]{1,0:T(8,128)(2,1)}, bf16[64,3072]{1,0:T(8,128)(2,1)}, u32[]{:S(2)}, u32[]{:S(2)}) %collective-permute-start.36) | collective-permute-done | bytes 393248 | tf_op jit(solution)/shard_map/ppermute | solution.py:21
  178.3 2.3 copy.27.refs_0_
  183.8 2.0 collective-permute-done.43.refs_2_
  186.3 3.7 collective-permute-done.45.refs_5_
  190.5 7.9 %collective-permute-done.42.refs_1_ = bf16[64,3072]{1,0:T(8,128)(2,1)S(1)} collective-permute-done((bf16[64,3072]{1,0:T(8,128)(2,1)}, bf16[64,3072]{1,0:T(8,128)(2,1)S(1)}, u32[]{:S(2)}, u32[]{:S(2)}) %collective-permute-start.42) | collective-permute-done | bytes 393248 | tf_op jit(solution)/shard_map/ppermute | solution.py:21
  199.2 11.0 %collective-permute-done.46.refs_6_ = bf16[64,3072]{1,0:T(8,128)(2,1)S(1)} collective-permute-done((bf16[64,3072]{1,0:T(8,128)(2,1)}, bf16[64,3072]{1,0:T(8,128)(2,1)S(1)}, u32[]{:S(2)}, u32[]{:S(2)}) %collective-permute-start.46) | collective-permute-done | bytes 393248 | tf_op jit(solution)/shard_map/ppermute | solution.py:21
  212.5 2.9 collective-permute-done.18.refs_5_
  215.9 16.4 %collective-permute-done.15.refs_1_ = bf16[128,3072]{1,0:T(8,128)(2,1)} collective-permute-done((bf16[128,3072]{1,0:T(8,128)(2,1)}, bf16[128,3072]{1,0:T(8,128)(2,1)}, u32[]{:S(2)}, u32[]{:S(2)}) %collective-permute-start.15) | collective-permute-done | bytes 786464 | tf_op jit(solution)/shard_map/ppermute | solution.py:21
  234.3 11.8 %collective-permute-done.25.refs_2_ = bf16[128,3072]{1,0:T(8,128)(2,1)} collective-permute-done((bf16[128,3072]{1,0:T(8,128)(2,1)S(1)}, bf16[128,3072]{1,0:T(8,128)(2,1)}, u32[]{:S(2)}, u32[]{:S(2)}) %collective-permute-start.25) | collective-permute-done | bytes 786464 | tf_op jit(solution)/shard_map/ppermute | solution.py:21
  249.5 7.9 %collective-permute-done.35.refs_3_ = bf16[64,3072]{1,0:T(8,128)(2,1)S(1)} collective-permute-done((bf16[64,3072]{1,0:T(8,128)(2,1)}, bf16[64,3072]{1,0:T(8,128)(2,1)S(1)}, u32[]{:S(2)}, u32[]{:S(2)}) %collective-permute-start.35) | collective-permute-done | bytes 393248 | tf_op jit(solution)/shard_map/ppermute | solution.py:21
  259.7 13.0 %collective-permute-done.38.refs_7_ = bf16[64,3072]{1,0:T(8,128)(2,1)S(1)} collective-permute-done((bf16[64,3072]{1,0:T(8,128)(2,1)}, bf16[64,3072]{1,0:T(8,128)(2,1)S(1)}, u32[]{:S(2)}, u32[]{:S(2)}) %collective-permute-start.38) | collective-permute-done | bytes 393248 | tf_op jit(solution)/shard_map/ppermute | solution.py:21
  272.8 9.9 %collective-permute-done.44.refs_3_ = bf16[64,3072]{1,0:T(8,128)(2,1)S(1)} collective-permute-done((bf16[64,3072]{1,0:T(8,128)(2,1)}, bf16[64,3072]{1,0:T(8,128)(2,1)S(1)}, u32[]{:S(2)}, u32[]{:S(2)}) %collective-permute-start.44) | collective-permute-done | bytes 393248 | tf_op jit(solution)/shard_map/ppermute | solution.py:21
  285.6 13.6 %right_product.4 = (bf16[128,1024]{1,0:T(8,128)(2,1)}, bf16[128,1024]{1,0:T(8,128)(2,1)}, bf16[128,1024]{1,0:T(8,128)(2,1)}, bf16[128,1024]{1,0:T(8,128)(2,1)}) custom-call(s32[1]{0:T(128)} %bitcast.turn_ref, bf16[8,512,768]{2,1,0:T(8,128)(2,1)} %bitcast.37, bf16[8,512,768]{2,1,0:T(8,128)(2,1)} %collective-permute-done.14.sib_ref, ...), custom_call_target="tpu_custom_call" | custom-call | flops 6442450944 | bytes 18874368 | tf_op jit(solution)/shard_map/right_product/pallas_call | solution.py:141
  299.2 9.0 %right_product.6 = (bf16[64,1024]{1,0:T(8,128)(2,1)}, bf16[64,1024]{1,0:T(8,128)(2,1)}, bf16[64,1024]{1,0:T(8,128)(2,1)}, bf16[64,1024]{1,0:T(8,128)(2,1)}) custom-call(s32[1]{0:T(128)} %bitcast.turn_ref, bf16[8,512,768]{2,1,0:T(8,128)(2,1)} %bitcast.38, bf16[8,512,768]{2,1,0:T(8,128)(2,1)} %collective-permute-done.14.sib_ref, bf16[64,3072]{1,0:T(8,128)(2,1)} %copy-done.2, ...), custom_call_target="tpu_custom_call" | custom-call | flops 3221225472 | bytes 15728640 | tf_op jit(solution)/shard_map/right_product/pallas_call | solution.py:141
  308.2 3.4 collective-permute-done.47.refs_7_
  313.2 9.0 %right_product.7 = (bf16[64,1024]{1,0:T(8,128)(2,1)}, bf16[64,1024]{1,0:T(8,128)(2,1)}, bf16[64,1024]{1,0:T(8,128)(2,1)}, bf16[64,1024]{1,0:T(8,128)(2,1)}) custom-call(s32[1]{0:T(128)} %bitcast.turn_ref, bf16[8,512,768]{2,1,0:T(8,128)(2,1)} %bitcast.39, bf16[8,512,768]{2,1,0:T(8,128)(2,1)} %collective-permute-done.14.sib_ref, ...), custom_call_target="tpu_custom_call" | custom-call | flops 3221225472 | bytes 15728640 | tf_op jit(solution)/shard_map/right_product/pallas_call | solution.py:141
  323.0 2.6 collective-permute-start.40
  327.1 13.3 %right_product.5 = (bf16[128,1024]{1,0:T(8,128)(2,1)}, bf16[128,1024]{1,0:T(8,128)(2,1)}, bf16[128,1024]{1,0:T(8,128)(2,1)}, bf16[128,1024]{1,0:T(8,128)(2,1)}) custom-call(s32[1]{0:T(128)} %bitcast.turn_ref, bf16[8,512,768]{2,1,0:T(8,128)(2,1)} %bitcast.40, bf16[8,512,768]{2,1,0:T(8,128)(2,1)} %collective-permute-done.14.sib_ref, ...), custom_call_target="tpu_custom_call" | custom-call | flops 6442450944 | bytes 18874368 | tf_op jit(solution)/shard_map/right_product/pallas_call | solution.py:141
  340.4 3.1 collective-permute-start.22
  345.4 2.0 collective-permute-start.50
  347.5 20.6 %collective-permute-done.49 = bf16[64,1024]{1,0:T(8,128)(2,1)S(1)} collective-permute-done((bf16[64,1024]{1,0:T(8,128)(2,1)S(1)}, bf16[64,1024]{1,0:T(8,128)(2,1)S(1)}, u32[]{:S(2)}, u32[]{:S(2)}) %collective-permute-start.49) | collective-permute-done | bytes 131104 | tf_op jit(solution)/shard_map/ppermute | solution.py:26
  368.5 3.7 collective-permute-start.31
  374.9 4.7 %collective-permute-done.30 = bf16[128,1024]{1,0:T(8,128)(2,1)S(1)} collective-permute-done((bf16[128,1024]{1,0:T(8,128)(2,1)}, bf16[128,1024]{1,0:T(8,128)(2,1)S(1)}, u32[]{:S(2)}, u32[]{:S(2)}) %collective-permute-start.30) | collective-permute-done | bytes 262176 | tf_op jit(solution)/shard_map/ppermute | solution.py:26
  379.6 11.2 %collective-permute-done.31 = bf16[128,1024]{1,0:T(8,128)(2,1)S(1)} collective-permute-done((bf16[128,1024]{1,0:T(8,128)(2,1)}, bf16[128,1024]{1,0:T(8,128)(2,1)S(1)}, u32[]{:S(2)}, u32[]{:S(2)}) %collective-permute-start.31) | collective-permute-done | bytes 262176 | tf_op jit(solution)/shard_map/ppermute | solution.py:26
  395.0 6.1 %collective-permute-done.58.refs_1_ = bf16[128,1024]{1,0:T(8,128)(2,1)S(1)} collective-permute-done((bf16[128,1024]{1,0:T(8,128)(2,1)S(1)}, bf16[128,1024]{1,0:T(8,128)(2,1)S(1)}, u32[]{:S(2)}, u32[]{:S(2)}) %collective-permute-start.58) | collective-permute-done | bytes 262176 | tf_op jit(solution)/shard_map/ppermute | solution.py:21
  403.3 3.5 collective-permute-done.61.refs_1_
  407.4 3.6 collective-permute-start.52
  419.3 4.9 %collective-permute-start.65 = (bf16[128,256]{1,0:T(8,128)(2,1)S(1)}, bf16[128,256]{1,0:T(8,128)(2,1)S(1)}, u32[]{:S(2)}, u32[]{:S(2)}) collective-permute-start(bf16[128,256]{1,0:T(8,128)(2,1)S(1)} %get-tuple-element.46), channel_id=1, source_target_pairs={{0,1},{1,0},{2,3},{3,2},{4,5},{5,4},{6,7},{7,6},{8,9},{9,8},{10,11... | collective-permute-start | bytes 196616 | tf_op jit(solution)/shard_map/ppermute | solution.py:26
  428.2 4.0 collective-permute-done.66
  (209 shorter events, 77.4 us)
Async XLA Ops:
  3.7 29.3 %collective-permute-start.1 = (bf16[192,3072]{1,0:T(8,128)(2,1)}, bf16[192,3072]{1,0:T(8,128)(2,1)}, u32[]{:S(2)}, u32[]{:S(2)}) collective-permute-start(bf16[192,3072]{1,0:T(8,128)(2,1)} %bitcast.23), channel_id=1, source_target_pairs={{0,16},{4,20},{8,24},{12,28},{16,0},{20,4},{24,8},{28,12},{1,17},{... | collective-permute-start | bytes 3538952 | tf_op jit(solution)/shard_map/ppermute | solution.py:21
  6.7 50.1 %collective-permute-start = (bf16[192,3072]{1,0:T(8,128)(2,1)}, bf16[192,3072]{1,0:T(8,128)(2,1)}, u32[]{:S(2)}, u32[]{:S(2)}) collective-permute-start(bf16[192,3072]{1,0:T(8,128)(2,1)} %bitcast.23), channel_id=1, source_target_pairs={{0,4},{4,0},{8,12},{12,8},{16,20},{20,16},{24,28},{28,24},{1,5},{5... | collective-permute-start | bytes 3538952 | tf_op jit(solution)/shard_map/ppermute | solution.py:21
  6.7 51.6 %collective-permute-start.3 = (bf16[192,3072]{1,0:T(8,128)(2,1)}, bf16[192,3072]{1,0:T(8,128)(2,1)}, u32[]{:S(2)}, u32[]{:S(2)}) collective-permute-start(bf16[192,3072]{1,0:T(8,128)(2,1)} %bitcast.23), channel_id=1, source_target_pairs={{0,8},{4,12},{8,0},{12,4},{16,24},{20,28},{24,16},{28,20},{1,9},{5... | collective-permute-start | bytes 3538952 | tf_op jit(solution)/shard_map/ppermute | solution.py:21
  8.3 52.8 %collective-permute-start.8 = (bf16[192,3072]{1,0:T(8,128)(2,1)S(1)}, bf16[192,3072]{1,0:T(8,128)(2,1)}, u32[]{:S(2)}, u32[]{:S(2)}) collective-permute-start(bf16[192,3072]{1,0:T(8,128)(2,1)S(1)} %bitcast.45), channel_id=1, source_target_pairs={{0,8},{4,12},{8,0},{12,4},{16,24},{20,28},{24,16},{28,20},{1,9},{5... | collective-permute-start | bytes 3538952 | tf_op jit(solution)/shard_map/ppermute | solution.py:21
  32.9 32.9 %collective-permute-start.2 = (bf16[192,3072]{1,0:T(8,128)(2,1)}, bf16[192,3072]{1,0:T(8,128)(2,1)}, u32[]{:S(2)}, u32[]{:S(2)}) collective-permute-start(bf16[192,3072]{1,0:T(8,128)(2,1)} %collective-permute-done.1), channel_id=1, source_target_pairs={{0,4},{4,0},{8,12},{12,8},{16,20},{20,16},{24,28},{28,24},{1,5},{5... | collective-permute-start | bytes 3538952 | tf_op jit(solution)/shard_map/ppermute | solution.py:21
  32.9 53.0 %collective-permute-start.5 = (bf16[192,3072]{1,0:T(8,128)(2,1)}, bf16[192,3072]{1,0:T(8,128)(2,1)}, u32[]{:S(2)}, u32[]{:S(2)}) collective-permute-start(bf16[192,3072]{1,0:T(8,128)(2,1)} %collective-permute-done.1), channel_id=1, source_target_pairs={{0,8},{4,12},{8,0},{12,4},{16,24},{20,28},{24,16},{28,20},{1,9},{5... | collective-permute-start | bytes 3538952 | tf_op jit(solution)/shard_map/ppermute | solution.py:21
  56.7 33.9 %collective-permute-start.10 = (bf16[192,3072]{1,0:T(8,128)(2,1)S(1)}, bf16[192,3072]{1,0:T(8,128)(2,1)S(1)}, u32[]{:S(2)}, u32[]{:S(2)}) collective-permute-start(bf16[192,3072]{1,0:T(8,128)(2,1)S(1)} %bitcast.46), channel_id=1, source_target_pairs={{0,16},{4,20},{8,24},{12,28},{16,0},{20,4},{24,8},{28,12},{1,17},{... | collective-permute-start | bytes 3538952 | tf_op jit(solution)/shard_map/ppermute | solution.py:21
  58.2 33.0 %collective-permute-start.4 = (bf16[192,3072]{1,0:T(8,128)(2,1)}, bf16[192,3072]{1,0:T(8,128)(2,1)S(1)}, u32[]{:S(2)}, u32[]{:S(2)}) collective-permute-start(bf16[192,3072]{1,0:T(8,128)(2,1)} %collective-permute-done.3), channel_id=1, source_target_pairs={{0,4},{4,0},{8,12},{12,8},{16,20},{20,16},{24,28},{28,24},{1,5},{5... | collective-permute-start | bytes 3538952 | tf_op jit(solution)/shard_map/ppermute | solution.py:21
  61.1 49.0 %collective-permute-start.12 = (bf16[192,3072]{1,0:T(8,128)(2,1)}, bf16[192,3072]{1,0:T(8,128)(2,1)S(1)}, u32[]{:S(2)}, u32[]{:S(2)}) collective-permute-start(bf16[192,3072]{1,0:T(8,128)(2,1)} %collective-permute-done.8), channel_id=1, source_target_pairs={{0,16},{4,20},{8,24},{12,28},{16,0},{20,4},{24,8},{28,12},{1,17},{... | collective-permute-start | bytes 3538952 | tf_op jit(solution)/shard_map/ppermute | solution.py:21
  65.8 50.0 %collective-permute-start.7 = (bf16[192,3072]{1,0:T(8,128)(2,1)S(1)}, bf16[192,3072]{1,0:T(8,128)(2,1)S(1)}, u32[]{:S(2)}, u32[]{:S(2)}) collective-permute-start(bf16[192,3072]{1,0:T(8,128)(2,1)S(1)} %bitcast.47), channel_id=1, source_target_pairs={{0,4},{4,0},{8,12},{12,8},{16,20},{20,16},{24,28},{28,24},{1,5},{5... | collective-permute-start | bytes 3538952 | tf_op jit(solution)/shard_map/ppermute | solution.py:21
  85.9 27.8 %collective-permute-start.6 = (bf16[192,3072]{1,0:T(8,128)(2,1)}, bf16[192,3072]{1,0:T(8,128)(2,1)S(1)}, u32[]{:S(2)}, u32[]{:S(2)}) collective-permute-start(bf16[192,3072]{1,0:T(8,128)(2,1)} %collective-permute-done.5), channel_id=1, source_target_pairs={{0,4},{4,0},{8,12},{12,8},{16,20},{20,16},{24,28},{28,24},{1,5},{5... | collective-permute-start | bytes 3538952 | tf_op jit(solution)/shard_map/ppermute | solution.py:21
  90.7 28.8 %collective-permute-start.9 = (bf16[192,3072]{1,0:T(8,128)(2,1)}, bf16[192,3072]{1,0:T(8,128)(2,1)S(1)}, u32[]{:S(2)}, u32[]{:S(2)}) collective-permute-start(bf16[192,3072]{1,0:T(8,128)(2,1)} %collective-permute-done.8), channel_id=1, source_target_pairs={{0,4},{4,0},{8,12},{12,8},{16,20},{20,16},{24,28},{28,24},{1,5},{5... | collective-permute-start | bytes 3538952 | tf_op jit(solution)/shard_map/ppermute | solution.py:21
  91.2 30.5 %collective-permute-start.11 = (bf16[192,3072]{1,0:T(8,128)(2,1)S(1)}, bf16[192,3072]{1,0:T(8,128)(2,1)S(1)}, u32[]{:S(2)}, u32[]{:S(2)}) collective-permute-start(bf16[192,3072]{1,0:T(8,128)(2,1)S(1)} %collective-permute-done.10), channel_id=1, source_target_pairs={{0,4},{4,0},{8,12},{12,8},{16,20},{20,16},{24,28},{28,24},{1,5},{5... | collective-permute-start | bytes 3538952 | tf_op jit(solution)/shard_map/ppermute | solution.py:21
  153.5 131.7 %collective-permute-start.14 = (bf16[8,512,768]{2,1,0:T(8,128)(2,1)}, bf16[8,512,768]{2,1,0:T(8,128)(2,1)}, u32[]{:S(2)}, u32[]{:S(2)}) collective-permute-start(bf16[8,512,768]{2,1,0:T(8,128)(2,1)} %bitcast.36), channel_id=1, source_target_pairs={{0,4},{4,0},{8,12},{12,8},{16,20},{20,16},{24,28},{28,24},{1,5},{5... | collective-permute-start | bytes 18874376 | tf_op jit(solution)/shard_map/ppermute | solution.py:21
  158.6 22.0 %collective-permute-start.33 = (bf16[64,3072]{1,0:T(8,128)(2,1)S(1)}, bf16[64,3072]{1,0:T(8,128)(2,1)}, u32[]{:S(2)}, u32[]{:S(2)}) collective-permute-start(bf16[64,3072]{1,0:T(8,128)(2,1)S(1)} %copy.31.refs_0_), channel_id=1, source_target_pairs={{0,8},{4,12},{8,0},{12,4},{16,24},{20,28},{24,16},{28,20},{1,9},{5... | collective-permute-start | bytes 1179656 | tf_op jit(solution)/shard_map/ppermute | solution.py:21
  160.0 17.8 %collective-permute-start.36 = (bf16[64,3072]{1,0:T(8,128)(2,1)}, bf16[64,3072]{1,0:T(8,128)(2,1)}, u32[]{:S(2)}, u32[]{:S(2)}) collective-permute-start(bf16[64,3072]{1,0:T(8,128)(2,1)} %copy.32.refs_4_), channel_id=1, source_target_pairs={{0,8},{4,12},{8,0},{12,4},{16,24},{20,28},{24,16},{28,20},{1,9},{5... | collective-permute-start | bytes 1179656 | tf_op jit(solution)/shard_map/ppermute | solution.py:21
  161.6 20.5 %collective-permute-start.37 = (bf16[64,3072]{1,0:T(8,128)(2,1)}, bf16[64,3072]{1,0:T(8,128)(2,1)}, u32[]{:S(2)}, u32[]{:S(2)}) collective-permute-start(bf16[64,3072]{1,0:T(8,128)(2,1)} %copy.32.refs_4_), channel_id=1, source_target_pairs={{0,16},{4,20},{8,24},{12,28},{16,0},{20,4},{24,8},{28,12},{1,17},{... | collective-permute-start | bytes 1179656 | tf_op jit(solution)/shard_map/ppermute | solution.py:21
  180.6 31.1 %collective-permute-start.16 = (bf16[128,3072]{1,0:T(8,128)(2,1)}, bf16[128,3072]{1,0:T(8,128)(2,1)}, u32[]{:S(2)}, u32[]{:S(2)}) collective-permute-start(bf16[128,3072]{1,0:T(8,128)(2,1)} %copy.27.refs_0_), channel_id=1, source_target_pairs={{0,16},{4,20},{8,24},{12,28},{16,0},{20,4},{24,8},{28,12},{1,17},{... | collective-permute-start | bytes 2359304 | tf_op jit(solution)/shard_map/ppermute | solution.py:21
  185.9 29.5 %collective-permute-start.18 = (bf16[128,3072]{1,0:T(8,128)(2,1)}, bf16[128,3072]{1,0:T(8,128)(2,1)}, u32[]{:S(2)}, u32[]{:S(2)}) collective-permute-start(bf16[128,3072]{1,0:T(8,128)(2,1)} %copy.28.refs_4_), channel_id=1, source_target_pairs={{0,8},{4,12},{8,0},{12,4},{16,24},{20,28},{24,16},{28,20},{1,9},{5... | collective-permute-start | bytes 2359304 | tf_op jit(solution)/shard_map/ppermute | solution.py:21
  190.0 20.1 %collective-permute-start.46 = (bf16[64,3072]{1,0:T(8,128)(2,1)}, bf16[64,3072]{1,0:T(8,128)(2,1)S(1)}, u32[]{:S(2)}, u32[]{:S(2)}) collective-permute-start(bf16[64,3072]{1,0:T(8,128)(2,1)} %copy.34.refs_4_), channel_id=1, source_target_pairs={{0,16},{4,20},{8,24},{12,28},{16,0},{20,4},{24,8},{28,12},{1,17},{... | collective-permute-start | bytes 1179656 | tf_op jit(solution)/shard_map/ppermute | solution.py:21
  198.5 33.8 %collective-permute-start.15 = (bf16[128,3072]{1,0:T(8,128)(2,1)}, bf16[128,3072]{1,0:T(8,128)(2,1)}, u32[]{:S(2)}, u32[]{:S(2)}) collective-permute-start(bf16[128,3072]{1,0:T(8,128)(2,1)} %copy.27.refs_0_), channel_id=1, source_target_pairs={{0,8},{4,12},{8,0},{12,4},{16,24},{20,28},{24,16},{28,20},{1,9},{5... | collective-permute-start | bytes 2359304 | tf_op jit(solution)/shard_map/ppermute | solution.py:21
  210.2 22.5 %collective-permute-start.19 = (bf16[128,3072]{1,0:T(8,128)(2,1)}, bf16[128,3072]{1,0:T(8,128)(2,1)}, u32[]{:S(2)}, u32[]{:S(2)}) collective-permute-start(bf16[128,3072]{1,0:T(8,128)(2,1)} %copy.28.refs_4_), channel_id=1, source_target_pairs={{0,16},{4,20},{8,24},{12,28},{16,0},{20,4},{24,8},{28,12},{1,17},{... | collective-permute-start | bytes 2359304 | tf_op jit(solution)/shard_map/ppermute | solution.py:21
  211.7 34.4 %collective-permute-start.25 = (bf16[128,3072]{1,0:T(8,128)(2,1)S(1)}, bf16[128,3072]{1,0:T(8,128)(2,1)}, u32[]{:S(2)}, u32[]{:S(2)}) collective-permute-start(bf16[128,3072]{1,0:T(8,128)(2,1)S(1)} %copy.29.refs_0_), channel_id=1, source_target_pairs={{0,16},{4,20},{8,24},{12,28},{16,0},{20,4},{24,8},{28,12},{1,17},{... | collective-permute-start | bytes 2359304 | tf_op jit(solution)/shard_map/ppermute | solution.py:21
  215.4 33.6 %collective-permute-start.27 = (bf16[128,3072]{1,0:T(8,128)(2,1)S(1)}, bf16[128,3072]{1,0:T(8,128)(2,1)S(1)}, u32[]{:S(2)}, u32[]{:S(2)}) collective-permute-start(bf16[128,3072]{1,0:T(8,128)(2,1)S(1)} %copy.30.refs_4_), channel_id=1, source_target_pairs={{0,8},{4,12},{8,0},{12,4},{16,24},{20,28},{24,16},{28,20},{1,9},{5... | collective-permute-start | bytes 2359304 | tf_op jit(solution)/shard_map/ppermute | solution.py:21
  232.3 25.2 %collective-permute-start.35 = (bf16[64,3072]{1,0:T(8,128)(2,1)}, bf16[64,3072]{1,0:T(8,128)(2,1)S(1)}, u32[]{:S(2)}, u32[]{:S(2)}) collective-permute-start(bf16[64,3072]{1,0:T(8,128)(2,1)} %collective-permute-done.34.refs_2_), channel_id=1, source_target_pairs={{0,8},{4,12},{8,0},{12,4},{16,24},{20,28},{24,16},{28,20},{1,9},{5... | collective-permute-start | bytes 1179656 | tf_op jit(solution)/shard_map/ppermute | solution.py:21
  232.7 50.5 %collective-permute-start.17 = (bf16[128,3072]{1,0:T(8,128)(2,1)}, bf16[128,3072]{1,0:T(8,128)(2,1)}, u32[]{:S(2)}, u32[]{:S(2)}) collective-permute-start(bf16[128,3072]{1,0:T(8,128)(2,1)} %collective-permute-done.16.refs_2_), channel_id=1, source_target_pairs={{0,8},{4,12},{8,0},{12,4},{16,24},{20,28},{24,16},{28,20},{1,9},{5... | collective-permute-start | bytes 2359304 | tf_op jit(solution)/shard_map/ppermute | solution.py:21
  246.1 38.6 %collective-permute-start.20 = (bf16[128,3072]{1,0:T(8,128)(2,1)}, bf16[128,3072]{1,0:T(8,128)(2,1)}, u32[]{:S(2)}, u32[]{:S(2)}) collective-permute-start(bf16[128,3072]{1,0:T(8,128)(2,1)} %collective-permute-done.18.refs_5_), channel_id=1, source_target_pairs={{0,16},{4,20},{8,24},{12,28},{16,0},{20,4},{24,8},{28,12},{1,17},{... | collective-permute-start | bytes 2359304 | tf_op jit(solution)/shard_map/ppermute | solution.py:21
  249.0 23.7 %collective-permute-start.38 = (bf16[64,3072]{1,0:T(8,128)(2,1)}, bf16[64,3072]{1,0:T(8,128)(2,1)S(1)}, u32[]{:S(2)}, u32[]{:S(2)}) collective-permute-start(bf16[64,3072]{1,0:T(8,128)(2,1)} %collective-permute-done.36.refs_5_), channel_id=1, source_target_pairs={{0,16},{4,20},{8,24},{12,28},{16,0},{20,4},{24,8},{28,12},{1,17},{... | collective-permute-start | bytes 1179656 | tf_op jit(solution)/shard_map/ppermute | solution.py:21
  257.5 25.3 %collective-permute-start.44 = (bf16[64,3072]{1,0:T(8,128)(2,1)}, bf16[64,3072]{1,0:T(8,128)(2,1)S(1)}, u32[]{:S(2)}, u32[]{:S(2)}) collective-permute-start(bf16[64,3072]{1,0:T(8,128)(2,1)} %collective-permute-done.43.refs_2_), channel_id=1, source_target_pairs={{0,8},{4,12},{8,0},{12,4},{16,24},{20,28},{24,16},{28,20},{1,9},{5... | collective-permute-start | bytes 1179656 | tf_op jit(solution)/shard_map/ppermute | solution.py:21
  272.7 49.5 %collective-permute-start.24 = (bf16[128,3072]{1,0:T(8,128)(2,1)S(1)}, bf16[128,3072]{1,0:T(8,128)(2,1)}, u32[]{:S(2)}, u32[]{:S(2)}) collective-permute-start(bf16[128,3072]{1,0:T(8,128)(2,1)S(1)} %copy.29.refs_0_), channel_id=1, source_target_pairs={{0,8},{4,12},{8,0},{12,4},{16,24},{20,28},{24,16},{28,20},{1,9},{5... | collective-permute-start | bytes 2359304 | tf_op jit(solution)/shard_map/ppermute | solution.py:21
  282.7 40.3 %collective-permute-start.28 = (bf16[128,3072]{1,0:T(8,128)(2,1)S(1)}, bf16[128,3072]{1,0:T(8,128)(2,1)}, u32[]{:S(2)}, u32[]{:S(2)}) collective-permute-start(bf16[128,3072]{1,0:T(8,128)(2,1)S(1)} %copy.30.refs_4_), channel_id=1, source_target_pairs={{0,16},{4,20},{8,24},{12,28},{16,0},{20,4},{24,8},{28,12},{1,17},{... | collective-permute-start | bytes 2359304 | tf_op jit(solution)/shard_map/ppermute | solution.py:21
  283.2 28.3 %collective-permute-start.47 = (bf16[64,3072]{1,0:T(8,128)(2,1)}, bf16[64,3072]{1,0:T(8,128)(2,1)S(1)}, u32[]{:S(2)}, u32[]{:S(2)}) collective-permute-start(bf16[64,3072]{1,0:T(8,128)(2,1)} %copy-done.5), channel_id=1, source_target_pairs={{0,16},{4,20},{8,24},{12,28},{16,0},{20,4},{24,8},{28,12},{1,17},{... | collective-permute-start | bytes 1179656 | tf_op jit(solution)/shard_map/ppermute | solution.py:21
  284.8 40.8 %collective-permute-start.26 = (bf16[128,3072]{1,0:T(8,128)(2,1)}, bf16[128,3072]{1,0:T(8,128)(2,1)}, u32[]{:S(2)}, u32[]{:S(2)}) collective-permute-start(bf16[128,3072]{1,0:T(8,128)(2,1)} %collective-permute-done.25.refs_2_), channel_id=1, source_target_pairs={{0,8},{4,12},{8,0},{12,4},{16,24},{20,28},{24,16},{28,20},{1,9},{5... | collective-permute-start | bytes 2359304 | tf_op jit(solution)/shard_map/ppermute | solution.py:21
  285.2 41.5 %collective-permute-start.29 = (bf16[128,3072]{1,0:T(8,128)(2,1)}, bf16[128,3072]{1,0:T(8,128)(2,1)}, u32[]{:S(2)}, u32[]{:S(2)}) collective-permute-start(bf16[128,3072]{1,0:T(8,128)(2,1)} %copy-done.18), channel_id=1, source_target_pairs={{0,16},{4,20},{8,24},{12,28},{16,0},{20,4},{24,8},{28,12},{1,17},{... | collective-permute-start | bytes 2359304 | tf_op jit(solution)/shard_map/ppermute | solution.py:21
  311.6 60.6 %collective-permute-start.21 = (bf16[128,1024]{1,0:T(8,128)(2,1)}, bf16[128,1024]{1,0:T(8,128)(2,1)S(1)}, u32[]{:S(2)}, u32[]{:S(2)}) collective-permute-start(bf16[128,1024]{1,0:T(8,128)(2,1)} %get-tuple-element.19), channel_id=1, source_target_pairs={{0,1},{1,0},{2,3},{3,2},{4,5},{5,4},{6,7},{7,6},{8,9},{9,8},{10,11... | collective-permute-start | bytes 786440 | tf_op jit(solution)/shard_map/ppermute | solution.py:26
  322.2 18.2 %collective-permute-start.39 = (bf16[64,1024]{1,0:T(8,128)(2,1)S(1)}, bf16[64,1024]{1,0:T(8,128)(2,1)S(1)}, u32[]{:S(2)}, u32[]{:S(2)}) collective-permute-start(bf16[64,1024]{1,0:T(8,128)(2,1)S(1)} %copy-done.25), channel_id=1, source_target_pairs={{0,1},{1,0},{2,3},{3,2},{4,5},{5,4},{6,7},{7,6},{8,9},{9,8},{10,11... | collective-permute-start | bytes 393224 | tf_op jit(solution)/shard_map/ppermute | solution.py:26
  323.0 20.5 %collective-permute-start.40 = (bf16[64,1024]{1,0:T(8,128)(2,1)S(1)}, bf16[64,1024]{1,0:T(8,128)(2,1)S(1)}, u32[]{:S(2)}, u32[]{:S(2)}) collective-permute-start(bf16[64,1024]{1,0:T(8,128)(2,1)S(1)} %copy-done.24), channel_id=1, source_target_pairs={{0,2},{1,3},{2,0},{3,1},{4,6},{5,7},{6,4},{7,5},{8,10},{9,11},{10,... | collective-permute-start | bytes 393224 | tf_op jit(solution)/shard_map/ppermute | solution.py:26
  325.6 19.0 %collective-permute-start.41 = (bf16[64,1024]{1,0:T(8,128)(2,1)S(1)}, bf16[64,1024]{1,0:T(8,128)(2,1)S(1)}, u32[]{:S(2)}, u32[]{:S(2)}) collective-permute-start(bf16[64,1024]{1,0:T(8,128)(2,1)S(1)} %copy-done.23), channel_id=1, source_target_pairs={{0,3},{1,2},{2,1},{3,0},{4,7},{5,6},{6,5},{7,4},{8,11},{9,10},{10,... | collective-permute-start | bytes 393224 | tf_op jit(solution)/shard_map/ppermute | solution.py:26
  326.8 18.7 %collective-permute-start.48 = (bf16[64,1024]{1,0:T(8,128)(2,1)}, bf16[64,1024]{1,0:T(8,128)(2,1)S(1)}, u32[]{:S(2)}, u32[]{:S(2)}) collective-permute-start(bf16[64,1024]{1,0:T(8,128)(2,1)} %get-tuple-element.31), channel_id=1, source_target_pairs={{0,1},{1,0},{2,3},{3,2},{4,5},{5,4},{6,7},{7,6},{8,9},{9,8},{10,11... | collective-permute-start | bytes 393224 | tf_op jit(solution)/shard_map/ppermute | solution.py:26
  340.4 33.1 %collective-permute-start.22 = (bf16[128,1024]{1,0:T(8,128)(2,1)S(1)}, bf16[128,1024]{1,0:T(8,128)(2,1)S(1)}, u32[]{:S(2)}, u32[]{:S(2)}) collective-permute-start(bf16[128,1024]{1,0:T(8,128)(2,1)S(1)} %copy-done.20), channel_id=1, source_target_pairs={{0,2},{1,3},{2,0},{3,1},{4,6},{5,7},{6,4},{7,5},{8,10},{9,11},{10,... | collective-permute-start | bytes 786440 | tf_op jit(solution)/shard_map/ppermute | solution.py:26
  343.5 30.6 %collective-permute-start.23 = (bf16[128,1024]{1,0:T(8,128)(2,1)S(1)}, bf16[128,1024]{1,0:T(8,128)(2,1)S(1)}, u32[]{:S(2)}, u32[]{:S(2)}) collective-permute-start(bf16[128,1024]{1,0:T(8,128)(2,1)S(1)} %copy-done.19), channel_id=1, source_target_pairs={{0,3},{1,2},{2,1},{3,0},{4,7},{5,6},{6,5},{7,4},{8,11},{9,10},{10,... | collective-permute-start | bytes 786440 | tf_op jit(solution)/shard_map/ppermute | solution.py:26
  344.6 23.5 %collective-permute-start.49 = (bf16[64,1024]{1,0:T(8,128)(2,1)S(1)}, bf16[64,1024]{1,0:T(8,128)(2,1)S(1)}, u32[]{:S(2)}, u32[]{:S(2)}) collective-permute-start(bf16[64,1024]{1,0:T(8,128)(2,1)S(1)} %copy-done.22), channel_id=1, source_target_pairs={{0,2},{1,3},{2,0},{3,1},{4,6},{5,7},{6,4},{7,5},{8,10},{9,11},{10,... | collective-permute-start | bytes 393224 | tf_op jit(solution)/shard_map/ppermute | solution.py:26
  345.4 23.0 %collective-permute-start.50 = (bf16[64,1024]{1,0:T(8,128)(2,1)S(1)}, bf16[64,1024]{1,0:T(8,128)(2,1)S(1)}, u32[]{:S(2)}, u32[]{:S(2)}) collective-permute-start(bf16[64,1024]{1,0:T(8,128)(2,1)S(1)} %copy-done.21), channel_id=1, source_target_pairs={{0,3},{1,2},{2,1},{3,0},{4,7},{5,6},{6,5},{7,4},{8,11},{9,10},{10,... | collective-permute-start | bytes 393224 | tf_op jit(solution)/shard_map/ppermute | solution.py:26
  368.5 22.3 %collective-permute-start.31 = (bf16[128,1024]{1,0:T(8,128)(2,1)}, bf16[128,1024]{1,0:T(8,128)(2,1)S(1)}, u32[]{:S(2)}, u32[]{:S(2)}) collective-permute-start(bf16[128,1024]{1,0:T(8,128)(2,1)} %get-tuple-element.24), channel_id=1, source_target_pairs={{0,2},{1,3},{2,0},{3,1},{4,6},{5,7},{6,4},{7,5},{8,10},{9,11},{10,... | collective-permute-start | bytes 786440 | tf_op jit(solution)/shard_map/ppermute | solution.py:26
  372.2 18.6 %collective-permute-start.32 = (bf16[128,1024]{1,0:T(8,128)(2,1)}, bf16[128,1024]{1,0:T(8,128)(2,1)S(1)}, u32[]{:S(2)}, u32[]{:S(2)}) collective-permute-start(bf16[128,1024]{1,0:T(8,128)(2,1)} %get-tuple-element.25), channel_id=1, source_target_pairs={{0,3},{1,2},{2,1},{3,0},{4,7},{5,6},{6,5},{7,4},{8,11},{9,10},{10,... | collective-permute-start | bytes 786440 | tf_op jit(solution)/shard_map/ppermute | solution.py:26
  373.5 28.5 %collective-permute-start.55 = (bf16[64,1024]{1,0:T(8,128)(2,1)S(1)}, bf16[64,1024]{1,0:T(8,128)(2,1)S(1)}, u32[]{:S(2)}, u32[]{:S(2)}) collective-permute-start(bf16[64,1024]{1,0:T(8,128)(2,1)S(1)} %add_convert_fusion.3.refs_0_), channel_id=1, source_target_pairs={{8,0},{12,4},{0,8},{4,12},{24,16},{28,20},{16,24},{20,28},{9,1},{1... | collective-permute-start | bytes 393224 | tf_op jit(solution)/shard_map/ppermute | solution.py:218
  374.3 20.6 %collective-permute-start.62 = (bf16[128,1024]{1,0:T(8,128)(2,1)S(1)}, bf16[128,1024]{1,0:T(8,128)(2,1)S(1)}, u32[]{:S(2)}, u32[]{:S(2)}) collective-permute-start(bf16[128,1024]{1,0:T(8,128)(2,1)S(1)} %add_convert_fusion.1.refs_0_), channel_id=1, source_target_pairs={{0,16},{4,20},{8,24},{12,28},{16,0},{20,4},{24,8},{28,12},{1,17},{... | collective-permute-start | bytes 786440 | tf_op jit(solution)/shard_map/ppermute | solution.py:21
  394.9 17.3 %collective-permute-start.63 = (bf16[128,1024]{1,0:T(8,128)(2,1)S(1)}, bf16[128,1024]{1,0:T(8,128)(2,1)S(1)}, u32[]{:S(2)}, u32[]{:S(2)}) collective-permute-start(bf16[128,1024]{1,0:T(8,128)(2,1)S(1)} %collective-permute-done.62.refs_2_), channel_id=1, source_target_pairs={{0,8},{4,12},{8,0},{12,4},{16,24},{20,28},{24,16},{28,20},{1,9},{5... | collective-permute-start | bytes 786440 | tf_op jit(solution)/shard_map/ppermute | solution.py:21
  (47 other events, 1059.7 us)
